TPU v7x, 32 devices: a whole 2x2x4 slice. The times are simulated.
32 devices in a mesh: expert: 8 (over z, x), hidden: 4 (over y, core).
Axes of the slice: x: 2, y: 2, z: 4, core: 2. Of those that a mesh axis runs over, the one named last changes fastest.
Arguments:
- tokens: bfloat16 [2, 16384, 512], P(None, ('expert', 'hidden')), may hold values from -6 to 6
- grad_out: bfloat16 [2, 16384, 512], P(None, ('expert', 'hidden')), may hold values from -6 to 6
- attn_routes: int32 [2, 16384, 4], P(None, ('expert', 'hidden')), may hold values from 0 to 23, all different within a row
- ffn_routes: int32 [2, 16384, 2], P(None, ('expert', 'hidden')), may hold values from 0 to 15, all different within a row; in each aligned block of 512 rows (0 to 511, 512 to 1023, ..., all dimensions but the last counted through in order) at most 128 rows name the same one
- segments: int32 [2, 64, 256], P(None, ('expert', 'hidden')), may hold values from 0 to 3, never falling along the last dimension, each value on 1 to 128 neighbouring positions
- pad_mask: int32 [2, 16384], P(None, ('expert', 'hidden')), may hold values 0 or 1
- norm1_gain: float32 [512], replicated, may hold values from 0.5 to 1.5
- norm1_bias: float32 [512], replicated, may hold values from -0.6 to 0.6
- attn_router: bfloat16 [512, 24], replicated, may hold values from -0.125 to 0.125
- query_w: bfloat16 [512, 1536], replicated, may hold values from -0.25 to 0.25
- key_w: bfloat16 [512, 64], replicated, may hold values from -0.25 to 0.25
- value_w: bfloat16 [512, 64], replicated, may hold values from -0.25 to 0.25
- attn_proj: bfloat16 [1536, 512], replicated, may hold values from -2 to 2
- norm2_gain: float32 [512], replicated, may hold values from 0.5 to 1.5
- norm2_bias: float32 [512], replicated, may hold values from -0.6 to 0.6
- ffn_router: bfloat16 [512, 16], replicated, may hold values from -0.1875 to 0.1875
- expert_in: bfloat16 [16, 512, 2048], P('expert', None, 'hidden'), may hold values from -0.25 to 0.25
- expert_out: bfloat16 [16, 2048, 512], P('expert', 'hidden'), may hold values from -0.1875 to 0.1875
- halt_w: float32 [512], replicated, may hold values from -0.25 to 0.25
- halt_b: float32 [1], replicated, may hold values from -2.5 to 2.5
Outputs:
- result: bfloat16 [2, 16384, 512], P(None, ('expert', 'hidden'))
- grad_tokens: float32 [2, 16384, 512], P(None, ('expert', 'hidden'))
- grad_norm1_gain: float32 [512], replicated
- grad_norm1_bias: float32 [512], replicated
- grad_attn_router: float32 [512, 24], replicated
- grad_query_w: float32 [512, 1536], replicated
- grad_key_w: float32 [512, 64], replicated
- grad_value_w: float32 [512, 64], replicated
- grad_attn_proj: float32 [1536, 512], replicated
- grad_norm2_gain: float32 [512], replicated
- grad_norm2_bias: float32 [512], replicated
- grad_ffn_router: float32 [512, 16], replicated
- grad_expert_in: float32 [16, 512, 2048], P('expert', None, 'hidden')
- grad_expert_out: float32 [16, 2048, 512], P('expert', 'hidden')
- grad_halt_w: float32 [512], replicated
- grad_halt_b: float32 [1], replicated
Inputs may be any that keep to these rules, and one draw needn't show every extreme that they name: `attn_routes`: each token names 4 different attention experts. `ffn_routes`: each token names 2 different feed-forward experts; in each micro-batch the 512 tokens of one device name no expert more than 128 times, a bound that some block reaches. `segments`: along a packed row the numbers never fall, and each of the 4 numbers covers 1 to 128 positions.
All inputs are finite; a program needn't handle non-finite values. No bound on the sum of `pad_mask` on one device may be relied on, other than what follows from the above.
Results may differ from a plain program's by a relative error of at most 0.015.
The roundings to bfloat16 on the way count: a program that leaves them out, or rounds other values in their place, can miss the bound.
Values may be sent and summed in bfloat16 or wider, within the bound.
A program may use at most 256 MiB of HBM per device.

v0:
```python
import jax
import jax.numpy as jnp
from jax import lax
from jax.sharding import PartitionSpec as P

SEQ = 256
ATT_BLOCK = 512


def layer_norm(value, gain, shift):
    center = value - jnp.mean(value, axis=-1, keepdims=True)
    spread = jnp.mean(center * center, axis=-1, keepdims=True)
    return center * lax.rsqrt(spread + 1e-05) * gain + shift


def norm_back(value, gain, shift, grad):
    unused, pullback = jax.vjp(layer_norm, value, gain, shift)
    return pullback(grad)


def gelu_back(pre, grad):
    unused, pullback = jax.vjp(jax.nn.gelu, pre)
    return pullback(grad)[0]


def softmax_back(probs, grad):
    return probs * (grad - jnp.sum(probs * grad, axis=-1, keepdims=True))


def spread_picks(pick, values):
    total = pick[:, 0, :, None] * values[:, 0, None, :]
    for which in range(1, pick.shape[1]):
        total = total + pick[:, which, :, None] * values[:, which, None, :]
    return total


def masked_scores(query_sel, keys, segment, padding):
    place = jnp.arange(segment.shape[0])
    same_row = place[:, None] // SEQ == place[None, :] // SEQ
    same_pair = segment[:, None] == segment[None, :]
    visible = (padding[None, :] == 1) | (place[:, None] == place[None, :])
    allowed = same_row & same_pair & visible
    scale = keys.shape[1] ** (-0.5)
    scores = jnp.einsum("qkh,jh->qkj", query_sel, keys, preferred_element_type=jnp.float32) * scale
    return jnp.where(allowed[:, None, :], scores, -1e30)


def attend_forward(operands):
    query_sel, keys, values, segment, padding = operands
    scores = masked_scores(query_sel, keys, segment, padding)
    top = jnp.max(scores, axis=-1, keepdims=True)
    expo = jnp.exp(scores - top)
    total = jnp.sum(expo, axis=-1, keepdims=True)
    probs = (expo / total).astype(jnp.bfloat16)
    heads = jnp.einsum("qkj,jh->qkh", probs, values, preferred_element_type=jnp.float32)
    return (heads, top + jnp.log(total))


def attend_backward(operands):
    query_sel, keys, values, segment, padding, logsum, grad_heads = operands
    scale = keys.shape[1] ** (-0.5)
    probs = jnp.exp(masked_scores(query_sel, keys, segment, padding) - logsum)
    probs_low = probs.astype(jnp.bfloat16)
    grad_values = jnp.einsum(
        "qkj,qkh->jh", probs_low, grad_heads, preferred_element_type=jnp.float32
    )
    grad_probs = jnp.einsum("qkh,jh->qkj", grad_heads, values, preferred_element_type=jnp.float32)
    grad_scores = softmax_back(probs, grad_probs).astype(jnp.bfloat16)
    grad_query = (
        jnp.einsum("qkj,jh->qkh", grad_scores, keys, preferred_element_type=jnp.float32) * scale
    )
    grad_keys = (
        jnp.einsum("qkj,qkh->jh", grad_scores, query_sel, preferred_element_type=jnp.float32)
        * scale
    )
    return (grad_query, grad_keys, grad_values)


def expert_forward(rows, first, second):
    pre = jnp.einsum("erd,edf->erf", rows, first, preferred_element_type=jnp.float32)
    act = jax.nn.gelu(pre).astype(jnp.bfloat16)
    total = jnp.einsum("erf,efd->erd", act, second, preferred_element_type=jnp.float32)
    return (pre, act, total)


def expert_backward(rows, pre, act, grad_rows_in, first, second):
    grad_act = jnp.einsum("erd,efd->erf", grad_rows_in, second, preferred_element_type=jnp.float32)
    grad_pre = gelu_back(pre, grad_act).astype(jnp.bfloat16)
    grad_second = jnp.einsum("erf,erd->efd", act, grad_rows_in, preferred_element_type=jnp.float32)
    grad_first = jnp.einsum("erd,erf->edf", rows, grad_pre, preferred_element_type=jnp.float32)
    grad_rows_out = jnp.einsum("erf,edf->erd", grad_pre, first, preferred_element_type=jnp.float32)
    return (grad_first, grad_second, grad_rows_out)


def per_device(
    tokens,
    grad_out,
    attn_routes,
    ffn_routes,
    segments,
    pad_mask,
    norm1_gain,
    norm1_bias,
    attn_router,
    query_w,
    key_w,
    value_w,
    attn_proj,
    norm2_gain,
    norm2_bias,
    ffn_router,
    expert_in,
    expert_out,
    halt_w,
    halt_b,
):
    micro_count, tok_rows, width = tokens.shape
    att_count = attn_router.shape[1]
    head = key_w.shape[1]
    experts_all = ffn_router.shape[1]
    top_ffn = ffn_routes.shape[2]
    capacity = 4 * tok_rows // experts_all
    blocks = tok_rows // ATT_BLOCK
    f32 = jnp.float32
    bf16 = jnp.bfloat16
    full_in, full_out = (
        lax.all_gather(expert_in, "hidden", axis=2, tiled=True),
        lax.all_gather(expert_out, "hidden", axis=1, tiled=True),
    )
    acc_in = jnp.zeros(full_in.shape, f32)
    acc_out = jnp.zeros(full_out.shape, f32)
    totals = (
        jnp.zeros(norm1_gain.shape, f32),
        jnp.zeros(norm1_bias.shape, f32),
        jnp.zeros(attn_router.shape, f32),
        jnp.zeros(query_w.shape, f32),
        jnp.zeros(key_w.shape, f32),
        jnp.zeros(value_w.shape, f32),
        jnp.zeros(attn_proj.shape, f32),
        jnp.zeros(norm2_gain.shape, f32),
        jnp.zeros(norm2_bias.shape, f32),
        jnp.zeros(ffn_router.shape, f32),
        jnp.zeros(halt_w.shape, f32),
        jnp.zeros(halt_b.shape, f32),
    )
    results = []
    grads_in = []
    for micro in range(micro_count):
        state_in = tokens[micro].astype(f32)
        segment = segments[micro].reshape(-1)
        padding = pad_mask[micro]
        route_attn = attn_routes[micro]
        route_ffn = ffn_routes[micro]
        normed = layer_norm(state_in, norm1_gain, norm1_bias)
        normed_low = normed.astype(bf16)
        logits_attn = jnp.dot(normed_low, attn_router, preferred_element_type=f32)
        pick_attn = (route_attn[:, :, None] == jnp.arange(att_count)[None, None, :]).astype(f32)
        gate_attn = jax.nn.softmax(jnp.sum(pick_attn * logits_attn[:, None, :], axis=-1), axis=-1)
        query_all = (
            jnp.dot(normed_low, query_w, preferred_element_type=f32)
            .astype(bf16)
            .reshape(tok_rows, att_count, head)
        )
        keys_low = jnp.dot(normed_low, key_w, preferred_element_type=f32).astype(bf16)
        values_low = jnp.dot(normed_low, value_w, preferred_element_type=f32).astype(bf16)
        pick_low = pick_attn.astype(bf16)
        query_sel = jnp.einsum(
            "tke,teh->tkh", pick_low, query_all, preferred_element_type=f32
        ).astype(bf16)
        block_query = query_sel.reshape(blocks, ATT_BLOCK, -1, head)
        block_keys = keys_low.reshape(blocks, ATT_BLOCK, head)
        block_values = values_low.reshape(blocks, ATT_BLOCK, head)
        block_segment = segment.reshape(blocks, ATT_BLOCK)
        block_padding = padding.reshape(blocks, ATT_BLOCK)
        heads, logsum = lax.map(
            attend_forward, (block_query, block_keys, block_values, block_segment, block_padding)
        )
        heads = heads.reshape(tok_rows, -1, head)
        mixed = spread_picks(pick_attn, gate_attn[:, :, None] * heads)
        mixed_low = mixed.reshape(tok_rows, -1).astype(bf16)
        state_mid = state_in + jnp.dot(mixed_low, attn_proj, preferred_element_type=f32)
        normed_two = layer_norm(state_mid, norm2_gain, norm2_bias)
        ffn_low = normed_two.astype(bf16)
        logits_ffn = jnp.dot(ffn_low, ffn_router, preferred_element_type=f32)
        pick_ffn = (route_ffn[:, :, None] == jnp.arange(experts_all)[None, None, :]).astype(f32)
        gate_ffn = jax.nn.softmax(jnp.sum(pick_ffn * logits_ffn[:, None, :], axis=-1), axis=-1)
        flat_route = route_ffn.reshape(-1)
        onehot = (flat_route[:, None] == jnp.arange(experts_all)[None, :]).astype(jnp.int32)
        rank = jnp.sum((jnp.cumsum(onehot, axis=0) - 1) * onehot, axis=1)
        slot = flat_route * capacity + rank
        outgoing = (
            jnp.zeros((experts_all * capacity, width), bf16)
            .at[slot]
            .set(jnp.repeat(ffn_low, top_ffn, axis=0))
        )
        arrived = lax.all_to_all(
            outgoing.reshape(experts_all, capacity, width),
            "expert",
            split_axis=0,
            concat_axis=1,
            tiled=True,
        )
        pre, act, expert_res = expert_forward(arrived, full_in, full_out)
        outgoing_back = expert_res.astype(bf16)
        returned = lax.all_to_all(
            outgoing_back, "expert", split_axis=1, concat_axis=0, tiled=True
        ).reshape(experts_all * capacity, width)
        picked = returned[slot].reshape(tok_rows, top_ffn, width).astype(f32)
        state_end = state_mid + jnp.sum(gate_ffn[:, :, None] * picked, axis=1)
        halting = jax.nn.sigmoid(jnp.sum(state_end * halt_w, axis=-1, keepdims=True) + halt_b)
        branch = state_end - state_in
        results.append((state_in + halting * branch).astype(bf16))
        grad_res = grad_out[micro].astype(f32)
        grad_halt = jnp.sum(grad_res * branch, axis=-1, keepdims=True) * halting * (1.0 - halting)
        grad_end = halting * grad_res + grad_halt * halt_w
        grad_state = grad_res * (1.0 - halting)
        grad_gate_ffn = jnp.sum(picked * grad_end[:, None, :], axis=-1)
        send_grad = (gate_ffn[:, :, None] * grad_end[:, None, :]).astype(bf16).reshape(-1, width)
        grad_buffer = jnp.zeros((experts_all * capacity, width), bf16).at[slot].set(send_grad)
        grad_arrived = lax.all_to_all(
            grad_buffer.reshape(experts_all, capacity, width),
            "expert",
            split_axis=0,
            concat_axis=1,
            tiled=True,
        )
        grad_first, grad_second, grad_rows_out = expert_backward(
            arrived, pre, act, grad_arrived, full_in, full_out
        )
        back_rows = grad_rows_out.astype(bf16)
        acc_in = acc_in + grad_first
        acc_out = acc_out + grad_second
        grad_back = lax.all_to_all(
            back_rows, "expert", split_axis=1, concat_axis=0, tiled=True
        ).reshape(experts_all * capacity, width)
        grad_slots = grad_back[slot].reshape(tok_rows, top_ffn, width).astype(f32)
        grad_sel_ffn = softmax_back(gate_ffn, grad_gate_ffn)
        grad_logits_ffn = jnp.sum(pick_ffn * grad_sel_ffn[:, :, None], axis=1).astype(bf16)
        grad_router_ffn = jnp.dot(ffn_low.T, grad_logits_ffn, preferred_element_type=f32)
        grad_normed_two = jnp.sum(grad_slots, axis=1) + jnp.dot(
            grad_logits_ffn, ffn_router.T, preferred_element_type=f32
        )
        grad_mid_norm, grad_gain_two, grad_bias_two = norm_back(
            state_mid, norm2_gain, norm2_bias, grad_normed_two
        )
        grad_mid = grad_end + grad_mid_norm
        grad_state = grad_state + grad_mid
        grad_attn = grad_mid.astype(bf16)
        grad_proj = jnp.dot(mixed_low.T, grad_attn, preferred_element_type=f32)
        grad_mixed = (
            jnp.dot(grad_attn, attn_proj.T, preferred_element_type=f32)
            .astype(bf16)
            .reshape(tok_rows, att_count, head)
        )
        grad_sel = jnp.einsum("tke,teh->tkh", pick_low, grad_mixed, preferred_element_type=f32)
        grad_gate_attn = jnp.sum(heads * grad_sel, axis=-1)
        grad_heads = (gate_attn[:, :, None] * grad_sel).astype(bf16)
        grad_query, grad_keys, grad_values = lax.map(
            attend_backward,
            (
                block_query,
                block_keys,
                block_values,
                block_segment,
                block_padding,
                logsum,
                grad_heads.reshape(blocks, ATT_BLOCK, -1, head),
            ),
        )
        grad_query_all = (
            spread_picks(pick_attn, grad_query.reshape(tok_rows, -1, head))
            .reshape(tok_rows, -1)
            .astype(bf16)
        )
        grad_keys_low = grad_keys.reshape(tok_rows, head).astype(bf16)
        grad_values_low = grad_values.reshape(tok_rows, head).astype(bf16)
        grad_query_w = jnp.dot(normed_low.T, grad_query_all, preferred_element_type=f32)
        grad_key_w = jnp.dot(normed_low.T, grad_keys_low, preferred_element_type=f32)
        grad_value_w = jnp.dot(normed_low.T, grad_values_low, preferred_element_type=f32)
        grad_sel_attn = softmax_back(gate_attn, grad_gate_attn)
        grad_logits_attn = jnp.sum(pick_attn * grad_sel_attn[:, :, None], axis=1).astype(bf16)
        grad_router_attn = jnp.dot(normed_low.T, grad_logits_attn, preferred_element_type=f32)
        grad_normed = (
            jnp.dot(grad_query_all, query_w.T, preferred_element_type=f32)
            + jnp.dot(grad_keys_low, key_w.T, preferred_element_type=f32)
            + jnp.dot(grad_values_low, value_w.T, preferred_element_type=f32)
            + jnp.dot(grad_logits_attn, attn_router.T, preferred_element_type=f32)
        )
        grad_in_norm, grad_gain_one, grad_bias_one = norm_back(
            state_in, norm1_gain, norm1_bias, grad_normed
        )
        grads_in.append(grad_state + grad_in_norm)
        grad_halt_w = jnp.sum(grad_halt * state_end, axis=0)
        grad_halt_b = jnp.sum(grad_halt, axis=0)
        summed = lax.psum(
            (
                grad_gain_one,
                grad_bias_one,
                grad_router_attn,
                grad_query_w,
                grad_key_w,
                grad_value_w,
                grad_proj,
                grad_gain_two,
                grad_bias_two,
                grad_router_ffn,
                grad_halt_w,
                grad_halt_b,
            ),
            ("expert", "hidden"),
        )
        totals = tuple(jax.tree.map(jnp.add, totals, tuple(summed)))
    acc_in, acc_out = (
        lax.psum_scatter(
            acc_in.astype(jnp.bfloat16), "hidden", scatter_dimension=2, tiled=True
        ).astype(jnp.float32),
        lax.psum_scatter(
            acc_out.astype(jnp.bfloat16), "hidden", scatter_dimension=1, tiled=True
        ).astype(jnp.float32),
    )
    return (
        jnp.stack(results),
        jnp.stack(grads_in),
        totals[0],
        totals[1],
        totals[2],
        totals[3],
        totals[4],
        totals[5],
        totals[6],
        totals[7],
        totals[8],
        totals[9],
        acc_in,
        acc_out,
        totals[10],
        totals[11],
    )


def solution(mesh):
    in_specs = (
        P(None, ("expert", "hidden"), None),
        P(None, ("expert", "hidden"), None),
        P(None, ("expert", "hidden"), None),
        P(None, ("expert", "hidden"), None),
        P(None, ("expert", "hidden"), None),
        P(None, ("expert", "hidden")),
        P(),
        P(),
        P(),
        P(),
        P(),
        P(),
        P(),
        P(),
        P(),
        P(),
        P("expert", None, "hidden"),
        P("expert", "hidden", None),
        P(),
        P(),
    )
    out_specs = (
        P(None, ("expert", "hidden"), None),
        P(None, ("expert", "hidden"), None),
        P(),
        P(),
        P(),
        P(),
        P(),
        P(),
        P(),
        P(),
        P(),
        P(),
        P("expert", None, "hidden"),
        P("expert", "hidden", None),
        P(),
        P(),
    )
    return jax.shard_map(
        per_device, mesh=mesh, in_specs=in_specs, out_specs=out_specs, check_vma=False
    )
```

profile of v0, /device:TPU:0, one launch (start us, length us, event | category | flops | bytes accessed | tf_op | source)
XLA Modules:
  0.0 937.1 jit_solution(10444804443158342972)
XLA Ops:
  27.1 8.9 select_reduce_fusion.3
  38.8 8.9 select_reduce_fusion.2
  134.6 7.2 scatter_custom_fusion.1
  141.8 7.4 all-to-all-start.2
  160.8 7.2 scatter_custom_fusion
  168.0 29.6 %all-to-all-done.2 = bf16[16,128,512]{2,1,0:T(8,128)(2,1)} async-done(((bf16[16,128,512]{2,1,0:T(8,128)(2,1)}), bf16[16,128,512]{2,1,0:T(8,128)(2,1)}, u32[]{:S(2)}, u32[]{:S(2)}) %all-to-all-start.2) | async-done | bytes 2097184 | tf_op jit(solution)/shard_map/all_to_all | solution.py:196
  205.4 13.1 %fusion.188 = f32[2,1024,2048]{2,1,0:T(8,128)} fusion(bf16[2,1024,512]{2,1,0:T(8,128)(2,1)} %bitcast.422, bf16[2,512,2048]{2,1,0:T(8,128)(2,1)} %all-gather.3.cloned.1.call-done), kind=kOutput, calls=%fused_computation.370 | convolution fusion | flops 4294967296 | bytes 23068672 | tf_op jit(solution)/shard_map/erd,edf->erf/dot_general | solution.py:80
  218.5 10.1 %convolution_convert_fusion.6 = bf16[2,1024,512]{2,1,0:T(8,128)(2,1)S(1)} fusion(bf16[2,2048,512]{2,1,0:T(8,128)(2,1)} %all-gather.5.cloned.1.call-done, f32[2,1024,2048]{2,1,0:T(8,128)} %fusion.188), kind=kOutput, calls=%fused_computation.71 | convolution fusion | flops 4333764608 | bytes 23068672 | tf_op jit(solution)/shard_map/erf,efd->erd/dot_general | solution.py:82
  232.1 18.0 %all-to-all-done = bf16[16,128,512]{2,1,0:T(8,128)(2,1)} async-done(((bf16[16,128,512]{2,1,0:T(8,128)(2,1)}), bf16[16,128,512]{2,1,0:T(8,128)(2,1)}, u32[]{:S(2)}, u32[]{:S(2)}) %all-to-all-start) | async-done | bytes 2097184 | tf_op jit(solution)/shard_map/all_to_all | solution.py:196
  257.5 10.4 %multiply_convert_fusion.1 = (bf16[2,1024,2048]{2,1,0:T(8,128)(2,1)S(1)}, f32[2,1024,2048]{2,1,0:T(8,128)}) fusion(bf16[2,1024,512]{2,1,0:T(8,128)(2,1)S(1)} %bitcast.424, bf16[2,512,2048]{2,1,0:T(8,128)(2,1)S(1)} %copy-done.202), kind=kOutput, calls=%fused_computation.27 | convolution fusion | flops 4332716032 | bytes 31457280 | tf_op jit(solution)/shard_map/erd,edf->erf/dot_general | solution.py:80
  276.1 26.4 %all-to-all-done.3 = bf16[2,1024,512]{2,0,1:T(2,128)(2,1)} async-done(((bf16[2,1024,512]{2,0,1:T(2,128)(2,1)}), bf16[2,1024,512]{2,0,1:T(2,128)(2,1)}, u32[]{:S(2)}, u32[]{:S(2)}) %all-to-all-start.3) | async-done | bytes 2097184 | tf_op jit(solution)/shard_map/all_to_all | solution.py:205
  321.6 7.0 gather_fusion.1
  339.8 15.0 %all-to-all-done.1 = bf16[2,1024,512]{2,0,1:T(2,128)(2,1)} async-done(((bf16[2,1024,512]{2,0,1:T(2,128)(2,1)}), bf16[2,1024,512]{2,0,1:T(2,128)(2,1)}, u32[]{:S(2)}, u32[]{:S(2)}) %all-to-all-start.1) | async-done | bytes 2097184 | tf_op jit(solution)/shard_map/all_to_all | solution.py:205
  358.2 7.0 gather_fusion
  389.2 8.2 scatter_custom_fusion.2
  411.0 7.7 scatter_custom_fusion.3
  418.8 30.8 %all-to-all-done.4 = bf16[16,128,512]{2,1,0:T(8,128)(2,1)} async-done(((bf16[16,128,512]{2,1,0:T(8,128)(2,1)}), bf16[16,128,512]{2,1,0:T(8,128)(2,1)}, u32[]{:S(2)}, u32[]{:S(2)}) %all-to-all-start.4) | async-done | bytes 2097184 | tf_op jit(solution)/shard_map/all_to_all | solution.py:220
  466.9 12.2 %fusion.194 = f32[2,2048,512]{2,1,0:T(8,128)} fusion(bf16[2,1024,2048]{2,1,0:T(8,128)(2,1)} %copy-done.208, bf16[2,1024,512]{2,1,0:T(8,128)(2,1)S(1)} %bitcast.426), kind=kOutput, calls=%fused_computation.376 | convolution fusion | flops 4294967296 | bytes 18874368 | tf_op jit(solution)/shard_map/erf,erd->efd/dot_general | solution.py:89
  479.1 22.7 %all-to-all-done.6 = bf16[16,128,512]{2,1,0:T(8,128)(2,1)} async-done(((bf16[16,128,512]{2,1,0:T(8,128)(2,1)}), bf16[16,128,512]{2,1,0:T(8,128)(2,1)}, u32[]{:S(2)}, u32[]{:S(2)}) %all-to-all-start.6) | async-done | bytes 2097184 | tf_op jit(solution)/shard_map/all_to_all | solution.py:220
  504.9 13.1 %add_convert_fusion = bf16[2,2048,512]{2,1,0:T(8,128)(2,1)} fusion(f32[2,2048,512]{2,1,0:T(8,128)} %fusion.194, bf16[2,1024,512]{2,1,0:T(8,128)(2,1)S(1)} %bitcast.428, f32[2,1024,2048]{2,1,0:T(8,128)} %fusion.188), kind=kOutput, calls=%fused_computation.28 | convolution fusion | flops 4336910336 | bytes 31457280 | tf_op jit(solution)/shard_map/erf,erd->efd/dot_general | solution.py:89
  518.0 20.5 %fusion.13 = bf16[2,1024,2048]{2,1,0:T(8,128)(2,1)} fusion(f32[2,1024,2048]{2,1,0:T(8,128)} %fusion.188, bf16[2,1024,512]{2,1,0:T(8,128)(2,1)} %bitcast.429, bf16[2,2048,512]{2,1,0:T(8,128)(2,1)} %all-gather.5.cloned.1.call-done), kind=kOutput, calls=%fused_computation.25 | convolution fusion | flops 4378853376 | bytes 31457280 | tf_op jit(solution)/shard_map/erd,efd->erf/dot_general | solution.py:87
  538.5 8.5 convolution_convert_fusion.4
  555.3 19.9 %fusion.6 = bf16[2,1024,2048]{2,1,0:T(8,128)(2,1)} fusion(f32[2,1024,2048]{2,1,0:T(8,128)} %get-tuple-element.359, bf16[2,1024,512]{2,1,0:T(8,128)(2,1)} %bitcast.427, bf16[2,2048,512]{2,1,0:T(8,128)(2,1)} %all-gather.5.cloned.1.call-done), kind=kOutput, calls=%fused_computation.18 | convolution fusion | flops 4378853376 | bytes 31457280 | tf_op jit(solution)/shard_map/erd,efd->erf/dot_general | solution.py:87
  575.2 8.5 convolution_convert_fusion.5
  587.2 15.7 %all-to-all-done.7 = bf16[2,1024,512]{2,0,1:T(2,128)(2,1)} async-done(((bf16[2,1024,512]{2,0,1:T(2,128)(2,1)}), bf16[2,1024,512]{2,0,1:T(2,128)(2,1)}, u32[]{:S(2)}, u32[]{:S(2)}) %all-to-all-start.7) | async-done | bytes 2097184 | tf_op jit(solution)/shard_map/all_to_all | solution.py:233
  609.6 7.9 fusion.193
  617.5 9.8 %add_convert_fusion.1 = bf16[2,512,2048]{2,1,0:T(8,128)(2,1)} fusion(f32[2,512,2048]{2,1,0:T(8,128)S(1)} %fusion.193, bf16[2,1024,512]{2,1,0:T(8,128)(2,1)S(1)} %bitcast.423, bf16[2,1024,2048]{2,1,0:T(8,128)(2,1)} %fusion.13), kind=kOutput, calls=%fused_computation.29 | convolution fusion | flops 4299161600 | bytes 23068672 | tf_op jit(solution)/shard_map/erd,erf->edf/dot_general | solution.py:90
  630.7 5.8 gather_fusion.3
  636.6 18.5 %all-to-all-done.5 = bf16[2,1024,512]{2,0,1:T(2,128)(2,1)} async-done(((bf16[2,1024,512]{2,0,1:T(2,128)(2,1)}), bf16[2,1024,512]{2,0,1:T(2,128)(2,1)}, u32[]{:S(2)}, u32[]{:S(2)}) %all-to-all-start.5) | async-done | bytes 2097184 | tf_op jit(solution)/shard_map/all_to_all | solution.py:233
  658.4 7.0 gather_fusion.2
  785.4 40.2 %all-reduce.6 = (f32[512]{0:T(512)}, f32[512]{0:T(512)}, f32[512,24]{0,1:T(8,128)}, f32[512]{0:T(512)}, f32[512]{0:T(512)}, /*index=5*/f32[512,16]{0,1:T(8,128)}, f32[512]{0:T(512)}, f32[1]{0:T(128)}) all-reduce(f32[512]{0:T(512)S(1)} %add.604, f32[512]{0:T(512)S(1)} %add.605, ...), channel_id=1, replica_groups=mesh['expert'=8,'hidden'=4] {'expert','hidden'}, use_global_device_ids=true, to_apply=%region_65.66 | all-reduce | flops 23041 | bytes 184328 | tf_op jit(solution)/shard_map/psum | solution.py:295
  831.4 92.1 %all-reduce.5.cloned.1.call-done = (f32[512,1536]{1,0:T(8,128)}, f32[512,64]{0,1:T(8,128)}, f32[512,64]{0,1:T(8,128)}, f32[1536,512]{1,0:T(8,128)}) async-done(((f32[512,1536]{1,0:T(8,128)}, f32[512,64]{0,1:T(8,128)}, f32[512,64]{0,1:T(8,128)}, f32[1536,512]{1,0:T(8,128)}), (f32[512,1536]{1,0:T(8,128)}, f32[512,64]{0,1:T(8,128)}, f32[512,64]{0,1:T(8,128)}, ...) | async-done | bytes 6553616 | tf_op jit(solution)/shard_map/psum | solution.py:295
  (706 shorter events, 393.1 us)
Async XLA Ops:
  7.2 111.5 %copy-start = (bf16[1536,512]{1,0:T(8,128)(2,1)S(1)}, bf16[1536,512]{1,0:T(8,128)(2,1)}, u32[]{:S(2)}) copy-start(bf16[1536,512]{1,0:T(8,128)(2,1)} %param.32) | copy-start | bytes 4718596
  7.2 198.2 %all-gather.3.cloned.1.call-start = ((), (), s32[]{:S(2)}) async-start(), calls=%async_computation.10 | async-start | bytes 5242880 | tf_op jit(solution)/shard_map/all_gather | solution.py:127
  7.9 210.6 %all-gather.5.cloned.1.call-start = ((), (), s32[]{:S(2)}) async-start(), calls=%async_computation.11 | async-start | bytes 5242880 | tf_op jit(solution)/shard_map/all_gather | solution.py:128
  13.8 441.7 %copy-start.5 = (bf16[1,512,512]{1,2,0:T(8,128)(2,1)}, bf16[1,512,512]{1,2,0:T(8,128)(2,1)S(1)}, u32[]{:S(2)}) copy-start(bf16[1,512,512]{1,2,0:T(8,128)(2,1)S(1)} %copy.704) | copy-start | bytes 1572868
  14.3 365.7 %copy-start.7 = (bf16[1,512,512]{1,2,0:T(8,128)(2,1)}, bf16[1,512,512]{1,2,0:T(8,128)(2,1)S(1)}, u32[]{:S(2)}) copy-start(bf16[1,512,512]{1,2,0:T(8,128)(2,1)S(1)} %copy.705) | copy-start | bytes 1572868
  15.7 38.6 %copy-start.14 = (bf16[512,512]{0,1:T(8,128)(2,1)}, bf16[512,512]{0,1:T(8,128)(2,1)S(1)}, u32[]{:S(2)}) copy-start(bf16[512,512]{0,1:T(8,128)(2,1)S(1)} %get-tuple-element.333) | copy-start | bytes 1572868
  15.9 104.8 %copy-start.73 = (bf16[512,64,1]{0,1,2:T(8,128)(2,1)}, bf16[512,64,1]{0,1,2:T(8,128)(2,1)S(1)}, u32[]{:S(2)}) copy-start(bf16[512,64,1]{0,1,2:T(8,128)(2,1)S(1)} %fusion.62) | copy-start | bytes 196612
  17.0 97.3 %copy-start.75 = (bf16[512,64,1]{0,1,2:T(8,128)(2,1)}, bf16[512,64,1]{0,1,2:T(8,128)(2,1)S(1)}, u32[]{:S(2)}) copy-start(bf16[512,64,1]{0,1,2:T(8,128)(2,1)S(1)} %fusion.64) | copy-start | bytes 196612
  20.1 75.2 %copy-start.44 = (s32[512,4]{1,0:T(8,128)}, s32[512,4]{1,0:T(8,128)S(1)}, u32[]{:S(2)}) copy-start(s32[512,4]{1,0:T(8,128)S(1)} %copy.585) | copy-start | bytes 24580
  37.1 47.5 %copy-start.105 = (f32[512,4]{0,1:T(4,128)}, f32[512,4]{0,1:T(4,128)S(1)}, u32[]{:S(2)}) copy-start(f32[512,4]{0,1:T(4,128)S(1)} %copy.588) | copy-start | bytes 24580
  50.4 36.7 %copy-start.103 = (f32[512,4]{0,1:T(4,128)}, f32[512,4]{0,1:T(4,128)S(1)}, u32[]{:S(2)}) copy-start(f32[512,4]{0,1:T(4,128)S(1)} %copy.611) | copy-start | bytes 24580
  87.8 27.9 %copy-start.122 = (f32[512,4]{0,1:T(4,128)}, f32[512,4]{0,1:T(4,128)S(1)}, u32[]{:S(2)}) copy-start(f32[512,4]{0,1:T(4,128)S(1)} %fusion.156) | copy-start | bytes 24580
  141.8 55.7 %all-to-all-start.2 = ((bf16[16,128,512]{2,1,0:T(8,128)(2,1)}), bf16[16,128,512]{2,1,0:T(8,128)(2,1)}, u32[]{:S(2)}, u32[]{:S(2)}) async-start(bf16[16,128,512]{2,1,0:T(8,128)(2,1)} %bitcast.410), calls=%async_computation.2 | async-start | bytes 4194304 | tf_op jit(solution)/shard_map/all_to_all | solution.py:196
  197.6 52.6 %all-to-all-start = ((bf16[16,128,512]{2,1,0:T(8,128)(2,1)}), bf16[16,128,512]{2,1,0:T(8,128)(2,1)}, u32[]{:S(2)}, u32[]{:S(2)}) async-start(bf16[16,128,512]{2,1,0:T(8,128)(2,1)} %bitcast.411), calls=%async_computation | async-start | bytes 4194304 | tf_op jit(solution)/shard_map/all_to_all | solution.py:196
  250.1 52.3 %all-to-all-start.3 = ((bf16[2,1024,512]{2,0,1:T(2,128)(2,1)}), bf16[2,1024,512]{2,0,1:T(2,128)(2,1)}, u32[]{:S(2)}, u32[]{:S(2)}) async-start(bf16[2,1024,512]{2,0,1:T(2,128)(2,1)} %copy.627), calls=%async_computation.3 | async-start | bytes 4194304 | tf_op jit(solution)/shard_map/all_to_all | solution.py:205
  302.5 52.4 %all-to-all-start.1 = ((bf16[2,1024,512]{2,0,1:T(2,128)(2,1)}), bf16[2,1024,512]{2,0,1:T(2,128)(2,1)}, u32[]{:S(2)}, u32[]{:S(2)}) async-start(bf16[2,1024,512]{2,0,1:T(2,128)(2,1)} %copy.604), calls=%async_computation.1 | async-start | bytes 4194304 | tf_op jit(solution)/shard_map/all_to_all | solution.py:205
  311.2 68.9 %copy-start.18 = (bf16[1,512,512]{1,2,0:T(8,128)(2,1)}, bf16[1,512,512]{1,2,0:T(8,128)(2,1)S(1)}, u32[]{:S(2)}) copy-start(bf16[1,512,512]{1,2,0:T(8,128)(2,1)S(1)} %copy.706) | copy-start | bytes 1572868
  318.2 39.9 %copy-start.140 = (s32[1024]{0:T(1024)}, s32[1024]{0:T(1024)S(1)}, u32[]{:S(2)}) copy-start(s32[1024]{0:T(1024)S(1)} %broadcast_clamp_fusion.1) | copy-start | bytes 12292
  397.3 52.3 %all-to-all-start.4 = ((bf16[16,128,512]{2,1,0:T(8,128)(2,1)}), bf16[16,128,512]{2,1,0:T(8,128)(2,1)}, u32[]{:S(2)}, u32[]{:S(2)}) async-start(bf16[16,128,512]{2,1,0:T(8,128)(2,1)} %bitcast.409), calls=%async_computation.4 | async-start | bytes 4194304 | tf_op jit(solution)/shard_map/all_to_all | solution.py:220
  402.6 289.6 %copy-start.135 = (f32[512]{0:T(512)}, f32[512]{0:T(512)S(1)}, u32[]{:S(2)}) copy-start(f32[512]{0:T(512)S(1)} %get-tuple-element.276) | copy-start | bytes 6148
  418.8 36.7 %copy-start.113 = (f32[512]{0:T(512)S(1)}, f32[512]{0:T(512)}, u32[]{:S(2)}) copy-start(f32[512]{0:T(512)} %param.26) | copy-start | bytes 6148
  418.8 36.7 %copy-start.116 = (f32[512]{0:T(512)S(1)}, f32[512]{0:T(512)}, u32[]{:S(2)}) copy-start(f32[512]{0:T(512)} %copy-done.115) | copy-start | bytes 6148
  418.8 36.7 %copy-start.133 = (f32[512]{0:T(512)S(1)}, f32[512]{0:T(512)}, u32[]{:S(2)}) copy-start(f32[512]{0:T(512)} %copy-done.132) | copy-start | bytes 6148
  418.8 36.7 %copy-start.177 = (f32[512]{0:T(512)S(1)}, f32[512]{0:T(512)}, u32[]{:S(2)}) copy-start(f32[512]{0:T(512)} %param.27) | copy-start | bytes 6148
  418.8 37.7 %copy-start.27 = (f32[512,512]{1,0:T(8,128)S(1)}, f32[512,512]{1,0:T(8,128)}, u32[]{:S(2)}) copy-start(f32[512,512]{1,0:T(8,128)} %copy-done.26) | copy-start | bytes 3145732
  449.6 52.2 %all-to-all-start.6 = ((bf16[16,128,512]{2,1,0:T(8,128)(2,1)}), bf16[16,128,512]{2,1,0:T(8,128)(2,1)}, u32[]{:S(2)}, u32[]{:S(2)}) async-start(bf16[16,128,512]{2,1,0:T(8,128)(2,1)} %bitcast.408), calls=%async_computation.6 | async-start | bytes 4194304 | tf_op jit(solution)/shard_map/all_to_all | solution.py:220
  454.0 371.6 %reduce-scatter.5.cloned.1.call-start = ((), (), s32[]{:S(2)}) async-start(), calls=%async_computation.13 | async-start | bytes 5242880 | tf_op jit(solution)/shard_map/reduce_scatter | solution.py:317
  550.5 52.4 %all-to-all-start.7 = ((bf16[2,1024,512]{2,0,1:T(2,128)(2,1)}), bf16[2,1024,512]{2,0,1:T(2,128)(2,1)}, u32[]{:S(2)}, u32[]{:S(2)}) async-start(bf16[2,1024,512]{2,0,1:T(2,128)(2,1)} %copy.656), calls=%async_computation.7 | async-start | bytes 4194304 | tf_op jit(solution)/shard_map/all_to_all | solution.py:233
  602.9 52.2 %all-to-all-start.5 = ((bf16[2,1024,512]{2,0,1:T(2,128)(2,1)}), bf16[2,1024,512]{2,0,1:T(2,128)(2,1)}, u32[]{:S(2)}, u32[]{:S(2)}) async-start(bf16[2,1024,512]{2,0,1:T(2,128)(2,1)} %copy.634), calls=%async_computation.5 | async-start | bytes 4194304 | tf_op jit(solution)/shard_map/all_to_all | solution.py:233
  607.3 221.2 %reduce-scatter.3.cloned.1.call-start = ((), (), s32[]{:S(2)}) async-start(), calls=%async_computation.12 | async-start | bytes 5242880 | tf_op jit(solution)/shard_map/reduce_scatter | solution.py:314
  627.3 296.2 %all-reduce.5.cloned.1.call-start = ((), (), s32[]{:S(2)}) async-start(), calls=%async_computation.14 | async-start | bytes 13107200 | tf_op jit(solution)/shard_map/psum | solution.py:295
  636.6 21.8 %copy-start.141 = (s32[1024]{0:T(1024)S(1)}, s32[1024]{0:T(1024)}, u32[]{:S(2)}) copy-start(s32[1024]{0:T(1024)} %copy-done.140) | copy-start | bytes 12292
  (190 other events, 921.7 us)
Sparse Core Ops, SparseCore 0:
  9.6 37.1 all-gather.2
  48.4 34.5 all-gather.4
  518.1 43.5 reduce-scatter.4
  627.4 45.7 reduce-scatter.2
  764.6 158.8 all-reduce.4
where the time goes:
time: 944 us; the launch traced here: 937 us
  waiting for transfers between devices  270 us (29%)
  local copies, waits for them, and re-layouts  224 us (24%)
  matrix products  212 us (22%)
  other arithmetic  133 us (14%)
  blocking collectives  40.2 us (4%)
  starting transfers between devices  39.6 us (4%)
  between operations  18.8 us (2%)
    psum x1, waiting for transfers between devices, per_device(): lax.psum((grad_gain_one, grad_bias_one, grad_router_attn, grad_query_w, g...  92.1 us
    all_to_all x2, waiting for transfers between devices, per_device(): lax.all_to_all(grad_buffer.reshape(experts_all, capacity, width), 'expert...  53.6 us
    all_to_all x2, waiting for transfers between devices, per_device(): lax.all_to_all(outgoing.reshape(experts_all, capacity, width), 'expert',...  47.6 us
    all_to_all x2, waiting for transfers between devices, per_device(): lax.all_to_all(outgoing_back, 'expert', split_axis=1, concat_axis=0, tile...  41.4 us
    dot_general x2, matrix products, expert_backward(): jnp.einsum('erd,efd->erf', grad_rows_in, second, preferred_element_type=j...  40.4 us
    psum x1, blocking collectives, per_device(): lax.psum((grad_gain_one, grad_bias_one, grad_router_attn, grad_query_w, g...  40.2 us
    all_to_all x2, waiting for transfers between devices, per_device(): lax.all_to_all(back_rows, 'expert', split_axis=1, concat_axis=0, tiled=True)  34.2 us
    unnamed x431, local copies, waits for them, and re-layouts  27 us
  transfers between devices with their start and end apart: 13, of which 9 were waited for; matrix products, arithmetic and copies ran while one was open for 53% of the time, Pallas kernels for 0%

commit v1 on v0

v1 whole, which is shorter than its diff:
```python
import functools
import math

import jax
import jax.numpy as jnp
from jax import lax
from jax.experimental import pallas as pl
from jax.experimental.pallas import tpu as pltpu
from jax.sharding import PartitionSpec as P

SEQ = 256
LANES = 128
F32 = jnp.float32
BF16 = jnp.bfloat16
GELU_C = math.sqrt(2.0 / math.pi)
GELU_A = 0.044715
VMEM_LIMIT = 60 * 1024 * 1024


def mm(left, right):
    return jnp.dot(left, right, preferred_element_type=F32)


def mm_nt(left, right):
    return lax.dot_general(left, right, (((1,), (1,)), ((), ())), preferred_element_type=F32)


def mm_tn(left, right):
    return lax.dot_general(left, right, (((0,), (0,)), ((), ())), preferred_element_type=F32)


def lane_iota(rows, lanes=LANES):
    return lax.broadcasted_iota(jnp.int32, (rows, lanes), 1)


def norm_parts(value):
    center = value - jnp.mean(value, axis=-1, keepdims=True)
    rstd = lax.rsqrt(jnp.mean(center * center, axis=-1, keepdims=True) + 1e-05)
    return center * rstd, rstd


def norm_back(hat, rstd, gain, grad):
    scaled = grad * gain
    first = jnp.mean(scaled, axis=-1, keepdims=True)
    second = jnp.mean(scaled * hat, axis=-1, keepdims=True)
    return rstd * (scaled - first - hat * second)


def fold_rows(value):
    return jnp.sum(value, axis=0, keepdims=True)


def pick_head(tiles, route, lane):
    pair = lax.shift_right_logical(route, 1)
    out = tiles[0]
    for j in range(1, len(tiles)):
        out = jnp.where(pair == j, tiles[j], out)
    odd = (route & 1) == 1
    return jnp.where(odd, pltpu.roll(out, LANES // 2, 1), out)


def place_heads(parts, routes, count, lane):
    half = lax.shift_right_logical(lane, 6)
    kept = [jnp.where(half == (r & 1), p, 0.0) for p, r in zip(parts, routes)]
    pairs = [lax.shift_right_logical(r, 1) for r in routes]
    tiles = []
    for j in range(count):
        total = jnp.where(pairs[0] == j, kept[0], 0.0)
        for k, p in zip(kept[1:], pairs[1:]):
            total = total + jnp.where(p == j, k, 0.0)
        tiles.append(total)
    return tiles


def softmax_cols(cols):
    top = functools.reduce(jnp.maximum, cols)
    expo = [jnp.exp(c - top) for c in cols]
    total = functools.reduce(jnp.add, expo)
    return [e / total for e in expo]


def put_cols(cols, rows, width):
    lane = lane_iota(rows, width)
    out = jnp.zeros((rows, width), cols[0].dtype)
    for i, c in enumerate(cols):
        out = jnp.where(lane == i, c, out)
    return out


def split_three(value):
    high = value.astype(BF16)
    rest = value - high.astype(F32)
    middle = rest.astype(BF16)
    last = (rest - middle.astype(F32)).astype(BF16)
    return jnp.concatenate([high.astype(F32), middle.astype(F32), last.astype(F32)], axis=0).astype(BF16)


def join_three(value):
    n = value.shape[0] // 3
    return value[:n] + value[n : 2 * n] + value[2 * n :]


def row_to_col(row):
    n = row.shape[1]
    place = lax.broadcasted_iota(jnp.int32, (n, n), 0)
    other = lax.broadcasted_iota(jnp.int32, (n, n), 1)
    return jnp.sum(jnp.where(place == other, row, 0.0), axis=-1, keepdims=True)


def dispatch(slot_rows, values, out_ref):
    chunk = 256
    tokens = values[0].shape[0]
    spot = lax.broadcasted_iota(jnp.int32, (chunk, tokens), 0)

    def body(k, carry):
        base = spot + k * chunk
        if len(values) == 1:
            pick = jnp.where((base == slot_rows[0]) | (base == slot_rows[1]), 1.0, 0.0).astype(BF16)
            out = mm(pick, values[0][...])
        else:
            out = mm(jnp.where(base == slot_rows[0], 1.0, 0.0).astype(BF16), values[0][...])
            out = out + mm(jnp.where(base == slot_rows[1], 1.0, 0.0).astype(BF16), values[1][...])
        out_ref[pl.ds(pl.multiple_of(k * chunk, chunk), chunk), :] = out.astype(BF16)
        return carry

    lax.fori_loop(0, out_ref.shape[0] // chunk, body, 0)


def route_kernel(capacity, row_ref, col_ref, grad_ref, slotrow_ref, slotcol_ref, out_ref):
    tokens = grad_ref.shape[1]
    before = lax.broadcasted_iota(jnp.int32, (tokens, tokens), 0)
    after = lax.broadcasted_iota(jnp.int32, (tokens, tokens), 1)
    upper = jnp.where(before < after, 1.0, 0.0).astype(BF16)
    lower = jnp.where(before > after, 1.0, 0.0).astype(BF16)
    sub = lax.broadcasted_iota(jnp.int32, (LANES, tokens), 0)
    row = row_ref[0]
    named = [jnp.where(sub == row[2 + i : 3 + i, :], 1.0, 0.0) for i in range(2)]
    rank = mm((named[0] + named[1]).astype(BF16), upper)
    slots = [
        fold_rows(named[i] * rank).astype(jnp.int32) + row[2 + i : 3 + i, :] * capacity for i in range(2)
    ]
    sub8 = lax.broadcasted_iota(jnp.int32, (8, tokens), 0)
    slotrow_ref[...] = jnp.where(sub8 == 0, slots[0], slots[1])
    lanes = lane_iota(tokens)
    col = col_ref[0]
    named_c = [jnp.where(lanes == col[:, 4 + i : 5 + i], 1.0, 0.0) for i in range(2)]
    rank_c = mm(lower, (named_c[0] + named_c[1]).astype(BF16))
    slots_c = [
        jnp.sum(named_c[i] * rank_c, axis=-1, keepdims=True).astype(jnp.int32) + col[:, 4 + i : 5 + i] * capacity
        for i in range(2)
    ]
    slotcol_ref[...] = put_cols(slots_c, tokens, slotcol_ref.shape[1])
    dispatch(slots, [grad_ref.at[0]], out_ref)


def route_step(micro, row, col, grad, slots, capacity):
    _, count, width = grad.shape
    out_shape = (
        jax.ShapeDtypeStruct((8, count), jnp.int32),
        jax.ShapeDtypeStruct((count, 8), jnp.int32),
        jax.ShapeDtypeStruct((slots, width), BF16),
    )
    return pl.pallas_call(
        functools.partial(route_kernel, capacity),
        grid=(1,),
        out_shape=out_shape,
        in_specs=[
            pl.BlockSpec((1, 8, count), lambda i: (micro, 0, 0)),
            pl.BlockSpec((1, count, 8), lambda i: (micro, 0, 0)),
            pl.BlockSpec((1, count, width), lambda i: (micro, 0, 0)),
        ],
        out_specs=[pl.BlockSpec(o.shape, lambda i: (0, 0)) for o in out_shape],
        compiler_params=pltpu.CompilerParams(vmem_limit_bytes=VMEM_LIMIT),
        cost_estimate=pl.CostEstimate(flops=2 * count * width * slots, bytes_accessed=3 << 20, transcendentals=0),
        name="route_step",
    )(row, col, grad)


def attention_forward_kernel(
    x_ref, grad_ref, col_ref, row_ref, slotrow_ref, vec_ref, hb_ref, qw_ref, kvr_ref, proj_ref, frw_ref,
    mid_ref, n2_ref, normed_ref, mixed_ref, probs_ref, qs_ref, kv_ref, gates_ref, scal_ref, out_ref,
    n2_all,
):
    step = pl.program_id(0)
    rows = x_ref.shape[1]
    top_attn = 4
    lane = lane_iota(rows)
    x = x_ref[0].astype(F32)
    col = col_ref[0]
    row = row_ref[0]
    hat, _ = norm_parts(x)
    normed = (hat * vec_ref[0:1, :] + vec_ref[1:2, :]).astype(BF16)
    normed_ref[...] = normed
    kvr = mm(normed, kvr_ref[...])
    kv = kvr[:, :LANES].astype(BF16)
    kv_ref[...] = kv
    logits = kvr[:, LANES:]
    routes = [col[:, i : i + 1] for i in range(top_attn)]
    picked = [
        jnp.sum(jnp.where(lane == r, logits, 0.0), axis=-1, keepdims=True) for r in routes
    ]
    gates = softmax_cols(picked)
    query = mm(normed, qw_ref[...])
    heads_pairs = query.shape[1] // LANES
    tiles = [query[:, j * LANES : (j + 1) * LANES] for j in range(heads_pairs)]
    low = lane < LANES // 2
    same = col[:, 6:7] == row[0:1, :]
    place = lax.broadcasted_iota(jnp.int32, (rows, rows), 0)
    other = lax.broadcasted_iota(jnp.int32, (rows, rows), 1)
    allowed = same & ((row[1:2, :] == 1) | (place == other))
    scale = 0.125
    shares = []
    for i in range(top_attn):
        sel = jnp.where(low, pick_head(tiles, routes[i], lane), 0.0).astype(BF16)
        qs_ref[0, i] = sel
        scores = mm_nt(sel, kv) * scale
        scores = jnp.where(allowed, scores, -1e30)
        expo = jnp.exp(scores - jnp.max(scores, axis=-1, keepdims=True))
        probs = (expo * (1.0 / jnp.sum(expo, axis=-1, keepdims=True))).astype(BF16)
        probs_ref[0, i] = probs
        heads = mm(probs, kv) * gates[i]
        shares.append(jnp.where(low, pltpu.roll(heads, LANES // 2, 1), heads))
    mixed_tiles = place_heads(shares, routes, heads_pairs, lane)
    mixed = jnp.concatenate([t.astype(BF16) for t in mixed_tiles], axis=1)
    mixed_ref[...] = mixed
    mid = x + mm(mixed, proj_ref[...])
    mid_ref[...] = mid
    hat2, _ = norm_parts(mid)
    n2 = (hat2 * vec_ref[2:3, :] + vec_ref[3:4, :]).astype(BF16)
    n2_ref[...] = n2
    n2_all[pl.ds(pl.multiple_of(step * rows, rows), rows), :] = n2
    logits_ffn = mm(n2, frw_ref[...])
    gates_ffn = softmax_cols(
        [
            jnp.sum(jnp.where(lane == col[:, 4 + i : 5 + i], logits_ffn, 0.0), axis=-1, keepdims=True)
            for i in range(2)
        ]
    )
    gates_ref[...] = put_cols(gates, rows, gates_ref.shape[1])
    stop = jnp.sum(mid * vec_ref[4:5, :], axis=-1, keepdims=True) + hb_ref[0:1, 0:1]
    pull = jnp.sum(grad_ref[0].astype(F32) * (mid - x), axis=-1, keepdims=True)
    scal_ref[...] = jnp.transpose(put_cols([stop, pull] + gates_ffn, rows, LANES))[:8, :]

    @pl.when(step == pl.num_programs(0) - 1)
    def _():
        dispatch([slotrow_ref[0:1, :], slotrow_ref[1:2, :]], [n2_all], out_ref)


def attention_forward(micro, tokens, grad, col, row, slotrow, vec, hb, qw, kvr, proj, frw, slots):
    _, count, width = tokens.shape
    steps = count // SEQ
    inner = qw.shape[1]
    whole = lambda a: pl.BlockSpec(a.shape, lambda r: (0,) * a.ndim)
    out_shape = (
        jax.ShapeDtypeStruct((count, width), F32),
        jax.ShapeDtypeStruct((count, width), BF16),
        jax.ShapeDtypeStruct((count, width), BF16),
        jax.ShapeDtypeStruct((count, inner), BF16),
        jax.ShapeDtypeStruct((steps, 4, SEQ, SEQ), BF16),
        jax.ShapeDtypeStruct((steps, 4, SEQ, LANES), BF16),
        jax.ShapeDtypeStruct((count, LANES), BF16),
        jax.ShapeDtypeStruct((count, 8), F32),
        jax.ShapeDtypeStruct((8, count), F32),
        jax.ShapeDtypeStruct((slots, width), BF16),
    )
    by_row = lambda c: pl.BlockSpec((SEQ, c), lambda r: (r, 0))
    return pl.pallas_call(
        attention_forward_kernel,
        grid=(steps,),
        out_shape=out_shape,
        in_specs=[
            pl.BlockSpec((1, SEQ, width), lambda r: (micro, r, 0)),
            pl.BlockSpec((1, SEQ, width), lambda r: (micro, r, 0)),
            pl.BlockSpec((1, SEQ, 8), lambda r: (micro, r, 0)),
            pl.BlockSpec((1, 8, SEQ), lambda r: (micro, 0, r)),
            whole(slotrow), whole(vec), whole(hb), whole(qw), whole(kvr), whole(proj), whole(frw),
        ],
        out_specs=[
            by_row(width), by_row(width), by_row(width), by_row(inner),
            pl.BlockSpec((1, 4, SEQ, SEQ), lambda r: (r, 0, 0, 0)),
            pl.BlockSpec((1, 4, SEQ, LANES), lambda r: (r, 0, 0, 0)),
            by_row(LANES), by_row(8),
            pl.BlockSpec((8, SEQ), lambda r: (0, r)),
            pl.BlockSpec((slots, width), lambda r: (0, 0)),
        ],
        scratch_shapes=[pltpu.VMEM((count, width), BF16)],
        compiler_params=pltpu.CompilerParams(vmem_limit_bytes=VMEM_LIMIT),
        cost_estimate=pl.CostEstimate(
            flops=2 * count * width * (2 * inner + 256 + slots), bytes_accessed=12 << 20, transcendentals=count * 4 * SEQ
        ),
        name="attention_forward",
    )(tokens, grad, col, row, slotrow, vec, hb, qw, kvr, proj, frw)


def gelu_parts(pre):
    square = pre * pre
    inner = jnp.tanh(GELU_C * pre * (1.0 + GELU_A * square))
    return square, inner


def expert_forward_kernel(rows_ref, grad_ref, vec_ref, first_ref, second_ref, out_ref, scal_ref, total):
    part = pl.program_id(1)
    src, _, cap, width = rows_ref.shape
    rows = rows_ref[...].reshape(src * cap, width)
    pre = mm(rows, first_ref[0, 0])
    _, inner = gelu_parts(pre)
    act = (0.5 * pre * (1.0 + inner)).astype(BF16)
    res = mm(act, second_ref[0, 0])

    @pl.when(part == 0)
    def _():
        total[...] = res

    @pl.when(part > 0)
    def _():
        total[...] += res

    @pl.when(part == pl.num_programs(1) - 1)
    def _():
        halt = split_three(jnp.broadcast_to(vec_ref[4:5, :], (8, width)))
        ones = jnp.ones((8, width), BF16)
        sub8 = lax.broadcasted_iota(jnp.int32, (8, cap), 0)
        for s in range(src):
            low = total[s * cap : (s + 1) * cap, :].astype(BF16)
            out_ref[s, 0] = low
            stop = join_three(mm_nt(halt, low))
            prod = low.astype(F32) * grad_ref[s, 0].astype(F32)
            high = prod.astype(BF16)
            rest = (prod - high.astype(F32)).astype(BF16)
            pull = mm_nt(ones, high) + mm_nt(ones, rest)
            scal_ref[s, 0] = jnp.where(sub8 == 0, stop, pull)


def expert_forward(rows, grad, vec, first, second):
    src, local, cap, width = rows.shape
    parts, _, _, hid = first.shape
    spec_rows = pl.BlockSpec((src, 1, cap, width), lambda e, h: (0, e, 0, 0))
    return pl.pallas_call(
        expert_forward_kernel,
        grid=(local, parts),
        out_shape=(
            jax.ShapeDtypeStruct(rows.shape, BF16),
            jax.ShapeDtypeStruct((src, local, 8, cap), F32),
        ),
        in_specs=[
            spec_rows,
            spec_rows,
            pl.BlockSpec(vec.shape, lambda e, h: (0, 0)),
            pl.BlockSpec((1, 1, width, hid), lambda e, h: (h, e, 0, 0)),
            pl.BlockSpec((1, 1, hid, width), lambda e, h: (h, e, 0, 0)),
        ],
        out_specs=[spec_rows, pl.BlockSpec((src, 1, 8, cap), lambda e, h: (0, e, 0, 0))],
        scratch_shapes=[pltpu.VMEM((src * cap, width), F32)],
        compiler_params=pltpu.CompilerParams(vmem_limit_bytes=VMEM_LIMIT),
        cost_estimate=pl.CostEstimate(
            flops=4 * src * local * cap * width * hid * parts,
            bytes_accessed=6 * src * local * cap * width + 4 * local * parts * width * hid,
            transcendentals=src * local * cap * hid * parts,
        ),
        name="expert_forward",
    )(rows, grad, vec, first, second)


def expert_backward_kernel(add_old, *refs):
    rows_ref, grad_ref, ab_ref, vec_ref, first_ref, second_ref = refs[:6]
    refs = refs[6:]
    if add_old:
        old_first_ref, old_second_ref = refs[:2]
        refs = refs[2:]
    gfirst_ref, gsecond_ref, out_ref, total, gin_all = refs
    part = pl.program_id(1)
    src, _, cap, width = rows_ref.shape

    @pl.when(part == 0)
    def _():
        for s in range(src):
            ab = ab_ref[s, 0]
            scaled = row_to_col(ab[0:1, :]) * grad_ref[s, 0].astype(F32) + row_to_col(ab[1:2, :]) * vec_ref[4:5, :]
            gin_all[s * cap : (s + 1) * cap, :] = scaled.astype(BF16)

    rows = rows_ref[...].reshape(src * cap, width)
    gin = gin_all[...]
    first = first_ref[0, 0]
    second = second_ref[0, 0]
    pre = mm(rows, first)
    gact = mm_nt(gin, second)
    square, inner = gelu_parts(pre)
    half = 0.5 * (1.0 + inner)
    act = (pre * half).astype(BF16)
    slope = half + 0.5 * pre * (1.0 - inner * inner) * (GELU_C + (3.0 * GELU_C * GELU_A) * square)
    gpre = (gact * slope).astype(BF16)
    gsecond = mm_tn(act, gin)
    gfirst = mm_tn(rows, gpre)
    if add_old:
        gsecond = gsecond + old_second_ref[0, 0].astype(F32)
        gfirst = gfirst + old_first_ref[0, 0].astype(F32)
    gsecond_ref[0, 0] = gsecond.astype(BF16)
    gfirst_ref[0, 0] = gfirst.astype(BF16)
    res = mm_nt(gpre, first)

    @pl.when(part == 0)
    def _():
        total[...] = res

    @pl.when(part > 0)
    def _():
        total[...] += res

    @pl.when(part == pl.num_programs(1) - 1)
    def _():
        out_ref[...] = total[...].astype(BF16).reshape(out_ref.shape)


def expert_backward(rows, grad, ab, vec, first, second, old):
    src, local, cap, width = rows.shape
    parts, _, _, hid = first.shape
    spec_rows = pl.BlockSpec((src, 1, cap, width), lambda e, h: (0, e, 0, 0))
    spec_first = pl.BlockSpec((1, 1, width, hid), lambda e, h: (h, e, 0, 0))
    spec_second = pl.BlockSpec((1, 1, hid, width), lambda e, h: (h, e, 0, 0))
    return pl.pallas_call(
        functools.partial(expert_backward_kernel, bool(old)),
        grid=(local, parts),
        out_shape=(
            jax.ShapeDtypeStruct(first.shape, BF16),
            jax.ShapeDtypeStruct(second.shape, BF16),
            jax.ShapeDtypeStruct(rows.shape, BF16),
        ),
        in_specs=[
            spec_rows, spec_rows,
            pl.BlockSpec((src, 1, 8, cap), lambda e, h: (0, e, 0, 0)),
            pl.BlockSpec(vec.shape, lambda e, h: (0, 0)),
            spec_first, spec_second,
        ] + [spec_first, spec_second][: len(old)],
        out_specs=[spec_first, spec_second, spec_rows],
        scratch_shapes=[pltpu.VMEM((src * cap, width), F32), pltpu.VMEM((src * cap, width), BF16)],
        compiler_params=pltpu.CompilerParams(vmem_limit_bytes=VMEM_LIMIT),
        cost_estimate=pl.CostEstimate(
            flops=10 * src * local * cap * width * hid * parts,
            bytes_accessed=6 * src * local * cap * width + 8 * local * parts * width * hid,
            transcendentals=src * local * cap * hid * parts,
        ),
        name="expert_backward",
    )(rows, grad, ab, vec, first, second, *old)


def greet(axis, peers, make_id):
    barrier = pltpu.get_barrier_semaphore()
    me = lax.axis_index(axis)
    for k in range(1, peers):
        pl.semaphore_signal(
            barrier, inc=1, device_id=make_id(lax.rem(me + k, peers)), device_id_type=pl.DeviceIdType.MESH
        )
    pl.semaphore_wait(barrier, peers - 1)
    return me


def scalar_kernel(n_expert, scal_ref, rowsc_ref, slotrow_ref, cols_ref, ab_ref, got, sent, got2, send_sem, recv_sem, send_sem2, recv_sem2):
    local, cap = scal_ref.shape[1], scal_ref.shape[3]
    tokens = rowsc_ref.shape[1]
    other = lax.axis_index("hidden")
    make_id = lambda e: (e, other)
    me = greet("expert", n_expert, make_id)

    def copies(source, target, ssem, rsem):
        out = []
        for k in range(1, n_expert):
            peer = lax.rem(me + k, n_expert)
            out.append(
                pltpu.make_async_remote_copy(
                    source.at[peer], target.at[me], ssem.at[k - 1], rsem.at[k - 1],
                    device_id=make_id(peer), device_id_type=pl.DeviceIdType.MESH,
                )
            )
        return out

    moves = copies(scal_ref, got, send_sem, recv_sem)
    for c in moves:
        c.start()
    got[me] = scal_ref[me]
    for c in moves:
        c.wait()
    slot = [slotrow_ref[i : i + 1, :] for i in range(2)]
    spot = lax.broadcasted_iota(jnp.int32, (cap, tokens), 0)

    def onehot(expert):
        base = spot + expert * cap
        return [jnp.where(base == s, 1.0, 0.0).astype(BF16) for s in slot]

    zero = jnp.zeros((24, tokens), F32)

    def collect(expert, carry):
        values = split_three(got[lax.div(expert, local), lax.rem(expert, local)])
        return tuple(c + mm(values, p) for c, p in zip(carry, onehot(expert)))

    found = lax.fori_loop(0, n_expert * local, collect, (zero, zero))
    found = [join_three(f) for f in found]
    stop, pull, gate0, gate1 = [rowsc_ref[i : i + 1, :] for i in range(4)]
    gates = [gate0, gate1]
    yh = [f[0:1, :] for f in found]
    yg = [f[1:2, :] for f in found]
    halting = jax.nn.sigmoid(stop + gate0 * yh[0] + gate1 * yh[1])
    s = (pull + gate0 * yg[0] + gate1 * yg[1]) * halting * (1.0 - halting)
    u = [halting * g + s * h for g, h in zip(yg, yh)]
    mean = gate0 * u[0] + gate1 * u[1]
    keep = [halting, s, gate0 * (u[0] - mean), gate1 * (u[1] - mean), gate0, gate1]
    sub = lax.broadcasted_iota(jnp.int32, (LANES, tokens), 0)
    table = jnp.zeros((LANES, tokens), F32)
    for i, r in enumerate(keep):
        table = jnp.where(sub == i, r, table)
    cols_ref[...] = jnp.transpose(table)[:, :8]
    sub8 = lax.broadcasted_iota(jnp.int32, (8, tokens), 0)
    ab = [
        split_three(jnp.where(sub8 == 0, g * halting, jnp.where(sub8 == 1, g * s, 0.0))) for g in gates
    ]

    def spread(expert, carry):
        picks = onehot(expert)
        sent[lax.div(expert, local), lax.rem(expert, local)] = join_three(mm_nt(ab[0], picks[0]) + mm_nt(ab[1], picks[1]))
        return carry

    lax.fori_loop(0, n_expert * local, spread, 0)
    moves = copies(sent, got2, send_sem2, recv_sem2)
    for c in moves:
        c.start()
    got2[me] = sent[me]
    for c in moves:
        c.wait()
    ab_ref[...] = got2[...]


def scalar_step(n_expert, scal, rowsc, slotrow):
    vmem = pl.BlockSpec(memory_space=pltpu.VMEM)
    tokens = rowsc.shape[1]
    return pl.pallas_call(
        functools.partial(scalar_kernel, n_expert),
        out_shape=(jax.ShapeDtypeStruct((tokens, 8), F32), jax.ShapeDtypeStruct(scal.shape, F32)),
        in_specs=[vmem] * 3,
        out_specs=[vmem] * 2,
        scratch_shapes=[pltpu.VMEM(scal.shape, F32)] * 3 + [pltpu.SemaphoreType.DMA((n_expert - 1,))] * 4,
        compiler_params=pltpu.CompilerParams(collective_id=0, has_side_effects=True),
        cost_estimate=pl.CostEstimate(flops=10**9, bytes_accessed=1 << 20, transcendentals=tokens),
        name="scalar_step",
    )(scal, rowsc, slotrow)


def result_kernel(has_old, *refs):
    x_ref, mid_ref, ret_ref, cols_ref, slotcol_ref = refs[:5]
    result_ref, hsum_ref = refs[-2:]
    tokens, width = mid_ref.shape
    chunk = 256
    chunks = ret_ref.shape[0] // chunk
    lane = lane_iota(tokens, chunk)
    slot_c = [slotcol_ref[:, i : i + 1] for i in range(2)]

    def gather(k, carry):
        block = ret_ref[pl.ds(pl.multiple_of(k * chunk, chunk), chunk), :]
        base = lane + k * chunk
        return tuple(
            c + mm(jnp.where(base == s, 1.0, 0.0).astype(BF16), block) for c, s in zip(carry, slot_c)
        )

    zero = jnp.zeros((tokens, width), F32)
    picked = lax.fori_loop(0, chunks, gather, (zero, zero))
    halting, s = cols_ref[:, 0:1], cols_ref[:, 1:2]
    x = x_ref[0].astype(F32)
    end = mid_ref[...] + (cols_ref[:, 4:5] * picked[0] + cols_ref[:, 5:6] * picked[1])
    result_ref[0] = (x + halting * (end - x)).astype(BF16)
    sub8 = lax.broadcasted_iota(jnp.int32, (8, width), 0)
    ssum = jnp.broadcast_to(jnp.sum(s, axis=0, keepdims=True), (1, width))
    hsum_ref[...] = jnp.where(sub8 == 0, fold_rows(s * end), jnp.where(sub8 == 1, ssum, 0.0))


def result_step(micro, tokens, mid, ret, cols, slotcol, old):
    _, count, width = tokens.shape
    whole = lambda a: pl.BlockSpec(a.shape, lambda i: (0,) * a.ndim)
    part = pl.BlockSpec((1, count, width), lambda i: (micro, 0, 0))
    return pl.pallas_call(
        functools.partial(result_kernel, bool(old)),
        grid=(1,),
        out_shape=(jax.ShapeDtypeStruct(tokens.shape, BF16), jax.ShapeDtypeStruct((8, width), F32)),
        in_specs=[part] + [whole(a) for a in (mid, ret, cols, slotcol)] + [pl.BlockSpec(memory_space=pl.ANY)] * len(old),
        out_specs=[part, pl.BlockSpec((8, width), lambda i: (0, 0))],
        input_output_aliases={5: 0} if old else {},
        compiler_params=pltpu.CompilerParams(vmem_limit_bytes=VMEM_LIMIT),
        cost_estimate=pl.CostEstimate(
            flops=4 * count * ret.shape[0] * width, bytes_accessed=5 << 20, transcendentals=count
        ),
        name="result_step",
    )(tokens, mid, ret, cols, slotcol, *old)


def attention_backward_kernel(last, n_old, *refs):
    (x_ref, grad_ref, col_ref, vec_ref, qw_ref, kvr_ref, proj_ref, frw_ref,
     mid_ref, n2_ref, normed_ref, mixed_ref, probs_ref, qs_ref, kv_ref, gates_ref, slotcol_ref,
     back_ref, cols_ref) = refs[:19]
    old = refs[19 : 19 + n_old]
    gtok_ref, gq_out, gproj_out, gkvr_out, gfr_out, gvec_out = refs[19 + n_old : 25 + n_old]
    gsum, gq_ref, gproj_ref, gkvr_ref, gfr_ref, gvec_ref = refs[25 + n_old :]
    step = pl.program_id(0)
    rows, width = mid_ref.shape
    lane = lane_iota(rows)
    low = lane < LANES // 2
    col = col_ref[0]
    chunk = 256
    slot_c = [slotcol_ref[:, i : i + 1] for i in range(2)]
    lane_c = lane_iota(rows, chunk)
    accs = (gq_ref, gproj_ref, gkvr_ref, gfr_ref, gvec_ref)

    @pl.when(step == 0)
    def _():
        for k, ref in enumerate(accs):
            ref[...] = old[k][...] if old else jnp.zeros_like(ref)

    gsum[...] = jnp.zeros_like(gsum)

    def gather(k, carry):
        block = back_ref[pl.ds(pl.multiple_of(k * chunk, chunk), chunk), :]
        base = lane_c + k * chunk
        pick = jnp.where((base == slot_c[0]) | (base == slot_c[1]), 1.0, 0.0).astype(BF16)
        gsum[...] += mm(pick, block)
        return carry

    lax.fori_loop(0, back_ref.shape[0] // chunk, gather, 0)
    glog = jnp.zeros((rows, LANES), F32)
    for i in range(2):
        glog = jnp.where(lane == col[:, 4 + i : 5 + i], cols_ref[:, 2 + i : 3 + i], glog)
    glog = glog.astype(BF16)
    n2 = n2_ref[...]
    gfr_ref[...] += mm_tn(n2, glog)
    gn2 = gsum[...] + mm_nt(glog, frw_ref[...])
    hat2, rstd2 = norm_parts(mid_ref[...])
    grad = grad_ref[0].astype(F32)
    halting = cols_ref[:, 0:1]
    gend = halting * grad + cols_ref[:, 1:2] * vec_ref[4:5, :]
    gmid = gend + norm_back(hat2, rstd2, vec_ref[2:3, :], gn2)
    ggain2 = fold_rows(gn2 * hat2)
    gbias2 = fold_rows(gn2)
    gattn = gmid.astype(BF16)
    gproj_ref[...] += mm_tn(mixed_ref[...], gattn)
    gmixed = mm_nt(gattn, proj_ref[...]).astype(BF16).astype(F32)
    pairs = gmixed.shape[1] // LANES
    tiles = [gmixed[:, j * LANES : (j + 1) * LANES] for j in range(pairs)]
    kv = kv_ref[...]
    scale = 0.125
    routes = [col[:, i : i + 1] for i in range(4)]
    gkv = jnp.zeros((rows, LANES), F32)
    ggates = []
    parts = []
    for i in range(4):
        gate = gates_ref[:, i : i + 1]
        sel = pltpu.roll(pick_head(tiles, routes[i], lane), LANES // 2, 1)
        sel = jnp.where(low, 0.0, sel)
        probs = probs_ref[0, i]
        heads = mm(probs, kv)
        ggates.append(jnp.sum(heads * sel, axis=-1, keepdims=True))
        gheads = (gate * sel).astype(BF16)
        gprobs = mm_nt(gheads, kv)
        probs_f = probs.astype(F32)
        inner = jnp.sum(probs_f * gprobs, axis=-1, keepdims=True)
        gscores = (probs_f * (gprobs - inner)).astype(BF16)
        gkv = gkv + mm_tn(probs, gheads) + mm_tn(gscores, qs_ref[0, i]) * scale
        gq = mm(gscores, kv) * scale
        parts.append(jnp.where(low, gq, pltpu.roll(gq, LANES // 2, 1)))
    gtiles = place_heads(parts, routes, pairs, lane)
    gquery = jnp.concatenate([t.astype(BF16) for t in gtiles], axis=1)
    normed = normed_ref[...]
    gq_ref[...] += mm_tn(normed, gquery)
    mean = ggates[0] * gates_ref[:, 0:1]
    for i in range(1, 4):
        mean = mean + ggates[i] * gates_ref[:, i : i + 1]
    alog = jnp.zeros((rows, LANES), F32)
    for i in range(4):
        alog = jnp.where(lane == routes[i], gates_ref[:, i : i + 1] * (ggates[i] - mean), alog)
    gkvr = jnp.concatenate([gkv.astype(BF16), alog.astype(BF16)], axis=1)
    gkvr_ref[...] += mm_tn(normed, gkvr)
    gnormed = mm_nt(gquery, qw_ref[...]) + mm_nt(gkvr, kvr_ref[...])
    hat, rstd = norm_parts(x_ref[0].astype(F32))
    gtok_ref[0] = grad * (1.0 - halting) + gmid + norm_back(hat, rstd, vec_ref[0:1, :], gnormed)
    sub8 = lax.broadcasted_iota(jnp.int32, (8, width), 0)
    gvec = jnp.where(sub8 == 0, fold_rows(gnormed * hat), 0.0)
    gvec = jnp.where(sub8 == 1, fold_rows(gnormed), gvec)
    gvec = jnp.where(sub8 == 2, ggain2, gvec)
    gvec_ref[...] += jnp.where(sub8 == 3, gbias2, gvec)

    @pl.when(step == pl.num_programs(0) - 1)
    def _():
        for ref, out in zip(accs, (gq_out, gproj_out, gkvr_out, gfr_out, gvec_out)):
            out[...] = ref[...].astype(out.dtype)


def attention_backward(micro, last, tokens, grad, col, vec, qw, kvr, proj, frw, saved, back, cols, old):
    mid, n2, normed, mixed, probs, qs, kv, gates, slotcol = saved
    _, count, width = tokens.shape
    steps = count // SEQ
    inner = qw.shape[1]
    whole = lambda a: pl.BlockSpec(a.shape, lambda r: (0,) * a.ndim)
    by_row = lambda c: pl.BlockSpec((SEQ, c), lambda r: (r, 0))
    part = pl.BlockSpec((1, SEQ, width), lambda r: (micro, r, 0))
    kind = BF16 if last else F32
    out_shape = (
        jax.ShapeDtypeStruct(tokens.shape, F32),
        jax.ShapeDtypeStruct(qw.shape, kind),
        jax.ShapeDtypeStruct(proj.shape, kind),
        jax.ShapeDtypeStruct(kvr.shape, kind),
        jax.ShapeDtypeStruct(frw.shape, kind),
        jax.ShapeDtypeStruct((8, width), F32),
    )
    old_in = [old[k] for k in (1, 2, 3, 4, 5)] if old else []
    return pl.pallas_call(
        functools.partial(attention_backward_kernel, last, len(old_in) + (1 if old else 0)),
        grid=(steps,),
        out_shape=out_shape,
        in_specs=[
            part, part,
            pl.BlockSpec((1, SEQ, 8), lambda r: (micro, r, 0)),
            whole(vec), whole(qw), whole(kvr), whole(proj), whole(frw),
            by_row(width), by_row(width), by_row(width), by_row(inner),
            pl.BlockSpec((1, 4, SEQ, SEQ), lambda r: (r, 0, 0, 0)),
            pl.BlockSpec((1, 4, SEQ, LANES), lambda r: (r, 0, 0, 0)),
            by_row(LANES), by_row(8), by_row(8),
            whole(back), by_row(8),
        ] + [whole(o) for o in old_in] + [pl.BlockSpec(memory_space=pl.ANY)] * (1 if old else 0),
        out_specs=[part] + [pl.BlockSpec(o.shape, lambda r: (0, 0)) for o in out_shape[1:]],
        scratch_shapes=[
            pltpu.VMEM((SEQ, width), F32),
            pltpu.VMEM(qw.shape, F32),
            pltpu.VMEM(proj.shape, F32),
            pltpu.VMEM(kvr.shape, F32),
            pltpu.VMEM(frw.shape, F32),
            pltpu.VMEM((8, width), F32),
        ],
        input_output_aliases={24: 0} if old else {},
        compiler_params=pltpu.CompilerParams(vmem_limit_bytes=VMEM_LIMIT),
        cost_estimate=pl.CostEstimate(
            flops=2 * count * width * (4 * inner + 512 + back.shape[0]), bytes_accessed=24 << 20, transcendentals=0
        ),
        name="attention_backward",
    )(tokens, grad, col, vec, qw, kvr, proj, frw, mid, n2, normed, mixed, probs, qs, kv, gates, slotcol, back, cols,
      *old_in, *(old[:1] if old else []))


def sum_kernel(sizes, value_ref, out_ref, got, got2, part, send_sem, recv_sem, send_sem2, recv_sem2):
    n_expert, n_hidden = sizes
    e = lax.axis_index("expert")
    h = lax.axis_index("hidden")
    barrier = pltpu.get_barrier_semaphore()
    for k in range(1, n_expert):
        pl.semaphore_signal(barrier, inc=1, device_id=(lax.rem(e + k, n_expert), h), device_id_type=pl.DeviceIdType.MESH)
    for k in range(1, n_hidden):
        pl.semaphore_signal(barrier, inc=1, device_id=(e, lax.rem(h + k, n_hidden)), device_id_type=pl.DeviceIdType.MESH)
    pl.semaphore_wait(barrier, n_expert + n_hidden - 2)
    moves = []
    for k in range(1, n_expert):
        moves.append(
            pltpu.make_async_remote_copy(
                value_ref, got.at[e], send_sem.at[k - 1], recv_sem.at[k - 1],
                device_id=(lax.rem(e + k, n_expert), h), device_id_type=pl.DeviceIdType.MESH,
            )
        )
    for c in moves:
        c.start()
    got[e] = value_ref[...]
    for c in moves:
        c.wait()
    part[...] = jnp.sum(got[...], axis=0)
    moves = []
    for k in range(1, n_hidden):
        moves.append(
            pltpu.make_async_remote_copy(
                part, got2.at[h], send_sem2.at[k - 1], recv_sem2.at[k - 1],
                device_id=(e, lax.rem(h + k, n_hidden)), device_id_type=pl.DeviceIdType.MESH,
            )
        )
    for c in moves:
        c.start()
    got2[h] = part[...]
    for c in moves:
        c.wait()
    out_ref[...] = jnp.sum(got2[...], axis=0)


def sum_everywhere(sizes, value):
    vmem = pl.BlockSpec(memory_space=pltpu.VMEM)
    return pl.pallas_call(
        functools.partial(sum_kernel, sizes),
        out_shape=jax.ShapeDtypeStruct(value.shape, F32),
        in_specs=[vmem],
        out_specs=vmem,
        scratch_shapes=[
            pltpu.VMEM((sizes[0],) + value.shape, F32),
            pltpu.VMEM((sizes[1],) + value.shape, F32),
            pltpu.VMEM(value.shape, F32),
        ]
        + [pltpu.SemaphoreType.DMA((sizes[0] - 1,))] * 2
        + [pltpu.SemaphoreType.DMA((sizes[1] - 1,))] * 2,
        compiler_params=pltpu.CompilerParams(collective_id=1, has_side_effects=True),
        name="sum_everywhere",
    )(value)


def pad_lanes(a):
    return jnp.pad(a, ((0, 0), (0, LANES - a.shape[1])))


def per_device(
    tokens, grad_out, attn_routes, ffn_routes, segments, pad_mask, norm1_gain, norm1_bias, attn_router,
    query_w, key_w, value_w, attn_proj, norm2_gain, norm2_bias, ffn_router, expert_in, expert_out, halt_w, halt_b,
    *, n_expert, n_hidden,
):
    micros, count, width = tokens.shape
    experts = ffn_router.shape[1]
    capacity = 4 * count // experts
    slots = experts * capacity
    local = experts // n_expert
    first = lax.all_gather(expert_in, "hidden", axis=0, tiled=False)
    second = lax.all_gather(expert_out, "hidden", axis=0, tiled=False)
    seg = segments.reshape(micros, count)
    zeros = jnp.zeros_like(seg)
    col = jnp.concatenate([attn_routes, ffn_routes, seg[:, :, None], pad_mask[:, :, None]], axis=2)
    row = jnp.stack([seg, pad_mask, ffn_routes[:, :, 0], ffn_routes[:, :, 1], zeros, zeros, zeros, zeros], axis=1)
    none = jnp.zeros_like(halt_w)
    vec = jnp.stack([norm1_gain, norm1_bias, norm2_gain, norm2_bias, halt_w, none, none, none])
    kvr = jnp.concatenate([key_w, value_w, pad_lanes(attn_router)], axis=1)
    frw = pad_lanes(ffn_router)
    hb = jnp.broadcast_to(halt_b.reshape(1, 1), (8, LANES))

    def exchange(a):
        return lax.all_to_all(a, "expert", split_axis=0, concat_axis=0, tiled=True)

    def slotted(a):
        return exchange(a.reshape(n_expert, local * capacity, width)).reshape(n_expert, local, capacity, width)

    def returned(a):
        return exchange(a.reshape(n_expert, local * capacity, width)).reshape(slots, width)

    plan = [route_step(m, row, col, grad_out, slots, capacity) for m in range(micros)]
    far_grad = [slotted(p[2]) for p in plan]
    fwd = [
        attention_forward(m, tokens, grad_out, col, row, plan[m][0], vec, hb, query_w, kvr, attn_proj, frw, slots)
        for m in range(micros)
    ]
    arrived = [slotted(f[9]) for f in fwd]
    results = []
    cols = []
    abs_ = []
    for m in range(micros):
        y, scal = expert_forward(arrived[m], far_grad[m], vec, first, second)
        results.append(y)
        c, ab = scalar_step(n_expert, scal, fwd[m][8], plan[m][0])
        cols.append(c)
        abs_.append(ab)
    gback = []
    old = ()
    for m in range(micros):
        gf, gs, rows = expert_backward(arrived[m], far_grad[m], abs_[m], vec, first, second, old)
        gback.append(returned(rows))
        old = (gf, gs)
    gfirst = lax.psum_scatter(old[0], "hidden", scatter_dimension=0, tiled=False).astype(F32)
    gsecond = lax.psum_scatter(old[1], "hidden", scatter_dimension=0, tiled=False).astype(F32)
    out = ()
    for m in range(micros):
        f = fwd[m]
        saved = f[:8] + (plan[m][1],)
        out = attention_backward(
            m, m == micros - 1, tokens, grad_out, col, vec, query_w, kvr, attn_proj, frw, saved, gback[m], cols[m], out
        )
    res = ()
    hsum = None
    for m in range(micros):
        res = result_step(m, tokens, fwd[m][0], returned(results[m]), cols[m], plan[m][1], res[:1])
        hsum = res[1] if hsum is None else hsum + res[1]
    gq, gproj, gkvr, gfr = [a.astype(F32) for a in lax.psum(tuple(out[1:5]), ("expert", "hidden"))]
    small = sum_everywhere((n_expert, n_hidden), jnp.concatenate([out[5], hsum], axis=0))
    head = key_w.shape[1]
    return (
        res[0],
        out[0],
        small[0],
        small[1],
        gkvr[:, LANES : LANES + attn_router.shape[1]],
        gq,
        gkvr[:, :head],
        gkvr[:, head : 2 * head],
        gproj,
        small[2],
        small[3],
        gfr[:, :experts],
        gfirst,
        gsecond,
        small[8],
        small[9, :1],
    )


def solution(mesh):
    rows = P(None, ("expert", "hidden"), None)
    in_specs = (rows,) * 5 + (P(None, ("expert", "hidden")),) + (P(),) * 10 + (
        P("expert", None, "hidden"), P("expert", "hidden", None), P(), P(),
    )
    out_specs = (rows,) * 2 + (P(),) * 10 + (P("expert", None, "hidden"), P("expert", "hidden", None), P(), P())
    return jax.shard_map(
        functools.partial(per_device, n_expert=mesh.shape["expert"], n_hidden=mesh.shape["hidden"]),
        mesh=mesh, in_specs=in_specs, out_specs=out_specs, check_vma=False,
    )
```

time: 944 us -> 785 us (0.83)
  Pallas kernels: 0 us -> 344 us
  matrix products: 212 us -> 0 us
  local copies, waits for them, and re-layouts: 224 us -> 22.6 us
  other arithmetic: 133 us -> 14.7 us
  waiting for transfers between devices: 270 us -> 343 us
  blocking collectives: 40.2 us -> 0 us
    pallas_call x0 -> x15, Pallas kernels: none -> 344 us  [the longest x2 84.1 us: scalar_step(): pl.pallas_call(functools.partial(scalar_kernel, n_expert), out_shape=(jax...]
    dot_general x64 -> x0, matrix products: 212 us -> none  [the longest x2 40.4 us: expert_backward(): jnp.einsum('erd,efd->erf', grad_rows_in, second, preferred_element_type=j...]
    reduce_scatter x2, waiting for transfers between devices: 0.01 us -> 79.5 us  [the longest x1 44.1 us: per_device(): lax.psum_scatter(old[0], 'hidden', scatter_dimension=0, tiled=False)]
    reduce_sum x43 -> x0, other arithmetic: 70.1 us -> none  [the longest x2 17.9 us: per_device(): jnp.sum(pick_attn * logits_attn[:, None, :], axis=-1)]
    psum x1, waiting for transfers between devices: 92.1 us -> 47.7 us  [per_device(): lax.psum(tuple(out[1:5]), ('expert', 'hidden'))]
    psum x1 -> x0, blocking collectives: 40.2 us -> none  [per_device(): lax.psum((grad_gain_one, grad_bias_one, grad_router_attn, grad_query_w, g...]
    convert_element_type x14 -> x0, local copies, waits for them, and re-layouts: 38.8 us -> none  [the longest x2 6.95 us: per_device(): outgoing_back = expert_res.astype(bf16)]
    all_to_all x8, waiting for transfers between devices: 177 us -> 213 us  [exchange(): return lax.all_to_all(a, 'expert', split_axis=0, concat_axis=0, tiled=True)]
  transfers between devices with their start and end apart: 13 -> 13, of which waited for: 9 -> 9; matrix products, arithmetic and copies ran while one was open for 53% -> 3% of each run, Pallas kernels for 0% -> 40%
where the time goes in v1:
time: 785 us; the launch traced here: 777 us
  Pallas kernels  344 us (44%)
  waiting for transfers between devices  343 us (44%)
  starting transfers between devices  36.9 us (5%)
  local copies, waits for them, and re-layouts  22.6 us (3%)
  between operations  15 us (2%)
  other arithmetic  14.7 us (2%)
    all_to_all x8, waiting for transfers between devices, exchange(): return lax.all_to_all(a, 'expert', split_axis=0, concat_axis=0, tiled=True)  213 us
    pallas_call x2, Pallas kernels, scalar_step(): pl.pallas_call(functools.partial(scalar_kernel, n_expert), out_shape=(jax...  84.1 us
    pallas_call x2, Pallas kernels, expert_backward(): pl.pallas_call(functools.partial(expert_backward_kernel, bool(old)), grid...  71.1 us
    pallas_call x2, Pallas kernels, attention_backward(): pl.pallas_call(functools.partial(attention_backward_kernel, last, len(old...  64.5 us
    psum x1, waiting for transfers between devices, per_device(): lax.psum(tuple(out[1:5]), ('expert', 'hidden'))  47.7 us
    reduce_scatter x1, waiting for transfers between devices, per_device(): lax.psum_scatter(old[0], 'hidden', scatter_dimension=0, tiled=False)  44.1 us
    pallas_call x2, Pallas kernels, attention_forward(): pl.pallas_call(attention_forward_kernel, grid=(steps,), out_shape=out_sha...  42.8 us
    pallas_call x2, Pallas kernels, expert_forward(): pl.pallas_call(expert_forward_kernel, grid=(local, parts), out_shape=(jax...  37.5 us
  transfers between devices with their start and end apart: 13, of which 9 were waited for; matrix products, arithmetic and copies ran while one was open for 3% of the time, Pallas kernels for 40%

profile of v1, /device:TPU:0, one launch (start us, length us, event | category | flops | bytes accessed | tf_op | source)
XLA Modules:
  0.0 776.5 jit_solution(5060814807516066597)
XLA Ops:
  13.7 6.0 route_step.3
  19.7 7.3 all-to-all-start.4
  27.0 6.0 route_step.2
  33.0 42.2 %all-to-all-done.4 = bf16[8,256,512]{2,1,0:T(8,128)(2,1)S(1)} async-done(((bf16[8,256,512]{2,1,0:T(8,128)(2,1)}), bf16[8,256,512]{2,1,0:T(8,128)(2,1)S(1)}, u32[]{:S(2)}, u32[]{:S(2)}) %all-to-all-start.4) | async-done | bytes 2097184 | tf_op jit(solution)/shard_map/all_to_all | solution.py:828
  76.5 3.6 all-to-all-start.1
  84.9 21.4 %attention_forward.3 = (f32[512,512]{1,0:T(8,128)}, bf16[512,512]{1,0:T(8,128)(2,1)}, bf16[512,512]{1,0:T(8,128)(2,1)}, bf16[512,1536]{1,0:T(8,128)(2,1)}, bf16[...) custom-call(bf16[2,512,512]{2,1,0:T(8,128)(2,1)} %refs_0_.7, ...), custom_call_target="tpu_custom_call" | custom-call | flops 2818572288 | bytes 12582912 | tf_op jit(solution)/shard_map/attention_forward/pallas_call | solution.py:267
  106.3 22.3 %all-to-all-done.1 = bf16[8,256,512]{2,1,0:T(8,128)(2,1)S(1)} async-done(((bf16[8,256,512]{2,1,0:T(8,128)(2,1)}), bf16[8,256,512]{2,1,0:T(8,128)(2,1)S(1)}, u32[]{:S(2)}, u32[]{:S(2)}) %all-to-all-start.1) | async-done | bytes 2097184 | tf_op jit(solution)/shard_map/all_to_all | solution.py:828
  129.9 4.9 all-to-all-start.3
  134.8 21.4 %attention_forward.2 = (f32[512,512]{1,0:T(8,128)}, bf16[512,512]{1,0:T(8,128)(2,1)}, bf16[512,512]{1,0:T(8,128)(2,1)}, bf16[512,1536]{1,0:T(8,128)(2,1)}, bf16[...) custom-call(bf16[2,512,512]{2,1,0:T(8,128)(2,1)} %refs_0_.7, ...), custom_call_target="tpu_custom_call" | custom-call | flops 2818572288 | bytes 12582912 | tf_op jit(solution)/shard_map/attention_forward/pallas_call | solution.py:267
  156.3 26.4 %all-to-all-done.3 = bf16[8,256,512]{2,1,0:T(8,128)(2,1)} async-done(((bf16[8,256,512]{2,1,0:T(8,128)(2,1)}), bf16[8,256,512]{2,1,0:T(8,128)(2,1)}, u32[]{:S(2)}, u32[]{:S(2)}) %all-to-all-start.3) | async-done | bytes 2097184 | tf_op jit(solution)/shard_map/all_to_all | solution.py:828
  182.6 3.8 all-to-all-start
  186.5 18.7 %expert_forward.3 = (bf16[8,2,128,512]{3,2,1,0:T(8,128)(2,1)}, f32[8,2,8,128]{3,2,1,0:T(8,128)}) custom-call(bf16[8,2,128,512]{3,2,1,0:T(8,128)(2,1)} %bitcast.18.rows_ref.refs_0_, bf16[8,2,128,512]{3,2,1,0:T(8,128)(2,1)} %bitcast.45, f32[8,512]{1,0:T(8,128)} %stack.39.vec_ref.refs_3_, bf16[4,2,512,512]{3,2,1,0:T(8,128)(2,1)} %bitcast.68, ...), custom_call_target="tpu_custom_call" | custom-call | flops 8589934592 | bytes 14680064 | tf_op jit(solution)/shard_map/expert_forward/pallas_call | solution.py:338
  205.2 42.9 %scalar_step.3 = (f32[512,8]{1,0:T(8,128)}, f32[8,2,8,128]{3,2,1,0:T(8,128)}) custom-call(f32[8,2,8,128]{3,2,1,0:T(8,128)} %get-tuple-element.86.scal_ref, f32[8,512]{1,0:T(8,128)} %get-tuple-element.87.rowsc_ref, s32[8,512]{1,0:T(8,128)} %get-tuple-element.81.slotrow_ref), custom_call_target="tpu_custom_call" | custom-call | flops 1000000000 | bytes 1048576 | tf_op jit(solution)/shard_map/scalar_step/pallas_call | solution.py:534
  248.2 35.3 %expert_backward.2 = (bf16[4,2,512,512]{3,2,1,0:T(8,128)(2,1)}, bf16[4,2,512,512]{3,2,1,0:T(8,128)(2,1)}, bf16[8,2,128,512]{3,2,1,0:T(8,128)(2,1)}) custom-call(bf16[8,2,128,512]{3,2,1,0:T(8,128)(2,1)} %bitcast.18.rows_ref.refs_0_, bf16[8,2,128,512]{3,2,1,0:T(8,128)(2,1)} %bitcast.46, f32[8,2,8,128]{3,2,1,0:T(8,128)} %get-tuple-element.100.refs_2_, ...), custom_call_target="tpu_custom_call" | custom-call | flops 21474836480 | bytes 23068672 | tf_op jit(solution)/shard_map/expert_backward/pallas_call | solution.py:420
  284.9 4.1 all-to-all-start.7
  289.0 18.8 %expert_forward.2 = (bf16[8,2,128,512]{3,2,1,0:T(8,128)(2,1)}, f32[8,2,8,128]{3,2,1,0:T(8,128)}) custom-call(bf16[8,2,128,512]{3,2,1,0:T(8,128)(2,1)} %bitcast.48, bf16[8,2,128,512]{3,2,1,0:T(8,128)(2,1)} %bitcast.43, f32[8,512]{1,0:T(8,128)} %stack.39.vec_ref.refs_3_, bf16[4,2,512,512]{3,2,1,0:T(8,128)(2,1)} %bitcast.70, bf16[4,2,512,512]{3,2,1,0:T(8,128)(2,1)} %bitcast.74), custom_call_target="tpu_custom_call" | custom-call | flops 8589934592 | bytes 14680064 | tf_op jit(solution)/shard_map/expert_forward/pallas_call | solution.py:338
  307.8 41.2 %scalar_step.2 = (f32[512,8]{1,0:T(8,128)}, f32[8,2,8,128]{3,2,1,0:T(8,128)}) custom-call(f32[8,2,8,128]{3,2,1,0:T(8,128)} %get-tuple-element.77.scal_ref, f32[8,512]{1,0:T(8,128)} %get-tuple-element.78.rowsc_ref, s32[8,512]{1,0:T(8,128)} %get-tuple-element.72.slotrow_ref), custom_call_target="tpu_custom_call" | custom-call | flops 1000000000 | bytes 1048576 | tf_op jit(solution)/shard_map/scalar_step/pallas_call | solution.py:534
  348.9 35.8 %expert_backward.3 = (bf16[4,2,512,512]{3,2,1,0:T(8,128)(2,1)}, bf16[4,2,512,512]{3,2,1,0:T(8,128)(2,1)}, bf16[8,2,128,512]{3,2,1,0:T(8,128)(2,1)}) custom-call(bf16[8,2,128,512]{3,2,1,0:T(8,128)(2,1)} %bitcast.49, bf16[8,2,128,512]{3,2,1,0:T(8,128)(2,1)} %bitcast.44, f32[8,2,8,128]{3,2,1,0:T(8,128)} %get-tuple-element.99.refs_2_, ...), custom_call_target="tpu_custom_call" | custom-call | flops 21474836480 | bytes 23068672 | tf_op jit(solution)/shard_map/expert_backward/pallas_call | solution.py:420
  386.0 4.6 all-to-all-start.6
  390.9 31.7 %attention_backward.2 = (f32[2,512,512]{2,1,0:T(8,128)}, f32[512,1536]{1,0:T(8,128)}, f32[1536,512]{1,0:T(8,128)}, f32[512,256]{1,0:T(8,128)}, f32[512,128]{1,0:T(8,128)}, /*index=5*/f32[8,512]{1,0:T(8,128)}) custom-call(bf16[2,512,512]{2,1,0:T(8,128)(2,1)} %refs_0_.7, bf16[2,512,512]{2,1,0:T(8,128)(2,1)} %refs_1_.3, ...), custom_call_target="tpu_custom_call" | custom-call | flops 4563402752 | bytes 25165824 | tf_op jit(solution)/shard_map/attention_backward/pallas_call | solution.py:709
  422.6 14.7 %all-to-all-done.6 = bf16[8,256,512]{2,1,0:T(8,128)(2,1)S(1)} async-done(((bf16[8,256,512]{2,1,0:T(8,128)(2,1)}), bf16[8,256,512]{2,1,0:T(8,128)(2,1)S(1)}, u32[]{:S(2)}, u32[]{:S(2)}) %all-to-all-start.6) | async-done | bytes 2097184 | tf_op jit(solution)/shard_map/all_to_all | solution.py:828
  438.6 32.8 %attention_backward.3 = (f32[2,512,512]{2,1,0:T(8,128)}, bf16[512,1536]{1,0:T(8,128)(2,1)}, bf16[1536,512]{1,0:T(8,128)(2,1)}, bf16[512,256]{1,0:T(8,128)(2,1)},...) custom-call(bf16[2,512,512]{2,1,0:T(8,128)(2,1)} %refs_0_.7, ...), custom_call_target="tpu_custom_call", output_to_operand_aliasing={{0}: (24, {})} | custom-call | flops 4563402752 | bytes 25165824 | tf_op jit(solution)/shard_map/attention_backward/pallas_call | solution.py:709
  472.0 3.6 all-to-all-start.5
  476.2 64.4 %all-to-all-done.5 = bf16[8,256,512]{2,1,0:T(8,128)(2,1)S(1)} async-done(((bf16[8,256,512]{2,1,0:T(8,128)(2,1)}), bf16[8,256,512]{2,1,0:T(8,128)(2,1)S(1)}, u32[]{:S(2)}, u32[]{:S(2)}) %all-to-all-start.5) | async-done | bytes 2097184 | tf_op jit(solution)/shard_map/all_to_all | solution.py:828
  542.0 4.5 all-to-all-start.2
  546.5 9.5 %result_step.2 = (bf16[2,512,512]{2,1,0:T(8,128)(2,1)}, f32[8,512]{1,0:T(8,128)}) custom-call(bf16[2,512,512]{2,1,0:T(8,128)(2,1)} %refs_0_.7, f32[512,512]{1,0:T(8,128)} %get-tuple-element.82.refs_1_.refs_8_, bf16[2048,512]{1,0:T(8,128)(2,1)} %bitcast.55, f32[512,8]{1,0:T(8,128)} %get-tuple-element.88.refs_3_.refs_18_, ...), custom_call_target="tpu_custom_call" | custom-call | flops 2147483648 | bytes 5242880 | tf_op jit(solution)/shard_map/result_step/pallas_call | solution.py:577
  556.0 43.4 %all-to-all-done.2 = bf16[8,256,512]{2,1,0:T(8,128)(2,1)} async-done(((bf16[8,256,512]{2,1,0:T(8,128)(2,1)}), bf16[8,256,512]{2,1,0:T(8,128)(2,1)}, u32[]{:S(2)}, u32[]{:S(2)}) %all-to-all-start.2) | async-done | bytes 2097184 | tf_op jit(solution)/shard_map/all_to_all | solution.py:828
  599.5 9.5 %result_step.3 = (bf16[2,512,512]{2,1,0:T(8,128)(2,1)}, f32[8,512]{1,0:T(8,128)}) custom-call(bf16[2,512,512]{2,1,0:T(8,128)(2,1)} %refs_0_.7, f32[512,512]{1,0:T(8,128)} %get-tuple-element.73.refs_1_.refs_8_, bf16[2048,512]{1,0:T(8,128)(2,1)} %bitcast.16.refs_2_, f32[512,8]{1,0:T(8,128)} %get-tuple-element.79.refs_3_.refs_18_, ...), custom_call_target="tpu_custom_call", output_to_operand_aliasing={{0}: (5, {})} | custom-call | flops 2147483648 | bytes 5242880 | tf_op jit(solution)/shard_map/result_step/pallas_call | solution.py:577
  610.4 13.0 %sum_everywhere.1 = f32[16,512]{1,0:T(8,128)} custom-call(f32[16,512]{1,0:T(8,128)} %pad_maximum_fusion.value_ref), custom_call_target="tpu_custom_call" | custom-call | tf_op jit(solution)/shard_map/sum_everywhere/pallas_call | solution.py:784
  626.1 47.7 %all-reduce.5.cloned.1.call-done = (bf16[512,256]{1,0:T(8,128)(2,1)}, bf16[512,1536]{1,0:T(8,128)(2,1)}, bf16[1536,512]{1,0:T(8,128)(2,1)}, bf16[512,128]{1,0:T(8,128)(2,1)}) async-done(((bf16[512,256]{1,0:T(8,128)(2,1)}, bf16[512,1536]{1,0:T(8,128)(2,1)}, bf16[1536,512]{1,0:T(8,128)(2,1)}, bf16[512,128]{1,0:T(8,128)(2,1)}), (bf16[512,256]{1,0:T(8,128)(2,1)}, bf16[512,1536]{1,0:T(8,128)(2,1)}, ...) | async-done | bytes 3538960 | tf_op jit(solution)/shard_map/psum | solution.py:872
  684.6 35.4 %reduce-scatter.5.cloned.1.call-done = bf16[1,2,512,512]{3,2,1,0:T(8,128)(2,1)} async-done(((bf16[4,2,512,512]{3,2,1,0:T(8,128)(2,1)}), bf16[1,2,512,512]{3,2,1,0:T(8,128)(2,1)}) %reduce-scatter.5.cloned.1.call-update) | async-done | bytes 1048592 | tf_op jit(solution)/shard_map/reduce_scatter | solution.py:859
  722.8 44.1 %reduce-scatter.3.cloned.1.call-done = bf16[1,2,512,512]{3,2,1,0:T(8,128)(2,1)} async-done(((bf16[4,2,512,512]{3,2,1,0:T(8,128)(2,1)}), bf16[1,2,512,512]{3,2,1,0:T(8,128)(2,1)}) %reduce-scatter.3.cloned.1.call-update) | async-done | bytes 1048592 | tf_op jit(solution)/shard_map/reduce_scatter | solution.py:858
  (91 shorter events, 40.2 us)
Async XLA Ops:
  7.2 4.1 copy-start.12
  7.2 4.4 copy-start.10
  7.2 179.3 %all-gather.5.cloned.1.call-start = ((), (), s32[]{:S(2)}) async-start(), calls=%async_computation.12 | async-start | bytes 5242880 | tf_op jit(solution)/shard_map/all_gather | solution.py:815
  19.7 55.5 %all-to-all-start.4 = ((bf16[8,256,512]{2,1,0:T(8,128)(2,1)}), bf16[8,256,512]{2,1,0:T(8,128)(2,1)S(1)}, u32[]{:S(2)}, u32[]{:S(2)}) async-start(bf16[8,256,512]{2,1,0:T(8,128)(2,1)} %bitcast.56), calls=%async_computation.4 | async-start | bytes 4194304 | tf_op jit(solution)/shard_map/all_to_all | solution.py:828
  75.2 1.3 copy-start.2
  75.2 6.4 copy-start.11
  75.2 6.5 copy-start.8
  75.2 6.6 copy-start.9
  75.2 6.7 copy-start.13
  75.2 7.6 copy-start.16
  75.3 7.6 copy-start.17
  75.3 7.5 copy-start.18
  75.3 7.5 copy-start.19
  75.3 7.5 copy-start.20
  76.5 52.1 %all-to-all-start.1 = ((bf16[8,256,512]{2,1,0:T(8,128)(2,1)}), bf16[8,256,512]{2,1,0:T(8,128)(2,1)S(1)}, u32[]{:S(2)}, u32[]{:S(2)}) async-start(bf16[8,256,512]{2,1,0:T(8,128)(2,1)} %bitcast.50), calls=%async_computation.1 | async-start | bytes 4194304 | tf_op jit(solution)/shard_map/all_to_all | solution.py:828
  80.2 106.3 %all-gather.7.cloned.1.call-start = ((), (), s32[]{:S(2)}) async-start(), calls=%async_computation.13 | async-start | bytes 5242880 | tf_op jit(solution)/shard_map/all_gather | solution.py:816
  128.6 1.3 copy-start.1
  129.9 52.7 %all-to-all-start.3 = ((bf16[8,256,512]{2,1,0:T(8,128)(2,1)}), bf16[8,256,512]{2,1,0:T(8,128)(2,1)}, u32[]{:S(2)}, u32[]{:S(2)}) async-start(bf16[8,256,512]{2,1,0:T(8,128)(2,1)} %bitcast.54), calls=%async_computation.3 | async-start | bytes 4194304 | tf_op jit(solution)/shard_map/all_to_all | solution.py:828
  182.6 100.9 %all-to-all-start = ((bf16[8,256,512]{2,1,0:T(8,128)(2,1)}), bf16[8,256,512]{2,1,0:T(8,128)(2,1)S(1)}, u32[]{:S(2)}, u32[]{:S(2)}) async-start(bf16[8,256,512]{2,1,0:T(8,128)(2,1)} %bitcast.51), calls=%async_computation | async-start | bytes 4194304 | tf_op jit(solution)/shard_map/all_to_all | solution.py:828
  283.5 1.3 copy-start.4
  284.9 99.9 %all-to-all-start.7 = ((bf16[8,256,512]{2,1,0:T(8,128)(2,1)}), bf16[8,256,512]{2,1,0:T(8,128)(2,1)S(1)}, u32[]{:S(2)}, u32[]{:S(2)}) async-start(bf16[8,256,512]{2,1,0:T(8,128)(2,1)} %bitcast.53), calls=%async_computation.7 | async-start | bytes 4194304 | tf_op jit(solution)/shard_map/all_to_all | solution.py:828
  384.7 1.3 copy-start.3
  386.0 51.3 %all-to-all-start.6 = ((bf16[8,256,512]{2,1,0:T(8,128)(2,1)}), bf16[8,256,512]{2,1,0:T(8,128)(2,1)S(1)}, u32[]{:S(2)}, u32[]{:S(2)}) async-start(bf16[8,256,512]{2,1,0:T(8,128)(2,1)} %bitcast.52), calls=%async_computation.6 | async-start | bytes 4194304 | tf_op jit(solution)/shard_map/all_to_all | solution.py:828
  390.6 283.2 %all-reduce.5.cloned.1.call-start = ((), (), s32[]{:S(2)}) async-start(), calls=%async_computation.14 | async-start | bytes 7077888 | tf_op jit(solution)/shard_map/psum | solution.py:872
  471.5 248.6 %reduce-scatter.5.cloned.1.call-start = ((), (), s32[]{:S(2)}) async-start(), calls=%async_computation.11 | async-start | bytes 5242880 | tf_op jit(solution)/shard_map/reduce_scatter | solution.py:859
  472.0 68.6 %all-to-all-start.5 = ((bf16[8,256,512]{2,1,0:T(8,128)(2,1)}), bf16[8,256,512]{2,1,0:T(8,128)(2,1)S(1)}, u32[]{:S(2)}, u32[]{:S(2)}) async-start(bf16[8,256,512]{2,1,0:T(8,128)(2,1)} %bitcast.21), calls=%async_computation.5 | async-start | bytes 4194304 | tf_op jit(solution)/shard_map/all_to_all | solution.py:828
  475.7 291.3 %reduce-scatter.3.cloned.1.call-start = ((), (), s32[]{:S(2)}) async-start(), calls=%async_computation.10 | async-start | bytes 5242880 | tf_op jit(solution)/shard_map/reduce_scatter | solution.py:858
  542.0 57.5 %all-to-all-start.2 = ((bf16[8,256,512]{2,1,0:T(8,128)(2,1)}), bf16[8,256,512]{2,1,0:T(8,128)(2,1)}, u32[]{:S(2)}, u32[]{:S(2)}) async-start(bf16[8,256,512]{2,1,0:T(8,128)(2,1)} %bitcast.15), calls=%async_computation.2 | async-start | bytes 4194304 | tf_op jit(solution)/shard_map/all_to_all | solution.py:828
  599.5 9.6 %copy-start.14 = (f32[8,512]{1,0:T(8,128)S(1)}, f32[8,512]{1,0:T(8,128)}, u32[]{:S(2)}) copy-start(f32[8,512]{1,0:T(8,128)} %get-tuple-element.120) | copy-start | bytes 49156
  599.5 10.3 %copy-start.15 = (f32[8,512]{1,0:T(8,128)S(1)}, f32[8,512]{1,0:T(8,128)}, u32[]{:S(2)}) copy-start(f32[8,512]{1,0:T(8,128)} %get-tuple-element.119) | copy-start | bytes 49156
  673.8 6.1 copy-start.7
  679.9 2.2 copy-start.6
  (2 other events, 2.6 us)
Sparse Core Ops, SparseCore 0:
  9.6 37.3 all-gather.4
  82.6 35.9 all-gather.6
  471.6 202.2 all-reduce.4
  676.4 43.5 reduce-scatter.4
  722.4 44.5 reduce-scatter.2

commit v2 on v1

--- a/solution.py
+++ b/solution.py
@@ -361,15 +361,39 @@
     )(rows, grad, vec, first, second)
 
 
-def expert_backward_kernel(add_old, *refs):
-    rows_ref, grad_ref, ab_ref, vec_ref, first_ref, second_ref = refs[:6]
-    refs = refs[6:]
+def exchange_copies(n_expert, source, target, send_sem, recv_sem, own_sem):
+    me = lax.axis_index("expert")
+    other = lax.axis_index("hidden")
+    moves = []
+    for k in range(1, n_expert):
+        peer = lax.rem(me + k, n_expert)
+        moves.append(
+            pltpu.make_async_remote_copy(
+                source.at[peer], target.at[me], send_sem.at[k - 1], recv_sem.at[k - 1],
+                device_id=(peer, other), device_id_type=pl.DeviceIdType.MESH,
+            )
+        )
+    return moves, pltpu.make_async_copy(source.at[me], target.at[me], own_sem)
+
+
+def expert_backward_kernel(n_expert, add_old, *refs):
+    rows_ref, grad_ref, ab_ref, vec_ref, first_ref, second_ref, away_ref = refs[:7]
+    refs = refs[7:]
     if add_old:
         old_first_ref, old_second_ref = refs[:2]
         refs = refs[2:]
-    gfirst_ref, gsecond_ref, out_ref, total, gin_all = refs
+    gfirst_ref, gsecond_ref, out_ref, home_ref, total, gin_all, send_sem, recv_sem, own_sem = refs
     part = pl.program_id(1)
     src, _, cap, width = rows_ref.shape
+    moves, own = exchange_copies(n_expert, away_ref, home_ref, send_sem, recv_sem, own_sem)
+
+    @pl.when((pl.program_id(0) == 0) & (part == 0))
+    def _():
+        other = lax.axis_index("hidden")
+        greet("expert", n_expert, lambda e: (e, other))
+        for c in moves:
+            c.start()
+        own.start()
 
     @pl.when(part == 0)
     def _():
@@ -410,37 +434,52 @@
     def _():
         out_ref[...] = total[...].astype(BF16).reshape(out_ref.shape)
 
-
-def expert_backward(rows, grad, ab, vec, first, second, old):
+    @pl.when((pl.program_id(0) == pl.num_programs(0) - 1) & (part == pl.num_programs(1) - 1))
+    def _():
+        for c in moves:
+            c.wait()
+        own.wait()
+
+
+def expert_backward(n_expert, rows, grad, ab, vec, first, second, away, old):
     src, local, cap, width = rows.shape
     parts, _, _, hid = first.shape
     spec_rows = pl.BlockSpec((src, 1, cap, width), lambda e, h: (0, e, 0, 0))
     spec_first = pl.BlockSpec((1, 1, width, hid), lambda e, h: (h, e, 0, 0))
     spec_second = pl.BlockSpec((1, 1, hid, width), lambda e, h: (h, e, 0, 0))
     return pl.pallas_call(
-        functools.partial(expert_backward_kernel, bool(old)),
+        functools.partial(expert_backward_kernel, n_expert, bool(old)),
         grid=(local, parts),
         out_shape=(
             jax.ShapeDtypeStruct(first.shape, BF16),
             jax.ShapeDtypeStruct(second.shape, BF16),
             jax.ShapeDtypeStruct(rows.shape, BF16),
+            jax.ShapeDtypeStruct(away.shape, BF16),
         ),
         in_specs=[
             spec_rows, spec_rows,
             pl.BlockSpec((src, 1, 8, cap), lambda e, h: (0, e, 0, 0)),
             pl.BlockSpec(vec.shape, lambda e, h: (0, 0)),
-            spec_first, spec_second,
+            spec_first, spec_second, pl.BlockSpec(memory_space=pl.ANY),
         ] + [spec_first, spec_second][: len(old)],
-        out_specs=[spec_first, spec_second, spec_rows],
-        scratch_shapes=[pltpu.VMEM((src * cap, width), F32), pltpu.VMEM((src * cap, width), BF16)],
-        compiler_params=pltpu.CompilerParams(vmem_limit_bytes=VMEM_LIMIT),
+        out_specs=[spec_first, spec_second, spec_rows, pl.BlockSpec(memory_space=pl.ANY)],
+        scratch_shapes=[
+            pltpu.VMEM((src * cap, width), F32),
+            pltpu.VMEM((src * cap, width), BF16),
+            pltpu.SemaphoreType.DMA((n_expert - 1,)),
+            pltpu.SemaphoreType.DMA((n_expert - 1,)),
+            pltpu.SemaphoreType.DMA,
+        ],
+        compiler_params=pltpu.CompilerParams(
+            vmem_limit_bytes=VMEM_LIMIT, collective_id=3 if old else 2, has_side_effects=True
+        ),
         cost_estimate=pl.CostEstimate(
             flops=10 * src * local * cap * width * hid * parts,
             bytes_accessed=6 * src * local * cap * width + 8 * local * parts * width * hid,
             transcendentals=src * local * cap * hid * parts,
         ),
         name="expert_backward",
-    )(rows, grad, ab, vec, first, second, *old)
+    )(rows, grad, ab, vec, first, second, away, *old)
 
 
 def greet(axis, peers, make_id):
@@ -850,9 +889,13 @@
         cols.append(c)
         abs_.append(ab)
     gback = []
+    homes = []
     old = ()
     for m in range(micros):
-        gf, gs, rows = expert_backward(arrived[m], far_grad[m], abs_[m], vec, first, second, old)
+        gf, gs, rows, home = expert_backward(
+            n_expert, arrived[m], far_grad[m], abs_[m], vec, first, second, results[m], old
+        )
+        homes.append(home.reshape(slots, width))
         gback.append(returned(rows))
         old = (gf, gs)
     gfirst = lax.psum_scatter(old[0], "hidden", scatter_dimension=0, tiled=False).astype(F32)
@@ -867,9 +910,10 @@
     res = ()
     hsum = None
     for m in range(micros):
-        res = result_step(m, tokens, fwd[m][0], returned(results[m]), cols[m], plan[m][1], res[:1])
+        res = result_step(m, tokens, fwd[m][0], homes[m], cols[m], plan[m][1], res[:1])
         hsum = res[1] if hsum is None else hsum + res[1]
-    gq, gproj, gkvr, gfr = [a.astype(F32) for a in lax.psum(tuple(out[1:5]), ("expert", "hidden"))]
+    shared, _ = lax.optimization_barrier((tuple(out[1:5]), (gfirst, gsecond)))
+    gq, gproj, gkvr, gfr = [a.astype(F32) for a in lax.psum(shared, ("expert", "hidden"))]
     small = sum_everywhere((n_expert, n_hidden), jnp.concatenate([out[5], hsum], axis=0))
     head = key_w.shape[1]
     return (

time: 785 us -> 700 us (0.89)
  waiting for transfers between devices: 343 us -> 213 us
  blocking collectives: 0 us -> 62.6 us
  starting transfers between devices: 36.9 us -> 24.1 us
    all_to_all x8 -> x5, waiting for transfers between devices: 213 us -> 105 us  [exchange(): return lax.all_to_all(a, 'expert', split_axis=0, concat_axis=0, tiled=True)]
    all_to_all x0 -> x1, blocking collectives: none -> 62.6 us  [exchange(): return lax.all_to_all(a, 'expert', split_axis=0, concat_axis=0, tiled=True)]
    psum x1, waiting for transfers between devices: 47.7 us -> 106 us  [per_device(): lax.psum(shared, ('expert', 'hidden'))]
    reduce_scatter x1, waiting for transfers between devices: 44.1 us -> 0.01 us  [per_device(): lax.psum_scatter(old[0], 'hidden', scatter_dimension=0, tiled=False)]
    reduce_scatter x1, waiting for transfers between devices: 35.4 us -> 0.02 us  [per_device(): lax.psum_scatter(old[1], 'hidden', scatter_dimension=0, tiled=False)]
    pallas_call x2, Pallas kernels: 84.1 us -> 60.9 us  [scalar_step(): pl.pallas_call(functools.partial(scalar_kernel, n_expert), out_shape=(jax...]
    pallas_call x2, Pallas kernels: 71.1 us -> 88.4 us  [expert_backward(): pl.pallas_call(functools.partial(expert_backward_kernel, n_expert, bool(o...]
    all_to_all x8 -> x5, starting transfers between devices: 36.4 us -> 23.3 us  [exchange(): return lax.all_to_all(a, 'expert', split_axis=0, concat_axis=0, tiled=True)]
  transfers between devices with their start and end apart: 13 -> 10, of which waited for: 9 -> 5; matrix products, arithmetic and copies ran while one was open for 3% -> 1% of each run, Pallas kernels for 40% -> 30%
where the time goes in v2:
time: 700 us; the launch traced here: 691 us
  Pallas kernels  340 us (49%)
  waiting for transfers between devices  213 us (30%)
  blocking collectives  62.6 us (9%)
  starting transfers between devices  24.1 us (3%)
  local copies, waits for them, and re-layouts  21.8 us (3%)
  between operations  15.1 us (2%)
  other arithmetic  14.2 us (2%)
    psum x1, waiting for transfers between devices, per_device(): lax.psum(shared, ('expert', 'hidden'))  106 us
    all_to_all x5, waiting for transfers between devices, exchange(): return lax.all_to_all(a, 'expert', split_axis=0, concat_axis=0, tiled=True)  105 us
    pallas_call x2, Pallas kernels, expert_backward(): pl.pallas_call(functools.partial(expert_backward_kernel, n_expert, bool(o...  88.4 us
    pallas_call x2, Pallas kernels, attention_backward(): pl.pallas_call(functools.partial(attention_backward_kernel, last, len(old...  64.6 us
    all_to_all x1, blocking collectives, exchange(): return lax.all_to_all(a, 'expert', split_axis=0, concat_axis=0, tiled=True)  62.6 us
    pallas_call x2, Pallas kernels, scalar_step(): pl.pallas_call(functools.partial(scalar_kernel, n_expert), out_shape=(jax...  60.9 us
    pallas_call x2, Pallas kernels, attention_forward(): pl.pallas_call(attention_forward_kernel, grid=(steps,), out_shape=out_sha...  42.8 us
    pallas_call x2, Pallas kernels, expert_forward(): pl.pallas_call(expert_forward_kernel, grid=(local, parts), out_shape=(jax...  37.4 us
  transfers between devices with their start and end apart: 10, of which 5 were waited for; matrix products, arithmetic and copies ran while one was open for 1% of the time, Pallas kernels for 30%

profile of v2, /device:TPU:0, one launch (start us, length us, event | category | flops | bytes accessed | tf_op | source)
XLA Modules:
  0.0 690.9 jit_solution(16318826790505080132)
XLA Ops:
  15.1 6.0 route_step.3
  21.1 7.3 %all-to-all-start.3 = ((bf16[8,256,512]{2,1,0:T(8,128)(2,1)}), bf16[8,256,512]{2,1,0:T(8,128)(2,1)S(1)}, u32[]{:S(2)}, u32[]{:S(2)}) async-start(bf16[8,256,512]{2,1,0:T(8,128)(2,1)} %bitcast.51), calls=%async_computation.3 | async-start | bytes 4194304 | tf_op jit(solution)/shard_map/all_to_all | solution.py:867
  29.1 6.0 route_step.2
  35.1 41.5 %all-to-all-done.3 = bf16[8,256,512]{2,1,0:T(8,128)(2,1)S(1)} async-done(((bf16[8,256,512]{2,1,0:T(8,128)(2,1)}), bf16[8,256,512]{2,1,0:T(8,128)(2,1)S(1)}, u32[]{:S(2)}, u32[]{:S(2)}) %all-to-all-start.3) | async-done | bytes 2097184 | tf_op jit(solution)/shard_map/all_to_all | solution.py:867
  77.9 4.4 all-to-all-start.1
  86.3 21.4 %attention_forward.2 = (f32[512,512]{1,0:T(8,128)}, bf16[512,512]{1,0:T(8,128)(2,1)}, bf16[512,512]{1,0:T(8,128)(2,1)}, bf16[512,1536]{1,0:T(8,128)(2,1)}, bf16[...) custom-call(bf16[2,512,512]{2,1,0:T(8,128)(2,1)} %refs_0_.7, ...), custom_call_target="tpu_custom_call" | custom-call | flops 2818572288 | bytes 12582912 | tf_op jit(solution)/shard_map/attention_forward/pallas_call | solution.py:267
  107.7 22.4 %all-to-all-done.1 = bf16[8,256,512]{2,1,0:T(8,128)(2,1)} async-done(((bf16[8,256,512]{2,1,0:T(8,128)(2,1)}), bf16[8,256,512]{2,1,0:T(8,128)(2,1)}, u32[]{:S(2)}, u32[]{:S(2)}) %all-to-all-start.1) | async-done | bytes 2097184 | tf_op jit(solution)/shard_map/all_to_all | solution.py:867
  130.1 3.6 all-to-all-start
  134.5 21.4 %attention_forward.3 = (f32[512,512]{1,0:T(8,128)}, bf16[512,512]{1,0:T(8,128)(2,1)}, bf16[512,512]{1,0:T(8,128)(2,1)}, bf16[512,1536]{1,0:T(8,128)(2,1)}, bf16[...) custom-call(bf16[2,512,512]{2,1,0:T(8,128)(2,1)} %refs_0_.7, ...), custom_call_target="tpu_custom_call" | custom-call | flops 2818572288 | bytes 12582912 | tf_op jit(solution)/shard_map/attention_forward/pallas_call | solution.py:267
  155.9 26.2 %all-to-all-done = bf16[8,256,512]{2,1,0:T(8,128)(2,1)S(1)} async-done(((bf16[8,256,512]{2,1,0:T(8,128)(2,1)}), bf16[8,256,512]{2,1,0:T(8,128)(2,1)S(1)}, u32[]{:S(2)}, u32[]{:S(2)}) %all-to-all-start) | async-done | bytes 2097184 | tf_op jit(solution)/shard_map/all_to_all | solution.py:867
  182.1 1.3 copy-done.2
  183.5 4.4 all-to-all-start.2
  188.3 18.7 %expert_forward.2 = (bf16[8,2,128,512]{3,2,1,0:T(8,128)(2,1)}, f32[8,2,8,128]{3,2,1,0:T(8,128)}) custom-call(bf16[8,2,128,512]{3,2,1,0:T(8,128)(2,1)} %bitcast.43, bf16[8,2,128,512]{3,2,1,0:T(8,128)(2,1)} %bitcast.12.grad_ref.refs_1_, f32[8,512]{1,0:T(8,128)} %stack.39.vec_ref.refs_3_, bf16[4,2,512,512]{3,2,1,0:T(8,128)(2,1)} %bitcast.63, ...), custom_call_target="tpu_custom_call" | custom-call | flops 8589934592 | bytes 14680064 | tf_op jit(solution)/shard_map/expert_forward/pallas_call | solution.py:338
  207.0 41.7 %scalar_step.2 = (f32[512,8]{1,0:T(8,128)}, f32[8,2,8,128]{3,2,1,0:T(8,128)}) custom-call(f32[8,2,8,128]{3,2,1,0:T(8,128)} %get-tuple-element.82.scal_ref, f32[8,512]{1,0:T(8,128)} %get-tuple-element.83.rowsc_ref, s32[8,512]{1,0:T(8,128)} %get-tuple-element.78.slotrow_ref), custom_call_target="tpu_custom_call" | custom-call | flops 1000000000 | bytes 1048576 | tf_op jit(solution)/shard_map/scalar_step/pallas_call | solution.py:573
  248.8 18.7 %expert_forward.3 = (bf16[8,2,128,512]{3,2,1,0:T(8,128)(2,1)}, f32[8,2,8,128]{3,2,1,0:T(8,128)}) custom-call(bf16[8,2,128,512]{3,2,1,0:T(8,128)(2,1)} %bitcast.16.rows_ref.refs_0_, bf16[8,2,128,512]{3,2,1,0:T(8,128)(2,1)} %bitcast.41, f32[8,512]{1,0:T(8,128)} %stack.39.vec_ref.refs_3_, bf16[4,2,512,512]{3,2,1,0:T(8,128)(2,1)} %bitcast.64, ...), custom_call_target="tpu_custom_call" | custom-call | flops 8589934592 | bytes 14680064 | tf_op jit(solution)/shard_map/expert_forward/pallas_call | solution.py:338
  267.5 19.2 %scalar_step.3 = (f32[512,8]{1,0:T(8,128)}, f32[8,2,8,128]{3,2,1,0:T(8,128)}) custom-call(f32[8,2,8,128]{3,2,1,0:T(8,128)} %get-tuple-element.89.scal_ref, f32[8,512]{1,0:T(8,128)} %get-tuple-element.90.rowsc_ref, s32[8,512]{1,0:T(8,128)} %get-tuple-element.86.slotrow_ref), custom_call_target="tpu_custom_call" | custom-call | flops 1000000000 | bytes 1048576 | tf_op jit(solution)/shard_map/scalar_step/pallas_call | solution.py:573
  286.7 37.9 %expert_backward.2 = (bf16[4,2,512,512]{3,2,1,0:T(8,128)(2,1)}, bf16[4,2,512,512]{3,2,1,0:T(8,128)(2,1)}, bf16[8,2,128,512]{3,2,1,0:T(8,128)(2,1)}, bf16[8,2,128,512]{3,2,1,0:T(8,128)(2,1)}) custom-call(bf16[8,2,128,512]{3,2,1,0:T(8,128)(2,1)} %bitcast.16.rows_ref.refs_0_, bf16[8,2,128,512]{3,2,1,0:T(8,128)(2,1)} %bitcast.42, ...), custom_call_target="tpu_custom_call" | custom-call | flops 21474836480 | bytes 23068672 | tf_op jit(solution)/shard_map/expert_backward/pallas_call | solution.py:450
  324.6 50.5 %expert_backward.3 = (bf16[4,2,512,512]{3,2,1,0:T(8,128)(2,1)}, bf16[4,2,512,512]{3,2,1,0:T(8,128)(2,1)}, bf16[8,2,128,512]{3,2,1,0:T(8,128)(2,1)}, bf16[8,2,128,512]{3,2,1,0:T(8,128)(2,1)}) custom-call(bf16[8,2,128,512]{3,2,1,0:T(8,128)(2,1)} %bitcast.44, bf16[8,2,128,512]{3,2,1,0:T(8,128)(2,1)} %bitcast.12.grad_ref.refs_1_, ...), custom_call_target="tpu_custom_call" | custom-call | flops 21474836480 | bytes 23068672 | tf_op jit(solution)/shard_map/expert_backward/pallas_call | solution.py:450
  376.8 62.6 %all_to_all.30 = bf16[8,256,512]{2,1,0:T(8,128)(2,1)} all-to-all(bf16[8,256,512]{2,1,0:T(8,128)(2,1)S(1)} %bitcast.49), channel_id=1, replica_groups=mesh['expert'=8,'hidden'=4] {'expert'}, dimensions={0} | all-to-all | bytes 4194304 | tf_op jit(solution)/shard_map/all_to_all | solution.py:867
  439.4 3.6 all-to-all-start.4
  443.1 32.1 %attention_backward.2 = (f32[2,512,512]{2,1,0:T(8,128)}, f32[512,1536]{1,0:T(8,128)}, f32[1536,512]{1,0:T(8,128)}, f32[512,256]{1,0:T(8,128)}, f32[512,128]{1,0:T(8,128)}, /*index=5*/f32[8,512]{1,0:T(8,128)}) custom-call(bf16[2,512,512]{2,1,0:T(8,128)(2,1)} %refs_0_.7, bf16[2,512,512]{2,1,0:T(8,128)(2,1)} %refs_1_.3, ...), custom_call_target="tpu_custom_call" | custom-call | flops 4563402752 | bytes 25165824 | tf_op jit(solution)/shard_map/attention_backward/pallas_call | solution.py:748
  475.1 15.3 %all-to-all-done.4 = bf16[8,256,512]{2,1,0:T(8,128)(2,1)S(1)} async-done(((bf16[8,256,512]{2,1,0:T(8,128)(2,1)}), bf16[8,256,512]{2,1,0:T(8,128)(2,1)S(1)}, u32[]{:S(2)}, u32[]{:S(2)}) %all-to-all-start.4) | async-done | bytes 2097184 | tf_op jit(solution)/shard_map/all_to_all | solution.py:867
  491.8 32.6 %attention_backward.3 = (f32[2,512,512]{2,1,0:T(8,128)}, bf16[512,1536]{1,0:T(8,128)(2,1)}, bf16[1536,512]{1,0:T(8,128)(2,1)}, bf16[512,256]{1,0:T(8,128)(2,1)},...) custom-call(bf16[2,512,512]{2,1,0:T(8,128)(2,1)} %refs_0_.7, ...), custom_call_target="tpu_custom_call", output_to_operand_aliasing={{0}: (24, {})} | custom-call | flops 4563402752 | bytes 25165824 | tf_op jit(solution)/shard_map/attention_backward/pallas_call | solution.py:748
  524.4 2.8 bitcast_convert_fusion
  527.2 2.8 bitcast_convert_fusion.1
  530.1 9.5 %result_step.2 = (bf16[2,512,512]{2,1,0:T(8,128)(2,1)}, f32[8,512]{1,0:T(8,128)}) custom-call(bf16[2,512,512]{2,1,0:T(8,128)(2,1)} %refs_0_.7, f32[512,512]{1,0:T(8,128)} %get-tuple-element.98.refs_1_.refs_8_, bf16[2048,512]{1,0:T(8,128)(2,1)} %bitcast.71, f32[512,8]{1,0:T(8,128)} %get-tuple-element.100.refs_3_.refs_18_, ...), custom_call_target="tpu_custom_call" | custom-call | flops 2147483648 | bytes 5242880 | tf_op jit(solution)/shard_map/result_step/pallas_call | solution.py:616
  539.6 9.6 %result_step.3 = (bf16[2,512,512]{2,1,0:T(8,128)(2,1)}, f32[8,512]{1,0:T(8,128)}) custom-call(bf16[2,512,512]{2,1,0:T(8,128)(2,1)} %refs_0_.7, f32[512,512]{1,0:T(8,128)} %get-tuple-element.79.refs_1_.refs_8_, bf16[2048,512]{1,0:T(8,128)(2,1)} %bitcast.72, f32[512,8]{1,0:T(8,128)} %get-tuple-element.96.refs_3_.refs_18_, ...), custom_call_target="tpu_custom_call", output_to_operand_aliasing={{0}: (5, {})} | custom-call | flops 2147483648 | bytes 5242880 | tf_op jit(solution)/shard_map/result_step/pallas_call | solution.py:616
  550.6 14.6 %sum_everywhere.1 = f32[16,512]{1,0:T(8,128)} custom-call(f32[16,512]{1,0:T(8,128)} %pad_maximum_fusion.value_ref), custom_call_target="tpu_custom_call" | custom-call | tf_op jit(solution)/shard_map/sum_everywhere/pallas_call | solution.py:823
  566.4 1.5 fusion.3
  567.9 105.9 %all-reduce.5.cloned.1.call-done = (bf16[512,256]{1,0:T(8,128)(2,1)}, bf16[512,1536]{1,0:T(8,128)(2,1)}, bf16[1536,512]{1,0:T(8,128)(2,1)}, bf16[512,128]{1,0:T(8,128)(2,1)}) async-done(((bf16[512,256]{1,0:T(8,128)(2,1)}, bf16[512,1536]{1,0:T(8,128)(2,1)}, bf16[1536,512]{1,0:T(8,128)(2,1)}, bf16[512,128]{1,0:T(8,128)(2,1)}), (bf16[512,256]{1,0:T(8,128)(2,1)}, bf16[512,1536]{1,0:T(8,128)(2,1)}, ...) | async-done | bytes 3538960 | tf_op jit(solution)/shard_map/psum | solution.py:916
  679.8 2.1 convert_element_type.31
  681.9 2.1 convert_element_type.32
  (78 shorter events, 26.0 us)
Async XLA Ops:
  21.1 55.5 %all-to-all-start.3 = ((bf16[8,256,512]{2,1,0:T(8,128)(2,1)}), bf16[8,256,512]{2,1,0:T(8,128)(2,1)S(1)}, u32[]{:S(2)}, u32[]{:S(2)}) async-start(bf16[8,256,512]{2,1,0:T(8,128)(2,1)} %bitcast.51), calls=%async_computation.3 | async-start | bytes 4194304 | tf_op jit(solution)/shard_map/all_to_all | solution.py:867
  28.4 159.9 %all-gather.5.cloned.1.call-start = ((), (), s32[]{:S(2)}) async-start(), calls=%async_computation.10 | async-start | bytes 5242880 | tf_op jit(solution)/shard_map/all_gather | solution.py:854
  76.6 1.3 copy-start.1
  76.6 6.3 copy-start.8
  76.6 6.5 copy-start.6
  76.6 6.6 copy-start.7
  76.6 6.7 copy-start.9
  76.6 7.6 %copy-start.12 = (f32[512]{0:T(512)S(1)}, f32[512]{0:T(512)}, u32[]{:S(2)}) copy-start(f32[512]{0:T(512)} %param.26) | copy-start | bytes 6148
  76.6 7.5 %copy-start.13 = (f32[512]{0:T(512)S(1)}, f32[512]{0:T(512)}, u32[]{:S(2)}) copy-start(f32[512]{0:T(512)} %param.27) | copy-start | bytes 6148
  76.7 7.5 %copy-start.14 = (f32[512]{0:T(512)S(1)}, f32[512]{0:T(512)}, u32[]{:S(2)}) copy-start(f32[512]{0:T(512)} %param.33) | copy-start | bytes 6148
  76.7 7.5 %copy-start.15 = (f32[512]{0:T(512)S(1)}, f32[512]{0:T(512)}, u32[]{:S(2)}) copy-start(f32[512]{0:T(512)} %param.34) | copy-start | bytes 6148
  76.7 7.5 %copy-start.16 = (f32[512]{0:T(512)S(1)}, f32[512]{0:T(512)}, u32[]{:S(2)}) copy-start(f32[512]{0:T(512)} %param.38) | copy-start | bytes 6148
  77.9 52.2 %all-to-all-start.1 = ((bf16[8,256,512]{2,1,0:T(8,128)(2,1)}), bf16[8,256,512]{2,1,0:T(8,128)(2,1)}, u32[]{:S(2)}, u32[]{:S(2)}) async-start(bf16[8,256,512]{2,1,0:T(8,128)(2,1)} %bitcast.46), calls=%async_computation.1 | async-start | bytes 4194304 | tf_op jit(solution)/shard_map/all_to_all | solution.py:867
  130.1 52.0 %all-to-all-start = ((bf16[8,256,512]{2,1,0:T(8,128)(2,1)}), bf16[8,256,512]{2,1,0:T(8,128)(2,1)S(1)}, u32[]{:S(2)}, u32[]{:S(2)}) async-start(bf16[8,256,512]{2,1,0:T(8,128)(2,1)} %bitcast.47), calls=%async_computation | async-start | bytes 4194304 | tf_op jit(solution)/shard_map/all_to_all | solution.py:867
  133.7 54.6 %all-gather.7.cloned.1.call-start = ((), (), s32[]{:S(2)}) async-start(), calls=%async_computation.11 | async-start | bytes 5242880 | tf_op jit(solution)/shard_map/all_gather | solution.py:855
  182.1 1.3 copy-start.2
  183.5 65.3 %all-to-all-start.2 = ((bf16[8,256,512]{2,1,0:T(8,128)(2,1)}), bf16[8,256,512]{2,1,0:T(8,128)(2,1)}, u32[]{:S(2)}, u32[]{:S(2)}) async-start(bf16[8,256,512]{2,1,0:T(8,128)(2,1)} %bitcast.48), calls=%async_computation.2 | async-start | bytes 4194304 | tf_op jit(solution)/shard_map/all_to_all | solution.py:867
  187.8 336.5 %reduce-scatter.5.cloned.1.call-start = ((), (), s32[]{:S(2)}) async-start(), calls=%async_computation.9 | async-start | bytes 5242880 | tf_op jit(solution)/shard_map/reduce_scatter | solution.py:902
  375.1 152.1 %reduce-scatter.3.cloned.1.call-start = ((), (), s32[]{:S(2)}) async-start(), calls=%async_computation.8 | async-start | bytes 5242880 | tf_op jit(solution)/shard_map/reduce_scatter | solution.py:901
  375.2 1.6 copy-start.3
  439.4 51.1 %all-to-all-start.4 = ((bf16[8,256,512]{2,1,0:T(8,128)(2,1)}), bf16[8,256,512]{2,1,0:T(8,128)(2,1)S(1)}, u32[]{:S(2)}, u32[]{:S(2)}) async-start(bf16[8,256,512]{2,1,0:T(8,128)(2,1)} %bitcast.45), calls=%async_computation.4 | async-start | bytes 4194304 | tf_op jit(solution)/shard_map/all_to_all | solution.py:867
  443.0 230.7 %all-reduce.5.cloned.1.call-start = ((), (), s32[]{:S(2)}) async-start(), calls=%async_computation.12 | async-start | bytes 7077888 | tf_op jit(solution)/shard_map/psum | solution.py:916
  490.5 1.3 copy-start
  539.6 9.6 %copy-start.10 = (f32[8,512]{1,0:T(8,128)S(1)}, f32[8,512]{1,0:T(8,128)}, u32[]{:S(2)}) copy-start(f32[8,512]{1,0:T(8,128)} %get-tuple-element.128) | copy-start | bytes 49156
  539.6 10.3 %copy-start.11 = (f32[8,512]{1,0:T(8,128)S(1)}, f32[8,512]{1,0:T(8,128)}, u32[]{:S(2)}) copy-start(f32[8,512]{1,0:T(8,128)} %get-tuple-element.127) | copy-start | bytes 49156
  673.8 6.1 copy-start.5
  679.8 2.1 copy-start.4
Sparse Core Ops, SparseCore 0:
  30.8 35.9 all-gather.4
  136.1 35.9 all-gather.6
  375.3 56.0 reduce-scatter.4
  433.9 44.5 reduce-scatter.2
  530.2 143.5 all-reduce.4

commit v3 on v1

v3 whole, which is shorter than its diff:
```python
import functools
import math

import jax
import jax.numpy as jnp
from jax import lax
from jax.experimental import pallas as pl
from jax.experimental.pallas import tpu as pltpu
from jax.sharding import PartitionSpec as P

SEQ = 256
LANES = 128
F32 = jnp.float32
BF16 = jnp.bfloat16
GELU_C = math.sqrt(2.0 / math.pi)
GELU_A = 0.044715
VMEM_LIMIT = 60 * 1024 * 1024


def mm(left, right):
    return jnp.dot(left, right, preferred_element_type=F32)


def mm_nt(left, right):
    return lax.dot_general(left, right, (((1,), (1,)), ((), ())), preferred_element_type=F32)


def mm_tn(left, right):
    return lax.dot_general(left, right, (((0,), (0,)), ((), ())), preferred_element_type=F32)


def lane_iota(rows, lanes=LANES):
    return lax.broadcasted_iota(jnp.int32, (rows, lanes), 1)


def norm_parts(value):
    center = value - jnp.mean(value, axis=-1, keepdims=True)
    rstd = lax.rsqrt(jnp.mean(center * center, axis=-1, keepdims=True) + 1e-05)
    return center * rstd, rstd


def norm_back(hat, rstd, gain, grad):
    scaled = grad * gain
    first = jnp.mean(scaled, axis=-1, keepdims=True)
    second = jnp.mean(scaled * hat, axis=-1, keepdims=True)
    return rstd * (scaled - first - hat * second)


def fold_rows(value):
    return jnp.sum(value, axis=0, keepdims=True)


def pick_head(tiles, route, lane):
    pair = lax.shift_right_logical(route, 1)
    out = tiles[0]
    for j in range(1, len(tiles)):
        out = jnp.where(pair == j, tiles[j], out)
    odd = (route & 1) == 1
    return jnp.where(odd, pltpu.roll(out, LANES // 2, 1), out)


def place_heads(parts, routes, count, lane):
    half = lax.shift_right_logical(lane, 6)
    kept = [jnp.where(half == (r & 1), p, 0.0) for p, r in zip(parts, routes)]
    pairs = [lax.shift_right_logical(r, 1) for r in routes]
    tiles = []
    for j in range(count):
        total = jnp.where(pairs[0] == j, kept[0], 0.0)
        for k, p in zip(kept[1:], pairs[1:]):
            total = total + jnp.where(p == j, k, 0.0)
        tiles.append(total)
    return tiles


def softmax_cols(cols):
    top = functools.reduce(jnp.maximum, cols)
    expo = [jnp.exp(c - top) for c in cols]
    total = functools.reduce(jnp.add, expo)
    return [e / total for e in expo]


def put_cols(cols, rows, width):
    lane = lane_iota(rows, width)
    out = jnp.zeros((rows, width), cols[0].dtype)
    for i, c in enumerate(cols):
        out = jnp.where(lane == i, c, out)
    return out


def split_three(value):
    high = value.astype(BF16)
    rest = value - high.astype(F32)
    middle = rest.astype(BF16)
    last = (rest - middle.astype(F32)).astype(BF16)
    return jnp.concatenate([high.astype(F32), middle.astype(F32), last.astype(F32)], axis=0).astype(BF16)


def join_three(value):
    n = value.shape[0] // 3
    return value[:n] + value[n : 2 * n] + value[2 * n :]


def row_to_col(row):
    n = row.shape[1]
    place = lax.broadcasted_iota(jnp.int32, (n, n), 0)
    other = lax.broadcasted_iota(jnp.int32, (n, n), 1)
    return jnp.sum(jnp.where(place == other, row, 0.0), axis=-1, keepdims=True)


def dispatch(slot_rows, values, out_ref):
    chunk = 256
    tokens = values[0].shape[0]
    spot = lax.broadcasted_iota(jnp.int32, (chunk, tokens), 0)

    def body(k, carry):
        base = spot + k * chunk
        if len(values) == 1:
            pick = jnp.where((base == slot_rows[0]) | (base == slot_rows[1]), 1.0, 0.0).astype(BF16)
            out = mm(pick, values[0][...])
        else:
            out = mm(jnp.where(base == slot_rows[0], 1.0, 0.0).astype(BF16), values[0][...])
            out = out + mm(jnp.where(base == slot_rows[1], 1.0, 0.0).astype(BF16), values[1][...])
        out_ref[pl.ds(pl.multiple_of(k * chunk, chunk), chunk), :] = out.astype(BF16)
        return carry

    lax.fori_loop(0, out_ref.shape[0] // chunk, body, 0)


def group_of():
    size = lax.axis_size("expert") // 2
    e = lax.axis_index("expert")
    me = lax.rem(e, size)
    return me, size, e - me


def group_greet():
    me, size, base = group_of()
    other = lax.axis_index("hidden")
    barrier = pltpu.get_barrier_semaphore()
    for k in range(1, size):
        pl.semaphore_signal(
            barrier, inc=1, device_id=(base + lax.rem(me + k, size), other), device_id_type=pl.DeviceIdType.MESH
        )
    pl.semaphore_wait(barrier, size - 1)


def group_copies(source, target, send_sem, recv_sem):
    me, size, base = group_of()
    other = lax.axis_index("hidden")
    moves = []
    for k in range(1, size):
        peer = lax.rem(me + k, size)
        moves.append(
            pltpu.make_async_remote_copy(
                source.at[peer], target.at[me], send_sem.at[k - 1], recv_sem.at[k - 1],
                device_id=(base + peer, other), device_id_type=pl.DeviceIdType.MESH,
            )
        )
    return moves


def at_step(which):
    found = True
    for axis, size in enumerate(which[1]):
        here = pl.program_id(axis) == (0 if which[0] == 0 else size - 1)
        found = here if found is True else found & here
    return found


def run_kernel(kernel, args, in_specs, out_shape, out_specs, scratch, grid, name, cost, moving=(), cid=None, aliases=None):
    n_in, n_out, n_move = len(args), len(out_shape), len(moving)
    peers = lax.axis_size("expert") // 2 - 1
    hbm = pl.BlockSpec(memory_space=pl.ANY)

    def body(*refs):
        ins, sources = refs[:n_in], refs[n_in : n_in + n_move]
        outs = refs[n_in + n_move : n_in + n_move + n_out]
        targets = refs[n_in + n_move + n_out : n_in + 2 * n_move + n_out]
        rest = refs[n_in + 2 * n_move + n_out :]
        sems = rest[len(scratch) :]
        moves, owns = [], []
        me = group_of()[0]
        pairs = []
        for a, b in zip(sources, targets):
            pairs += [(a, b)] if len(a.shape) == 4 else [(a.at[i], b.at[i]) for i in range(a.shape[0])]
        for i, (a, b) in enumerate(pairs):
            moves += group_copies(a, b, sems[3 * i], sems[3 * i + 1])
            owns.append(pltpu.make_async_copy(a.at[me], b.at[me], sems[3 * i + 2]))

        if moving:

            @pl.when(at_step((0, grid)))
            def _():
                group_greet()
                for c in moves + owns:
                    c.start()

        kernel(*ins, *outs, *rest[: len(scratch)])

        if moving:

            @pl.when(at_step((1, grid)))
            def _():
                for c in moves + owns:
                    c.wait()

    sems = []
    for _ in range(sum(1 if a.ndim == 4 else a.shape[0] for a in moving)):
        sems += [pltpu.SemaphoreType.DMA((peers,)), pltpu.SemaphoreType.DMA((peers,)), pltpu.SemaphoreType.DMA]
    more = dict(collective_id=cid, has_side_effects=True) if moving else {}
    return pl.pallas_call(
        body,
        grid=grid,
        out_shape=tuple(out_shape) + tuple(jax.ShapeDtypeStruct(a.shape, a.dtype) for a in moving),
        in_specs=list(in_specs) + [hbm] * n_move,
        out_specs=list(out_specs) + [hbm] * n_move,
        scratch_shapes=list(scratch) + sems,
        input_output_aliases=aliases or {},
        compiler_params=pltpu.CompilerParams(vmem_limit_bytes=VMEM_LIMIT, **more),
        cost_estimate=cost,
        name=name,
    )(*args, *moving)


def route_kernel(row_ref, grad_ref, slotrow_ref, slotcol_ref, out_ref):
    tokens = grad_ref.shape[1]
    before = lax.broadcasted_iota(jnp.int32, (tokens, tokens), 0)
    after = lax.broadcasted_iota(jnp.int32, (tokens, tokens), 1)
    upper = jnp.where(before < after, 1.0, 0.0).astype(BF16)
    sub = lax.broadcasted_iota(jnp.int32, (LANES, tokens), 0)
    row = row_ref[0]
    named = [jnp.where(sub == row[2 + i : 3 + i, :], 1.0, 0.0) for i in range(2)]
    rank = mm((named[0] + named[1]).astype(BF16), upper)
    slots = [fold_rows(named[i] * rank).astype(jnp.int32) + row[4 + i : 5 + i, :] for i in range(2)]
    sub8 = lax.broadcasted_iota(jnp.int32, (8, tokens), 0)
    slotrow_ref[0] = jnp.where(sub8 == 0, slots[0], slots[1])
    table = jnp.where(sub == 0, slots[0].astype(F32), slots[1].astype(F32))
    slotcol_ref[0] = jnp.transpose(table)[:, :8].astype(jnp.int32)
    dispatch(slots, [grad_ref.at[0]], out_ref.at[0])


def route_step(row, grad, slots):
    micros, count, width = grad.shape
    out_shape = (
        jax.ShapeDtypeStruct((micros, 8, count), jnp.int32),
        jax.ShapeDtypeStruct((micros, count, 8), jnp.int32),
        jax.ShapeDtypeStruct((micros, slots, width), BF16),
    )
    spec = lambda a, b: pl.BlockSpec((1, a, b), lambda m: (m, 0, 0))
    return run_kernel(
        route_kernel, (row, grad), [spec(8, count), spec(count, width)], out_shape,
        [spec(8, count), spec(count, 8), spec(slots, width)], (), (micros,), "route_step",
        pl.CostEstimate(flops=4 * count * width * slots, bytes_accessed=6 << 20, transcendentals=0),
    )


def attention_forward_kernel(
    x_ref, grad_ref, col_ref, row_ref, slotrow_ref, vec_ref, hb_ref, qw_ref, kvr_ref, proj_ref, frw_ref,
    mid_ref, n2_ref, normed_ref, mixed_ref, probs_ref, qs_ref, kv_ref, gates_ref, scal_ref, out_ref,
    n2_all,
):
    step = pl.program_id(0)
    rows = x_ref.shape[1]
    top_attn = 4
    lane = lane_iota(rows)
    x = x_ref[0].astype(F32)
    col = col_ref[0]
    row = row_ref[0]
    hat, _ = norm_parts(x)
    normed = (hat * vec_ref[0:1, :] + vec_ref[1:2, :]).astype(BF16)
    normed_ref[...] = normed
    kvr = mm(normed, kvr_ref[...])
    kv = kvr[:, :LANES].astype(BF16)
    kv_ref[...] = kv
    logits = kvr[:, LANES:]
    routes = [col[:, i : i + 1] for i in range(top_attn)]
    picked = [
        jnp.sum(jnp.where(lane == r, logits, 0.0), axis=-1, keepdims=True) for r in routes
    ]
    gates = softmax_cols(picked)
    query = mm(normed, qw_ref[...])
    heads_pairs = query.shape[1] // LANES
    tiles = [query[:, j * LANES : (j + 1) * LANES] for j in range(heads_pairs)]
    low = lane < LANES // 2
    same = col[:, 6:7] == row[0:1, :]
    place = lax.broadcasted_iota(jnp.int32, (rows, rows), 0)
    other = lax.broadcasted_iota(jnp.int32, (rows, rows), 1)
    allowed = same & ((row[1:2, :] == 1) | (place == other))
    scale = 0.125
    shares = []
    for i in range(top_attn):
        sel = jnp.where(low, pick_head(tiles, routes[i], lane), 0.0).astype(BF16)
        qs_ref[0, i] = sel
        scores = mm_nt(sel, kv) * scale
        scores = jnp.where(allowed, scores, -1e30)
        expo = jnp.exp(scores - jnp.max(scores, axis=-1, keepdims=True))
        probs = (expo * (1.0 / jnp.sum(expo, axis=-1, keepdims=True))).astype(BF16)
        probs_ref[0, i] = probs
        heads = mm(probs, kv) * gates[i]
        shares.append(jnp.where(low, pltpu.roll(heads, LANES // 2, 1), heads))
    mixed_tiles = place_heads(shares, routes, heads_pairs, lane)
    mixed = jnp.concatenate([t.astype(BF16) for t in mixed_tiles], axis=1)
    mixed_ref[...] = mixed
    mid = x + mm(mixed, proj_ref[...])
    mid_ref[...] = mid
    hat2, _ = norm_parts(mid)
    n2 = (hat2 * vec_ref[2:3, :] + vec_ref[3:4, :]).astype(BF16)
    n2_ref[...] = n2
    n2_all[pl.ds(pl.multiple_of(step * rows, rows), rows), :] = n2
    logits_ffn = mm(n2, frw_ref[...])
    gates_ffn = softmax_cols(
        [
            jnp.sum(jnp.where(lane == col[:, 4 + i : 5 + i], logits_ffn, 0.0), axis=-1, keepdims=True)
            for i in range(2)
        ]
    )
    gates_ref[...] = put_cols(gates, rows, gates_ref.shape[1])
    stop = jnp.sum(mid * vec_ref[4:5, :], axis=-1, keepdims=True) + hb_ref[0:1, 0:1]
    pull = jnp.sum(grad_ref[0].astype(F32) * (mid - x), axis=-1, keepdims=True)
    scal_ref[...] = jnp.transpose(put_cols([stop, pull] + gates_ffn, rows, LANES))[:8, :]

    @pl.when(step == pl.num_programs(0) - 1)
    def _():
        dispatch([slotrow_ref[0, 0:1, :], slotrow_ref[0, 1:2, :]], [n2_all], out_ref)


def attention_forward(micro, tokens, grad, col, row, slotrow, vec, hb, qw, kvr, proj, frw, slots, moving, cid):
    _, count, width = tokens.shape
    steps = count // SEQ
    inner = qw.shape[1]
    whole = lambda a: pl.BlockSpec(a.shape, lambda r: (0,) * a.ndim)
    out_shape = (
        jax.ShapeDtypeStruct((count, width), F32),
        jax.ShapeDtypeStruct((count, width), BF16),
        jax.ShapeDtypeStruct((count, width), BF16),
        jax.ShapeDtypeStruct((count, inner), BF16),
        jax.ShapeDtypeStruct((steps, 4, SEQ, SEQ), BF16),
        jax.ShapeDtypeStruct((steps, 4, SEQ, LANES), BF16),
        jax.ShapeDtypeStruct((count, LANES), BF16),
        jax.ShapeDtypeStruct((count, 8), F32),
        jax.ShapeDtypeStruct((8, count), F32),
        jax.ShapeDtypeStruct((slots, width), BF16),
    )
    by_row = lambda c: pl.BlockSpec((SEQ, c), lambda r: (r, 0))
    in_specs = [
        pl.BlockSpec((1, SEQ, width), lambda r: (micro, r, 0)),
        pl.BlockSpec((1, SEQ, width), lambda r: (micro, r, 0)),
        pl.BlockSpec((1, SEQ, 8), lambda r: (micro, r, 0)),
        pl.BlockSpec((1, 8, SEQ), lambda r: (micro, 0, r)),
        pl.BlockSpec((1, 8, count), lambda r: (micro, 0, 0)),
        whole(vec), whole(hb), whole(qw), whole(kvr), whole(proj), whole(frw),
    ]
    out_specs = [
        by_row(width), by_row(width), by_row(width), by_row(inner),
        pl.BlockSpec((1, 4, SEQ, SEQ), lambda r: (r, 0, 0, 0)),
        pl.BlockSpec((1, 4, SEQ, LANES), lambda r: (r, 0, 0, 0)),
        by_row(LANES), by_row(8),
        pl.BlockSpec((8, SEQ), lambda r: (0, r)),
        pl.BlockSpec((slots, width), lambda r: (0, 0)),
    ]
    return run_kernel(
        attention_forward_kernel, (tokens, grad, col, row, slotrow, vec, hb, qw, kvr, proj, frw), in_specs,
        out_shape, out_specs, [pltpu.VMEM((count, width), BF16)], (steps,), "attention_forward",
        pl.CostEstimate(
            flops=2 * count * width * (2 * inner + 256 + slots), bytes_accessed=12 << 20, transcendentals=count * 4 * SEQ
        ),
        moving, cid,
    )


def gelu_parts(pre):
    square = pre * pre
    inner = jnp.tanh(GELU_C * pre * (1.0 + GELU_A * square))
    return square, inner


def expert_forward_kernel(rows0_ref, rows1_ref, first_ref, second_ref, out0_ref, out1_ref, total):
    part = pl.program_id(1)
    _, src, _, cap, width = rows0_ref.shape
    half = src * cap
    rows = jnp.concatenate([r[...].reshape(half, width) for r in (rows0_ref, rows1_ref)], axis=0)
    pre = mm(rows, first_ref[0, 0])
    _, inner = gelu_parts(pre)
    act = (0.5 * pre * (1.0 + inner)).astype(BF16)
    res = mm(act, second_ref[0, 0])

    @pl.when(part == 0)
    def _():
        total[...] = res

    @pl.when(part > 0)
    def _():
        total[...] += res

    @pl.when(part == pl.num_programs(1) - 1)
    def _():
        out0_ref[...] = total[:half, :].astype(BF16).reshape(out0_ref.shape)
        out1_ref[...] = total[half:, :].astype(BF16).reshape(out1_ref.shape)


def expert_forward(kind, rows, first, second, moving, cid):
    _, src, local, cap, width = rows[0].shape
    parts, _, _, hid = first.shape
    spec_in = pl.BlockSpec((1, src, 1, cap, width), lambda e, h: (kind, 0, e, 0, 0))
    spec_rows = pl.BlockSpec((src, 1, cap, width), lambda e, h: (0, e, 0, 0))
    work = 2 * src * local * cap * width * hid * parts
    return run_kernel(
        expert_forward_kernel, (*rows, first, second),
        [
            spec_in, spec_in,
            pl.BlockSpec((1, 1, width, hid), lambda e, h: (h, e, 0, 0)),
            pl.BlockSpec((1, 1, hid, width), lambda e, h: (h, e, 0, 0)),
        ],
        [jax.ShapeDtypeStruct(r.shape[1:], BF16) for r in rows], [spec_rows] * 2,
        [pltpu.VMEM((2 * src * cap, width), F32)], (local, parts), "expert_forward",
        pl.CostEstimate(flops=4 * work, bytes_accessed=24 << 20, transcendentals=work // width), moving, cid,
    )


def reading_kernel(*refs):
    outs, grads = refs[:4], refs[4:8]
    vec_ref, scal_ref = refs[8:]
    src, _, cap, width = outs[0].shape
    halt = split_three(jnp.broadcast_to(vec_ref[4:5, :], (8, width)))
    ones = jnp.ones((8, width), BF16)
    sub8 = lax.broadcasted_iota(jnp.int32, (8, cap), 0)
    for kind in range(2):
        for m in range(2):
            for s in range(src):
                low = outs[2 * kind + m][s, 0]
                stop = join_three(mm_nt(halt, low))
                prod = low.astype(F32) * grads[2 * kind + m][0, s, 0].astype(F32)
                high = prod.astype(BF16)
                rest = (prod - high.astype(F32)).astype(BF16)
                pull = mm_nt(ones, high) + mm_nt(ones, rest)
                scal_ref[s, m, kind, 0] = jnp.where(sub8 == 0, stop, pull)


def reading_step(outs, grads, vec):
    src, local, cap, width = outs[0].shape
    spec_rows = pl.BlockSpec((src, 1, cap, width), lambda e: (0, e, 0, 0))
    spec_grad = lambda kind: pl.BlockSpec((1, src, 1, cap, width), lambda e: (kind, 0, e, 0, 0))
    return run_kernel(
        reading_kernel, (*outs, *grads, *grads, vec),
        [spec_rows] * 4 + [spec_grad(0)] * 2 + [spec_grad(1)] * 2 + [pl.BlockSpec(vec.shape, lambda e: (0, 0))],
        [jax.ShapeDtypeStruct((src, 2, 2, local, 8, cap), F32)],
        [pl.BlockSpec((src, 2, 2, 1, 8, cap), lambda e: (0, 0, 0, e, 0, 0))], (), (local,), "reading_step",
        pl.CostEstimate(flops=10**9, bytes_accessed=8 << 20, transcendentals=0),
    )[0].reshape(src, 2, 2 * local, 8, cap)


def expert_backward_kernel(
    rows0_ref, rows1_ref, grad0_ref, grad1_ref, ab_ref, vec_ref, first_ref, second_ref,
    gfirst_ref, gsecond_ref, out0_ref, out1_ref, total, gin_all,
):
    part = pl.program_id(1)
    _, src, _, cap, width = rows0_ref.shape
    half = src * cap

    @pl.when(part == 0)
    def _():
        for m, grad_ref in enumerate((grad0_ref, grad1_ref)):
            for s in range(src):
                ab = ab_ref[s, m, 0]
                scaled = row_to_col(ab[0:1, :]) * grad_ref[0, s, 0].astype(F32) + row_to_col(ab[1:2, :]) * vec_ref[4:5, :]
                gin_all[m * half + s * cap : m * half + (s + 1) * cap, :] = scaled.astype(BF16)

    rows = jnp.concatenate([r[...].reshape(half, width) for r in (rows0_ref, rows1_ref)], axis=0)
    gin = gin_all[...]
    first = first_ref[0, 0]
    second = second_ref[0, 0]
    pre = mm(rows, first)
    gact = mm_nt(gin, second)
    square, inner = gelu_parts(pre)
    part_one = 0.5 * (1.0 + inner)
    act = (pre * part_one).astype(BF16)
    slope = part_one + 0.5 * pre * (1.0 - inner * inner) * (GELU_C + (3.0 * GELU_C * GELU_A) * square)
    gpre = (gact * slope).astype(BF16)
    gsecond_ref[0, 0] = mm_tn(act, gin).astype(BF16)
    gfirst_ref[0, 0] = mm_tn(rows, gpre).astype(BF16)
    res = mm_nt(gpre, first)

    @pl.when(part == 0)
    def _():
        total[...] = res

    @pl.when(part > 0)
    def _():
        total[...] += res

    @pl.when(part == pl.num_programs(1) - 1)
    def _():
        out0_ref[...] = total[:half, :].astype(BF16).reshape(out0_ref.shape)
        out1_ref[...] = total[half:, :].astype(BF16).reshape(out1_ref.shape)


def expert_backward(kind, rows, grads, ab, vec, first, second, moving, cid):
    _, src, local, cap, width = rows[0].shape
    parts, _, _, hid = first.shape
    spec_in = pl.BlockSpec((1, src, 1, cap, width), lambda e, h: (kind, 0, e, 0, 0))
    spec_rows = pl.BlockSpec((src, 1, cap, width), lambda e, h: (0, e, 0, 0))
    spec_first = pl.BlockSpec((1, 1, width, hid), lambda e, h: (h, e, 0, 0))
    spec_second = pl.BlockSpec((1, 1, hid, width), lambda e, h: (h, e, 0, 0))
    work = 2 * src * local * cap * width * hid * parts
    return run_kernel(
        expert_backward_kernel, (*rows, *grads, ab, vec, first, second),
        [spec_in] * 4
        + [pl.BlockSpec((src, 2, 1, 8, cap), lambda e, h: (0, 0, kind * local + e, 0, 0)), pl.BlockSpec(vec.shape, lambda e, h: (0, 0))]
        + [spec_first, spec_second],
        [jax.ShapeDtypeStruct(first.shape, BF16), jax.ShapeDtypeStruct(second.shape, BF16)]
        + [jax.ShapeDtypeStruct(r.shape[1:], BF16) for r in rows],
        [spec_first, spec_second, spec_rows, spec_rows],
        [pltpu.VMEM((2 * src * cap, width), F32), pltpu.VMEM((2 * src * cap, width), BF16)],
        (local, parts), "expert_backward",
        pl.CostEstimate(flops=10 * work, bytes_accessed=48 << 20, transcendentals=work // width), moving, cid,
    )


def scalar_kernel(scal_ref, rowsc0_ref, rowsc1_ref, slotrow_ref, cols_ref, ab_ref, got, sent, got2, send_sem, recv_sem, send_sem2, recv_sem2):
    src, micros, local, _, cap = scal_ref.shape
    tokens = rowsc0_ref.shape[1]
    me = group_of()[0]
    group_greet()
    moves = group_copies(scal_ref, got, send_sem, recv_sem)
    for c in moves:
        c.start()
    got[me] = scal_ref[me]
    for c in moves:
        c.wait()
    spot = lax.broadcasted_iota(jnp.int32, (cap, tokens), 0)
    sub = lax.broadcasted_iota(jnp.int32, (LANES, tokens), 0)
    sub8 = lax.broadcasted_iota(jnp.int32, (8, tokens), 0)
    for m, rowsc_ref in enumerate((rowsc0_ref, rowsc1_ref)):
        slot = [slotrow_ref[m, i : i + 1, :] for i in range(2)]

        def onehot(expert):
            per = local // 2
            which = lax.rem(expert, local)
            base = lax.div(which, per) * (src * per) + lax.div(expert, local) * per + lax.rem(which, per)
            base = spot + base * cap
            return [jnp.where(base == s, 1.0, 0.0).astype(BF16) for s in slot]

        zero = jnp.zeros((24, tokens), F32)

        def collect(expert, carry):
            values = split_three(got[lax.div(expert, local), m, lax.rem(expert, local)])
            return tuple(c + mm(values, p) for c, p in zip(carry, onehot(expert)))

        found = lax.fori_loop(0, src * local, collect, (zero, zero))
        found = [join_three(f) for f in found]
        stop, pull, gate0, gate1 = [rowsc_ref[i : i + 1, :] for i in range(4)]
        gates = [gate0, gate1]
        yh = [f[0:1, :] for f in found]
        yg = [f[1:2, :] for f in found]
        halting = jax.nn.sigmoid(stop + gate0 * yh[0] + gate1 * yh[1])
        s = (pull + gate0 * yg[0] + gate1 * yg[1]) * halting * (1.0 - halting)
        u = [halting * g + s * h for g, h in zip(yg, yh)]
        mean = gate0 * u[0] + gate1 * u[1]
        keep = [halting, s, gate0 * (u[0] - mean), gate1 * (u[1] - mean), gate0, gate1]
        table = jnp.zeros((LANES, tokens), F32)
        for i, r in enumerate(keep):
            table = jnp.where(sub == i, r, table)
        cols_ref[m] = jnp.transpose(table)[:, :8]
        ab = [split_three(jnp.where(sub8 == 0, g * halting, jnp.where(sub8 == 1, g * s, 0.0))) for g in gates]

        def spread(expert, carry):
            picks = onehot(expert)
            sent[lax.div(expert, local), m, lax.rem(expert, local)] = join_three(
                mm_nt(ab[0], picks[0]) + mm_nt(ab[1], picks[1])
            )
            return carry

        lax.fori_loop(0, src * local, spread, 0)
    moves = group_copies(sent, got2, send_sem2, recv_sem2)
    for c in moves:
        c.start()
    got2[me] = sent[me]
    for c in moves:
        c.wait()
    ab_ref[...] = got2[...]


def scalar_step(scal, rowsc, slotrow):
    vmem = pl.BlockSpec(memory_space=pltpu.VMEM)
    tokens = rowsc[0].shape[1]
    peers = scal.shape[0] - 1
    return pl.pallas_call(
        scalar_kernel,
        out_shape=(jax.ShapeDtypeStruct((2, tokens, 8), F32), jax.ShapeDtypeStruct(scal.shape, F32)),
        in_specs=[vmem] * 4,
        out_specs=[vmem] * 2,
        scratch_shapes=[pltpu.VMEM(scal.shape, F32)] * 3 + [pltpu.SemaphoreType.DMA((peers,))] * 4,
        compiler_params=pltpu.CompilerParams(collective_id=0, has_side_effects=True),
        cost_estimate=pl.CostEstimate(flops=10**9, bytes_accessed=1 << 20, transcendentals=tokens),
        name="scalar_step",
    )(scal, *rowsc, slotrow)


def result_kernel(has_old, *refs):
    x_ref, mid_ref, near_ref, far_ref, cols_ref, slotcol_ref = refs[:6]
    result_ref, hsum_ref = refs[-2:]
    tokens, width = mid_ref.shape
    chunk = 256
    chunks = near_ref.shape[0] // chunk
    lane = lane_iota(tokens, chunk)
    slot_c = [slotcol_ref[0, :, i : i + 1] for i in range(2)]

    def gather(k, carry):
        for kind, ref in enumerate((near_ref, far_ref)):
            block = ref[pl.ds(pl.multiple_of(k * chunk, chunk), chunk), :]
            base = lane + (k + kind * chunks) * chunk
            carry = tuple(
                c + mm(jnp.where(base == s, 1.0, 0.0).astype(BF16), block) for c, s in zip(carry, slot_c)
            )
        return carry

    zero = jnp.zeros((tokens, width), F32)
    picked = lax.fori_loop(0, chunks, gather, (zero, zero))
    cols = cols_ref[0]
    halting, s = cols[:, 0:1], cols[:, 1:2]
    x = x_ref[0].astype(F32)
    end = mid_ref[...] + (cols[:, 4:5] * picked[0] + cols[:, 5:6] * picked[1])
    result_ref[0] = (x + halting * (end - x)).astype(BF16)
    sub8 = lax.broadcasted_iota(jnp.int32, (8, width), 0)
    ssum = jnp.broadcast_to(jnp.sum(s, axis=0, keepdims=True), (1, width))
    hsum_ref[...] = jnp.where(sub8 == 0, fold_rows(s * end), jnp.where(sub8 == 1, ssum, 0.0))


def result_step(micro, tokens, mid, near, far, cols, slotcol, old, moving, cid):
    _, count, width = tokens.shape
    whole = lambda a: pl.BlockSpec(a.shape, lambda i: (0,) * a.ndim)
    part = pl.BlockSpec((1, count, width), lambda i: (micro, 0, 0))
    cols_spec = pl.BlockSpec((1, count, 8), lambda i: (micro, 0, 0))
    return run_kernel(
        functools.partial(result_kernel, bool(old)), (tokens, mid, near, far, cols, slotcol, *old),
        [part, whole(mid), whole(near), whole(far), cols_spec, cols_spec] + [pl.BlockSpec(memory_space=pl.ANY)] * len(old),
        (jax.ShapeDtypeStruct(tokens.shape, BF16), jax.ShapeDtypeStruct((8, width), F32)),
        [part, pl.BlockSpec((8, width), lambda i: (0, 0))], (), (1,), "result_step",
        pl.CostEstimate(
            flops=8 * count * near.shape[0] * width, bytes_accessed=5 << 20, transcendentals=count
        ),
        moving, cid, {6: 0} if old else None,
    )


def attention_backward_kernel(last, n_old, *refs):
    (x_ref, grad_ref, col_ref, vec_ref, qw_ref, kvr_ref, proj_ref, frw_ref,
     mid_ref, n2_ref, normed_ref, mixed_ref, probs_ref, qs_ref, kv_ref, gates_ref, slotcol_ref,
     near_ref, far_ref, cols_ref) = refs[:20]
    old = refs[20 : 20 + n_old]
    gtok_ref = refs[20 + n_old]
    outs = refs[21 + n_old : -6]
    gsum, gq_ref, gproj_ref, gkvr_ref, gfr_ref, gvec_ref = refs[-6:]
    step = pl.program_id(0)
    rows, width = mid_ref.shape
    lane = lane_iota(rows)
    low = lane < LANES // 2
    col = col_ref[0]
    chunk = 256
    cols = cols_ref[0]
    slot_c = [slotcol_ref[0, :, i : i + 1] for i in range(2)]
    lane_c = lane_iota(rows, chunk)
    accs = (gq_ref, gproj_ref, gkvr_ref, gfr_ref, gvec_ref)

    @pl.when(step == 0)
    def _():
        for k, ref in enumerate(accs):
            ref[...] = old[k][...] if old else jnp.zeros_like(ref)

    gsum[...] = jnp.zeros_like(gsum)

    chunks = near_ref.shape[0] // chunk

    def gather(k, carry):
        for kind, ref in enumerate((near_ref, far_ref)):
            block = ref[pl.ds(pl.multiple_of(k * chunk, chunk), chunk), :]
            base = lane_c + (k + kind * chunks) * chunk
            pick = jnp.where((base == slot_c[0]) | (base == slot_c[1]), 1.0, 0.0).astype(BF16)
            gsum[...] += mm(pick, block)
        return carry

    lax.fori_loop(0, chunks, gather, 0)
    glog = jnp.zeros((rows, LANES), F32)
    for i in range(2):
        glog = jnp.where(lane == col[:, 4 + i : 5 + i], cols[:, 2 + i : 3 + i], glog)
    glog = glog.astype(BF16)
    n2 = n2_ref[...]
    gfr_ref[...] += mm_tn(n2, glog)
    gn2 = gsum[...] + mm_nt(glog, frw_ref[...])
    hat2, rstd2 = norm_parts(mid_ref[...])
    grad = grad_ref[0].astype(F32)
    halting = cols[:, 0:1]
    gend = halting * grad + cols[:, 1:2] * vec_ref[4:5, :]
    gmid = gend + norm_back(hat2, rstd2, vec_ref[2:3, :], gn2)
    ggain2 = fold_rows(gn2 * hat2)
    gbias2 = fold_rows(gn2)
    gattn = gmid.astype(BF16)
    gproj_ref[...] += mm_tn(mixed_ref[...], gattn)
    gmixed = mm_nt(gattn, proj_ref[...]).astype(BF16).astype(F32)
    pairs = gmixed.shape[1] // LANES
    tiles = [gmixed[:, j * LANES : (j + 1) * LANES] for j in range(pairs)]
    kv = kv_ref[...]
    scale = 0.125
    routes = [col[:, i : i + 1] for i in range(4)]
    gkv = jnp.zeros((rows, LANES), F32)
    ggates = []
    parts = []
    for i in range(4):
        gate = gates_ref[:, i : i + 1]
        sel = pltpu.roll(pick_head(tiles, routes[i], lane), LANES // 2, 1)
        sel = jnp.where(low, 0.0, sel)
        probs = probs_ref[0, i]
        heads = mm(probs, kv)
        ggates.append(jnp.sum(heads * sel, axis=-1, keepdims=True))
        gheads = (gate * sel).astype(BF16)
        gprobs = mm_nt(gheads, kv)
        probs_f = probs.astype(F32)
        inner = jnp.sum(probs_f * gprobs, axis=-1, keepdims=True)
        gscores = (probs_f * (gprobs - inner)).astype(BF16)
        gkv = gkv + mm_tn(probs, gheads) + mm_tn(gscores, qs_ref[0, i]) * scale
        gq = mm(gscores, kv) * scale
        parts.append(jnp.where(low, gq, pltpu.roll(gq, LANES // 2, 1)))
    gtiles = place_heads(parts, routes, pairs, lane)
    gquery = jnp.concatenate([t.astype(BF16) for t in gtiles], axis=1)
    normed = normed_ref[...]
    gq_ref[...] += mm_tn(normed, gquery)
    mean = ggates[0] * gates_ref[:, 0:1]
    for i in range(1, 4):
        mean = mean + ggates[i] * gates_ref[:, i : i + 1]
    alog = jnp.zeros((rows, LANES), F32)
    for i in range(4):
        alog = jnp.where(lane == routes[i], gates_ref[:, i : i + 1] * (ggates[i] - mean), alog)
    gkvr = jnp.concatenate([gkv.astype(BF16), alog.astype(BF16)], axis=1)
    gkvr_ref[...] += mm_tn(normed, gkvr)
    gnormed = mm_nt(gquery, qw_ref[...]) + mm_nt(gkvr, kvr_ref[...])
    hat, rstd = norm_parts(x_ref[0].astype(F32))
    gtok_ref[0] = grad * (1.0 - halting) + gmid + norm_back(hat, rstd, vec_ref[0:1, :], gnormed)
    sub8 = lax.broadcasted_iota(jnp.int32, (8, width), 0)
    gvec = jnp.where(sub8 == 0, fold_rows(gnormed * hat), 0.0)
    gvec = jnp.where(sub8 == 1, fold_rows(gnormed), gvec)
    gvec = jnp.where(sub8 == 2, ggain2, gvec)
    gvec_ref[...] += jnp.where(sub8 == 3, gbias2, gvec)

    @pl.when(step == pl.num_programs(0) - 1)
    def _():
        if not last:
            for ref, out in zip(accs, outs):
                out[...] = ref[...]
            return
        pack, gvec_out = outs
        gvec_out[...] = gvec_ref[...]
        blocks = gq_ref.shape[1] // width
        for j in range(blocks):
            pack[j * width : (j + 1) * width, :] = gq_ref[:, j * width : (j + 1) * width].astype(BF16)
        place = blocks * width
        pack[place : place + gproj_ref.shape[0], :] = gproj_ref[...].astype(BF16)
        place = place + gproj_ref.shape[0]
        wide = gkvr_ref.shape[1]
        pack[place : place + width, :wide] = gkvr_ref[...].astype(BF16)
        pack[place : place + width, wide : wide + LANES] = gfr_ref[...].astype(BF16)
        pack[place : place + width, wide + LANES :] = jnp.zeros((width, width - wide - LANES), BF16)
        if pack.shape[0] > place + width:
            pack[place + width :, :] = jnp.zeros((pack.shape[0] - place - width, width), BF16)


def attention_backward(micro, last, packed_rows, tokens, grad, col, vec, qw, kvr, proj, frw, saved, near, far, cols, old, moving, cid):
    mid, n2, normed, mixed, probs, qs, kv, gates, slotcol = saved
    _, count, width = tokens.shape
    steps = count // SEQ
    inner = qw.shape[1]
    whole = lambda a: pl.BlockSpec(a.shape, lambda r: (0,) * a.ndim)
    by_row = lambda c: pl.BlockSpec((SEQ, c), lambda r: (r, 0))
    part = pl.BlockSpec((1, SEQ, width), lambda r: (micro, r, 0))
    out_shape = [jax.ShapeDtypeStruct(tokens.shape, F32)]
    if last:
        out_shape += [jax.ShapeDtypeStruct((packed_rows, width), BF16)]
    else:
        out_shape += [jax.ShapeDtypeStruct(a.shape, F32) for a in (qw, proj, kvr, frw)]
    out_shape += [jax.ShapeDtypeStruct((8, width), F32)]
    old_in = [old[k] for k in (1, 2, 3, 4, 5)] if old else []
    hbm = pl.BlockSpec(memory_space=pl.ANY)
    cols_spec = pl.BlockSpec((1, SEQ, 8), lambda r: (micro, r, 0))
    in_specs = [
        part, part, cols_spec,
        whole(vec), whole(qw), whole(kvr), whole(proj), whole(frw),
        by_row(width), by_row(width), by_row(width), by_row(inner),
        pl.BlockSpec((1, 4, SEQ, SEQ), lambda r: (r, 0, 0, 0)),
        pl.BlockSpec((1, 4, SEQ, LANES), lambda r: (r, 0, 0, 0)),
        by_row(LANES), by_row(8), cols_spec,
        whole(near), whole(far), cols_spec,
    ] + [whole(o) for o in old_in] + [hbm] * (1 if old else 0)
    args = (
        tokens, grad, col, vec, qw, kvr, proj, frw, mid, n2, normed, mixed, probs, qs, kv, gates, slotcol, near, far, cols,
        *old_in, *(old[:1] if old else []),
    )
    return run_kernel(
        functools.partial(attention_backward_kernel, last, len(old_in) + (1 if old else 0)), args, in_specs,
        out_shape, [part] + [pl.BlockSpec(o.shape, lambda r: (0, 0)) for o in out_shape[1:]],
        [
            pltpu.VMEM((SEQ, width), F32),
            pltpu.VMEM(qw.shape, F32),
            pltpu.VMEM(proj.shape, F32),
            pltpu.VMEM(kvr.shape, F32),
            pltpu.VMEM(frw.shape, F32),
            pltpu.VMEM((8, width), F32),
        ],
        (steps,), "attention_backward",
        pl.CostEstimate(
            flops=2 * count * width * (4 * inner + 512 + 2 * near.shape[0]), bytes_accessed=24 << 20, transcendentals=0
        ),
        moving, cid, {25: 0} if old else None,
    )


def total_plan(n_expert, n_hidden, rows):
    ny = nx = n_hidden // 2
    nz = n_expert // nx
    unit = 16 * ny * nx * nz
    units = -(-rows // (2 * unit))
    first = (units + 1) // 2
    return (nz, nx, ny), (first * unit, (units - first) * unit)


def total_kernel(
    sizes, parts, pack_ref, small_ref, gq_ref, gproj_ref, gkvr_ref, gfr_ref, sum_ref,
    buf, done, core_in, land_a, land_b, small_got, small_part, small_got2, sems, small_sems,
):
    nz, nx, ny = sizes
    e, h = lax.axis_index("expert"), lax.axis_index("hidden")
    n_expert, n_hidden = nz * nx, ny * 2
    z, x = lax.div(e, nx), lax.rem(e, nx)
    y, c = lax.div(h, 2), lax.rem(h, 2)
    half = sum(parts)
    width = pack_ref.shape[1]
    mesh_id = pl.DeviceIdType.MESH
    barrier = pltpu.get_barrier_semaphore()
    for k in range(1, n_expert):
        pl.semaphore_signal(barrier, inc=1, device_id=(lax.rem(e + k, n_expert), h), device_id_type=mesh_id)
    for k in range(1, n_hidden):
        pl.semaphore_signal(barrier, inc=1, device_id=(e, lax.rem(h + k, n_hidden)), device_id_type=mesh_id)
    pl.semaphore_wait(barrier, n_expert + n_hidden - 2)

    counter = [0]

    def copy(source, target, device, pool=sems):
        i = counter[0] if pool is sems else counter[1]
        if pool is sems:
            counter[0] += 1
        else:
            counter[1] += 1
        return pltpu.make_async_remote_copy(
            source, target, pool.at[0, i], pool.at[1, i], device_id=device, device_id_type=mesh_id
        )

    counter.append(0)

    def rows_at(ref, start, count):
        return ref.at[pl.ds(pl.multiple_of(start, 16), count)]

    def add_rows(start, count, pieces):
        step = 112 if count % 112 == 0 else 64 if count % 64 == 0 else 16

        def body(i, carry):
            place = pl.ds(pl.multiple_of(start + i * step, 16), step)
            total = buf[place, :].astype(F32)
            for ref in pieces:
                total = total + ref[pl.ds(pl.multiple_of(i * step, 16), step), :].astype(F32)
            buf[place, :] = total.astype(BF16)
            return carry

        lax.fori_loop(0, count // step, body, 0)

    axes = {
        "y": (ny, y, lambda p: (e, p * 2 + c)),
        "x": (nx, x, lambda p: (z * nx + p, h)),
        "z": (nz, z, lambda p: (p * nx + x, h)),
    }
    orders = ("yxz", "xyz")
    lands = (land_a, land_b)
    starts = [c * half, c * half + parts[0]]
    spans = list(parts)
    todo = [i for i in range(2) if parts[i]]

    small = [
        copy(small_ref, small_got.at[e], (lax.rem(e + k, n_expert), h), small_sems) for k in range(1, n_expert)
    ]
    for m in small:
        m.start()
    swap = copy(rows_at(pack_ref, (1 - c) * half, half), core_in, (e, h + 1 - 2 * c))
    swap.start()
    small_got[e] = small_ref[...]
    buf[pl.ds(pl.multiple_of(c * half, 16), half), :] = pack_ref[pl.ds(pl.multiple_of(c * half, 16), half), :]
    swap.wait()
    add_rows(c * half, half, [core_in])
    trail = []
    offset = [0, 0]
    for stage in range(3):
        running = []
        for i in todo:
            size, me, device = axes[orders[i][stage]]
            chunk = spans[i] // size
            moves = []
            pieces = []
            for k in range(1, size):
                peer = lax.rem(me + k, size)
                piece = lands[i].at[pl.ds(offset[i], chunk)]
                offset[i] += chunk
                moves.append(copy(rows_at(buf, starts[i] + peer * chunk, chunk), piece, device(peer)))
                pieces.append(piece)
            for m in moves:
                m.start()
            running.append((i, size, me, device, chunk, moves, pieces))
        for i, size, me, device, chunk, moves, pieces in running:
            for m in moves:
                m.wait()
            trail.append((stage, i, starts[i], chunk, size, me, device))
            starts[i] = starts[i] + me * chunk
            spans[i] = chunk
            add_rows(starts[i], chunk, pieces)
        if stage == 0:
            for m in small:
                m.wait()
            small_part[...] = jnp.sum(small_got[...], axis=0)
            small = [
                copy(small_part, small_got2.at[h], (e, lax.rem(h + k, n_hidden)), small_sems) for k in range(1, n_hidden)
            ]
            for m in small:
                m.start()
            small_got2[h] = small_part[...]
    for i in todo:
        here = pl.ds(pl.multiple_of(starts[i], 16), spans[i])
        done[here, :] = buf[here, :]
    for stage in (2, 1, 0):
        moves = []
        for s, i, start, chunk, size, me, device in trail:
            if s == stage:
                place = rows_at(done, start + me * chunk, chunk)
                moves += [copy(place, place, device(lax.rem(me + k, size))) for k in range(1, size)]
        for m in moves:
            m.start()
        for m in moves:
            m.wait()
    place = rows_at(done, c * half, half)
    swap = copy(place, place, (e, h + 1 - 2 * c))
    swap.start()
    for m in small:
        m.wait()
    sum_ref[...] = jnp.sum(small_got2[...], axis=0)
    swap.wait()
    blocks = gq_ref.shape[1] // width

    def widen(target, lanes, base, count, span):
        def body(i, carry):
            here = pl.multiple_of(i * 64, 64)
            target[pl.ds(here, 64), lanes] = done[pl.ds(base + here, 64), span].astype(F32)
            return carry

        lax.fori_loop(0, count // 64, body, 0)

    for j in range(blocks):
        widen(gq_ref, slice(j * width, (j + 1) * width), j * width, width, slice(0, width))
    base = blocks * width
    widen(gproj_ref, slice(0, width), base, gproj_ref.shape[0], slice(0, width))
    base = base + gproj_ref.shape[0]
    wide = gkvr_ref.shape[1]
    widen(gkvr_ref, slice(0, wide), base, width, slice(0, wide))
    widen(gfr_ref, slice(0, LANES), base, width, slice(wide, wide + LANES))


def total_step(n_expert, n_hidden, rows, pack, small, qw, proj, kvr, frw):
    sizes, parts = total_plan(n_expert, n_hidden, rows)
    nz, nx, ny = sizes
    width = pack.shape[1]
    half = sum(parts)
    vmem = pl.BlockSpec(memory_space=pltpu.VMEM)
    lands = []
    for part, order in zip(parts, ((ny, nx, nz), (nx, ny, nz))):
        total = 0
        for size in order:
            part = part // size
            total += part * (size - 1)
        lands.append(pltpu.VMEM((max(total, 16), width), BF16))
    steps = 2 + 4 * ((ny - 1) + (nx - 1) + (nz - 1))
    return pl.pallas_call(
        functools.partial(total_kernel, sizes, parts),
        out_shape=tuple(jax.ShapeDtypeStruct(a.shape, F32) for a in (qw, proj, kvr, frw, small)),
        in_specs=[vmem] * 2,
        out_specs=[vmem] * 5,
        scratch_shapes=[
            pltpu.VMEM((2 * half, width), BF16),
            pltpu.VMEM((2 * half, width), BF16),
            pltpu.VMEM((half, width), BF16),
            *lands,
            pltpu.VMEM((n_expert,) + small.shape, F32),
            pltpu.VMEM(small.shape, F32),
            pltpu.VMEM((n_hidden,) + small.shape, F32),
            pltpu.SemaphoreType.DMA((2, steps)),
            pltpu.SemaphoreType.DMA((2, n_expert + n_hidden)),
        ],
        compiler_params=pltpu.CompilerParams(collective_id=8, has_side_effects=True, vmem_limit_bytes=VMEM_LIMIT),
        name="total_step",
    )(pack, small)


def move_only(moving, cid):
    return run_kernel(
        lambda *refs: None, (), [], (), [], (), (1,), "move_only",
        pl.CostEstimate(flops=0, bytes_accessed=4 << 20, transcendentals=0), moving, cid,
    )


def pad_lanes(a):
    return jnp.pad(a, ((0, 0), (0, LANES - a.shape[1])))


def per_device(
    tokens, grad_out, attn_routes, ffn_routes, segments, pad_mask, norm1_gain, norm1_bias, attn_router,
    query_w, key_w, value_w, attn_proj, norm2_gain, norm2_bias, ffn_router, expert_in, expert_out, halt_w, halt_b,
    *, n_expert, n_hidden,
):
    micros, count, width = tokens.shape
    experts = ffn_router.shape[1]
    capacity = 4 * count // experts
    slots = experts * capacity
    per = experts // n_expert
    group = n_expert // 2
    across = [(i, (i + group) % n_expert) for i in range(n_expert)]

    def gathered(a):
        return lax.all_gather(a, "hidden", axis=0, tiled=False)

    crossed = [lax.ppermute(a, "expert", across) for a in (expert_in, expert_out)]
    near_first, near_second = gathered(expert_in), gathered(expert_out)
    seg = segments.reshape(micros, count)
    zeros = jnp.zeros_like(seg)
    mine = lax.axis_index("expert") // group
    kind = (ffn_routes // (experts // 2) != mine).astype(jnp.int32)
    base = (kind * (experts // 2) + ffn_routes % (experts // 2)) * capacity
    col = jnp.concatenate([attn_routes, ffn_routes, seg[:, :, None], pad_mask[:, :, None]], axis=2)
    row = jnp.stack(
        [seg, pad_mask, ffn_routes[:, :, 0], ffn_routes[:, :, 1], base[:, :, 0], base[:, :, 1], zeros, zeros], axis=1
    )
    none = jnp.zeros_like(halt_w)
    vec = jnp.stack([norm1_gain, norm1_bias, norm2_gain, norm2_bias, halt_w, none, none, none])
    kvr = jnp.concatenate([key_w, value_w, pad_lanes(attn_router)], axis=1)
    frw = pad_lanes(ffn_router)
    hb = jnp.broadcast_to(halt_b.reshape(1, 1), (8, LANES))
    shape = (2, group, per, capacity, width)
    packed = query_w.size // width + attn_proj.shape[0] + width
    packed_rows = 2 * sum(total_plan(n_expert, n_hidden, packed)[1])

    slotrow, slotcol, gslots = route_step(row, grad_out, slots)
    weights = (vec, hb, query_w, kvr, attn_proj, frw)
    f0 = attention_forward(0, tokens, grad_out, col, row, slotrow, *weights, slots, (), None)
    crossed[0], n0_out = lax.optimization_barrier((crossed[0], f0[9]))
    far_first = gathered(crossed[0])
    *f1, n0 = attention_forward(1, tokens, grad_out, col, row, slotrow, *weights, slots, [n0_out.reshape(shape)], 2)
    crossed[1], n1_out = lax.optimization_barrier((crossed[1], f1[9]))
    far_second = gathered(crossed[1])
    (n1,) = move_only([n1_out.reshape(shape)], 3)
    rows = (n0, n1)
    y0, y1, g1 = expert_forward(0, rows, near_first, near_second, [gslots[1].reshape(shape)], 4)
    far0, far1, g0 = expert_forward(1, rows, far_first, far_second, [gslots[0].reshape(shape)], 1)
    grads = (g0, g1)
    scal = reading_step((y0, y1, far0, far1), grads, vec)
    cols, ab = scalar_step(scal, (f0[8], f1[8]), slotrow)
    gf_far, gs_far, bf0, bf1, r0, rf0 = expert_backward(1, rows, grads, ab, vec, far_first, far_second, [y0, far0], 5)
    gf_near, gs_near, bn0, bn1, qf0, qf1 = expert_backward(
        0, rows, grads, ab, vec, near_first, near_second, [bf0, bf1], 6
    )

    flat = lambda a: a.reshape(slots // 2, width)

    def reduced(a):
        return lax.psum_scatter(a, "hidden", scatter_dimension=0, tiled=False)

    far_grads = [lax.ppermute(reduced(a), "expert", across) for a in (gf_far, gs_far)]
    near_grads = [reduced(a) for a in (gf_near, gs_near)]
    *res0, qn0 = result_step(0, tokens, f0[0], flat(r0), flat(rf0), cols, slotcol, (), [bn0], 7)
    common = (tokens, grad_out, col, vec, query_w, kvr, attn_proj, frw)
    *out, qn1, r1 = attention_backward(
        0, False, packed_rows, *common, list(f0[:8]) + [slotcol], flat(qn0), flat(qf0), cols, (), [bn1, y1], 9
    )
    *out, rf1 = attention_backward(
        1, True, packed_rows, *common, list(f1[:8]) + [slotcol], flat(qn1), flat(qf1), cols, tuple(out), [far1], 10
    )
    res1 = result_step(1, tokens, f1[0], flat(r1), flat(rf1), cols, slotcol, tuple(res0[:1]), (), None)
    gfirst, gsecond = [a.astype(F32) + b.astype(F32) for a, b in zip(near_grads, far_grads)]
    small = jnp.concatenate([out[2], res0[1] + res1[1]], axis=0)
    gq, gproj, gkvr, gfr, small = total_step(
        n_expert, n_hidden, packed, out[1], small, query_w, attn_proj, kvr, frw
    )
    head = key_w.shape[1]
    return (
        res1[0],
        out[0],
        small[0],
        small[1],
        gkvr[:, LANES : LANES + attn_router.shape[1]],
        gq,
        gkvr[:, :head],
        gkvr[:, head : 2 * head],
        gproj,
        small[2],
        small[3],
        gfr[:, :experts],
        gfirst,
        gsecond,
        small[8],
        small[9, :1],
    )


def solution(mesh):
    rows = P(None, ("expert", "hidden"), None)
    in_specs = (rows,) * 5 + (P(None, ("expert", "hidden")),) + (P(),) * 10 + (
        P("expert", None, "hidden"), P("expert", "hidden", None), P(), P(),
    )
    out_specs = (rows,) * 2 + (P(),) * 10 + (P("expert", None, "hidden"), P("expert", "hidden", None), P(), P())
    return jax.shard_map(
        functools.partial(per_device, n_expert=mesh.shape["expert"], n_hidden=mesh.shape["hidden"]),
        mesh=mesh, in_specs=in_specs, out_specs=out_specs, check_vma=False,
    )
```

time: 785 us -> 546 us (0.70)
  waiting for transfers between devices: 343 us -> 8.17 us
  Pallas kernels: 344 us -> 466 us
  starting transfers between devices: 36.9 us -> 8.56 us
  local copies, waits for them, and re-layouts: 22.6 us -> 31.4 us
    all_to_all x8 -> x0, waiting for transfers between devices: 213 us -> none  [exchange(): return lax.all_to_all(a, 'expert', split_axis=0, concat_axis=0, tiled=True)]
    pallas_call x15, Pallas kernels: 344 us -> 466 us  [the longest x13 337 us: run_kernel(): pl.pallas_call(body, grid=grid, out_shape=tuple(out_shape) + tuple((jax.S...]
    reduce_scatter x2 -> x4, waiting for transfers between devices: 79.5 us -> 0.05 us  [reduced(): return lax.psum_scatter(a, 'hidden', scatter_dimension=0, tiled=False)]
    psum x1 -> x0, waiting for transfers between devices: 47.7 us -> none  [per_device(): lax.psum(tuple(out[1:5]), ('expert', 'hidden'))]
    all_to_all x8 -> x0, starting transfers between devices: 36.4 us -> none  [exchange(): return lax.all_to_all(a, 'expert', split_axis=0, concat_axis=0, tiled=True)]
    convert_element_type x4 -> x0, other arithmetic: 10.2 us -> none  [the longest x2 4.53 us: per_device(): a.astype(F32)]
    unnamed x52 -> x48, local copies, waits for them, and re-layouts: 12.7 us -> 15.8 us
  transfers between devices with their start and end apart: 13 -> 12, of which waited for: 9 -> 2; matrix products, arithmetic and copies ran while one was open for 3% -> 5% of each run, Pallas kernels for 40% -> 69%
where the time goes in v3:
time: 546 us; the launch traced here: 539 us
  Pallas kernels  466 us (85%)
  local copies, waits for them, and re-layouts  31.4 us (6%)
  between operations  15.4 us (3%)
  other arithmetic  9.32 us (2%)
  starting transfers between devices  8.56 us (2%)
  waiting for transfers between devices  8.17 us (1%)
    pallas_call x13, Pallas kernels, run_kernel(): pl.pallas_call(body, grid=grid, out_shape=tuple(out_shape) + tuple((jax.S...  337 us
    pallas_call x1, Pallas kernels, total_step(): pl.pallas_call(functools.partial(total_kernel, sizes, parts), out_shape=t...  106 us
    pallas_call x1, Pallas kernels, scalar_step(): pl.pallas_call(scalar_kernel, out_shape=(jax.ShapeDtypeStruct((2, tokens,...  23.4 us
    unnamed x48, local copies, waits for them, and re-layouts  15.8 us
  transfers between devices with their start and end apart: 12, of which 2 were waited for; matrix products, arithmetic and copies ran while one was open for 5% of the time, Pallas kernels for 69%

profile of v3, /device:TPU:0, one launch (start us, length us, event | category | flops | bytes accessed | tf_op | source)
XLA Modules:
  0.0 539.1 jit_solution(14968732219482352147)
XLA Ops:
  8.8 4.1 collective-permute-start
  15.9 1.6 pad.9.refs_10_.refs_7_
  18.1 1.4 stack.32.refs_0_.refs_3_
  19.5 1.4 stack.39.refs_5_.refs_8_.refs_3_
  21.8 1.3 pad_add_fusion.refs_2_
  23.1 8.3 %route_step.1 = (s32[2,8,512]{2,1,0:T(8,128)}, s32[2,512,8]{2,1,0:T(8,128)}, bf16[2,2048,512]{2,1,0:T(8,128)(2,1)}) custom-call(s32[2,8,512]{2,1,0:T(8,128)} %stack.32.refs_0_.refs_3_, bf16[2,512,512]{2,1,0:T(8,128)(2,1)} %refs_1_.9), custom_call_target="tpu_custom_call" | custom-call | flops 2147483648 | bytes 6291456 | tf_op jit(solution)/shard_map/route_step/pallas_call | solution.py:211
  32.0 21.5 %attention_forward.2 = (f32[512,512]{1,0:T(8,128)}, bf16[512,512]{1,0:T(8,128)(2,1)}, bf16[512,512]{1,0:T(8,128)(2,1)}, bf16[512,1536]{1,0:T(8,128)(2,1)}, bf16[...) custom-call(bf16[2,512,512]{2,1,0:T(8,128)(2,1)} %refs_0_.11, ...), custom_call_target="tpu_custom_call" | custom-call | flops 2818572288 | bytes 12582912 | tf_op jit(solution)/shard_map/attention_forward/pallas_call | solution.py:211
  53.5 5.2 collective-permute-done
  59.3 47.2 %attention_forward.3 = (f32[512,512]{1,0:T(8,128)}, bf16[512,512]{1,0:T(8,128)(2,1)}, bf16[512,512]{1,0:T(8,128)(2,1)}, bf16[512,1536]{1,0:T(8,128)(2,1)}, bf16[...) custom-call(bf16[2,512,512]{2,1,0:T(8,128)(2,1)} %refs_0_.11, ...), custom_call_target="tpu_custom_call" | custom-call | flops 2818572288 | bytes 12582912 | tf_op jit(solution)/shard_map/attention_forward/pallas_call | solution.py:211
  108.3 4.5 fusion.4
  112.8 30.5 %move_only.1.refs_1_ = bf16[2,4,2,128,512]{4,3,2,1,0:T(8,128)(2,1)} custom-call(bf16[2,4,2,128,512]{4,3,2,1,0:T(8,128)(2,1)} %bitcast.48), custom_call_target="tpu_custom_call" | custom-call | bytes 4194304 | tf_op jit(solution)/shard_map/move_only/pallas_call | solution.py:211
  143.3 29.0 %expert_forward.3 = (bf16[4,2,128,512]{3,2,1,0:T(8,128)(2,1)}, bf16[4,2,128,512]{3,2,1,0:T(8,128)(2,1)}, bf16[2,4,2,128,512]{4,3,2,1,0:T(8,128)(2,1)}) custom-call(bf16[2,4,2,128,512]{4,3,2,1,0:T(8,128)(2,1)} %get-tuple-element.99.refs_0_, bf16[2,4,2,128,512]{4,3,2,1,0:T(8,128)(2,1)} %move_only.1.refs_1_, bf16[4,2,512,512]{3,2,1,0:T(8,128)(2,1)} %bitcast.68, ...), custom_call_target="tpu_custom_call" | custom-call | flops 8589934592 | bytes 25165824 | tf_op jit(solution)/shard_map/expert_forward/pallas_call | solution.py:211
  172.4 28.1 %expert_forward.2 = (bf16[4,2,128,512]{3,2,1,0:T(8,128)(2,1)}, bf16[4,2,128,512]{3,2,1,0:T(8,128)(2,1)}, bf16[2,4,2,128,512]{4,3,2,1,0:T(8,128)(2,1)}) custom-call(bf16[2,4,2,128,512]{4,3,2,1,0:T(8,128)(2,1)} %get-tuple-element.99.refs_0_, bf16[2,4,2,128,512]{4,3,2,1,0:T(8,128)(2,1)} %move_only.1.refs_1_, bf16[4,2,512,512]{3,2,1,0:T(8,128)(2,1)} %bitcast.72, ...), custom_call_target="tpu_custom_call" | custom-call | flops 8589934592 | bytes 25165824 | tf_op jit(solution)/shard_map/expert_forward/pallas_call | solution.py:211
  200.5 6.8 %reading_step.1 = f32[4,2,2,2,8,128]{5,4,3,2,1,0:T(8,128)} custom-call(bf16[4,2,128,512]{3,2,1,0:T(8,128)(2,1)} %get-tuple-element.107.refs_0_.refs_8_, bf16[4,2,128,512]{3,2,1,0:T(8,128)(2,1)} %get-tuple-element.108.refs_1_.refs_21_, bf16[4,2,128,512]{3,2,1,0:T(8,128)(2,1)} %get-tuple-element.109.refs_2_.refs_9_, ...), custom_call_target="tpu_custom_call" | custom-call | flops 1000000000 | bytes 8388608 | tf_op jit(solution)/shard_map/reading_step/pallas_call | solution.py:211
  207.3 23.4 %scalar_step.1 = (f32[2,512,8]{2,1,0:T(8,128)}, f32[4,2,4,8,128]{4,3,2,1,0:T(8,128)}) custom-call(f32[4,2,4,8,128]{4,3,2,1,0:T(8,128)} %bitcast.56, f32[8,512]{1,0:T(8,128)} %get-tuple-element.111.rowsc0_ref, f32[8,512]{1,0:T(8,128)} %get-tuple-element.112.rowsc1_ref, s32[2,8,512]{2,1,0:T(8,128)} %get-tuple-element.86.refs_4_.slotrow_ref), custom_call_target="tpu_custom_call" | custom-call | flops 1000000000 | bytes 1048576 | tf_op jit(solution)/shard_map/scalar_step/pallas_call | solution.py:587
  230.7 37.6 %expert_backward.2 = (bf16[4,2,512,512]{3,2,1,0:T(8,128)(2,1)}, bf16[4,2,512,512]{3,2,1,0:T(8,128)(2,1)}, bf16[4,2,128,512]{3,2,1,0:T(8,128)(2,1)}, bf16[4,2,128...) custom-call(bf16[2,4,2,128,512]{4,3,2,1,0:T(8,128)(2,1)} %get-tuple-element.99.refs_0_, ...), custom_call_target="tpu_custom_call" | custom-call | flops 21474836480 | bytes 50331648 | tf_op jit(solution)/shard_map/expert_backward/pallas_call | solution.py:211
  268.9 37.6 %expert_backward.3 = (bf16[4,2,512,512]{3,2,1,0:T(8,128)(2,1)}, bf16[4,2,512,512]{3,2,1,0:T(8,128)(2,1)}, bf16[4,2,128,512]{3,2,1,0:T(8,128)(2,1)}, bf16[4,2,128...) custom-call(bf16[2,4,2,128,512]{4,3,2,1,0:T(8,128)(2,1)} %get-tuple-element.99.refs_0_, ...), custom_call_target="tpu_custom_call" | custom-call | flops 21474836480 | bytes 50331648 | tf_op jit(solution)/shard_map/expert_backward/pallas_call | solution.py:211
  307.3 14.5 %result_step.2 = (bf16[2,512,512]{2,1,0:T(8,128)(2,1)}, f32[8,512]{1,0:T(8,128)}, bf16[4,2,128,512]{3,2,1,0:T(8,128)(2,1)}) custom-call(bf16[2,512,512]{2,1,0:T(8,128)(2,1)} %refs_0_.11, f32[512,512]{1,0:T(8,128)} %get-tuple-element.90.refs_1_.refs_8_, bf16[1024,512]{1,0:T(8,128)(2,1)} %bitcast.81, bf16[1024,512]{1,0:T(8,128)(2,1)} %bitcast.82, ...), custom_call_target="tpu_custom_call" | custom-call | flops 2147483648 | bytes 5242880 | tf_op jit(solution)/shard_map/result_step/pallas_call | solution.py:211
  321.8 33.7 %attention_backward.2 = (f32[2,512,512]{2,1,0:T(8,128)}, f32[512,1536]{1,0:T(8,128)}, f32[1536,512]{1,0:T(8,128)}, f32[512,256]{1,0:T(8,128)}, f32[512,128]{1,0:...) custom-call(bf16[2,512,512]{2,1,0:T(8,128)(2,1)} %refs_0_.11, ...), custom_call_target="tpu_custom_call" | custom-call | flops 4563402752 | bytes 25165824 | tf_op jit(solution)/shard_map/attention_backward/pallas_call | solution.py:211
  355.6 3.0 collective-permute-start.3
  358.5 34.3 %attention_backward.3 = (f32[2,512,512]{2,1,0:T(8,128)}, bf16[3584,512]{1,0:T(8,128)(2,1)}, f32[8,512]{1,0:T(8,128)}, bf16[4,2,128,512]{3,2,1,0:T(8,128)(2,1)}) custom-call(bf16[2,512,512]{2,1,0:T(8,128)(2,1)} %refs_0_.11, bf16[2,512,512]{2,1,0:T(8,128)(2,1)} %refs_1_.9, s32[2,512,8]{2,1,0:T(8,128)} %pad_add_fusion.refs_2_, ...), custom_call_target="tpu_custom_call", output_to_operand_aliasing={{0}: (25, {})} | custom-call | flops 4563402752 | bytes 25165824 | tf_op jit(solution)/shard_map/attention_backward/pallas_call | solution.py:211
  392.9 7.8 %result_step.3 = (bf16[2,512,512]{2,1,0:T(8,128)(2,1)}, f32[8,512]{1,0:T(8,128)}) custom-call(bf16[2,512,512]{2,1,0:T(8,128)(2,1)} %refs_0_.11, f32[512,512]{1,0:T(8,128)} %get-tuple-element.89.refs_8_.refs_1_, bf16[1024,512]{1,0:T(8,128)(2,1)} %bitcast.78, bf16[1024,512]{1,0:T(8,128)(2,1)} %bitcast.79, ...), custom_call_target="tpu_custom_call", output_to_operand_aliasing={{0}: (6, {})} | custom-call | flops 2147483648 | bytes 5242880 | tf_op jit(solution)/shard_map/result_step/pallas_call | solution.py:211
  402.0 106.1 %total_step.1 = (f32[512,1536]{1,0:T(8,128)}, f32[1536,512]{1,0:T(8,128)}, f32[512,256]{1,0:T(8,128)}, f32[512,128]{1,0:T(8,128)}, f32[16,512]{1,0:T(8,128)}) custom-call(bf16[3584,512]{1,0:T(8,128)(2,1)} %get-tuple-element.143.pack_ref, f32[16,512]{1,0:T(8,128)} %pad_maximum_fusion.small_ref), custom_call_target="tpu_custom_call" | custom-call | tf_op jit(solution)/shard_map/total_step/pallas_call | solution.py:984
  509.4 1.7 copy.85
  515.4 1.5 fusion.6
  517.0 2.8 convert_add_fusion
  519.8 2.9 convert_add_fusion.1
  524.7 1.3 copy.94
  526.0 1.3 copy-done.2
  527.3 1.7 copy.95
  529.0 1.4 copy-done.1
  530.4 1.7 copy.96
  (87 shorter events, 18.7 us)
Async XLA Ops:
  7.2 1.6 copy-start.3
  7.2 5.7 %copy-start.11 = (s32[2,2,256]{2,1,0:T(2,128)S(1)}, s32[2,2,256]{2,1,0:T(2,128)}, u32[]{:S(2)}) copy-start(s32[2,2,256]{2,1,0:T(2,128)} %param.24) | copy-start | bytes 12292
  7.2 6.7 %copy-start.12 = (s32[2,512]{1,0:T(2,128)S(1)}, s32[2,512]{1,0:T(2,128)}, u32[]{:S(2)}) copy-start(s32[2,512]{1,0:T(2,128)} %param.25) | copy-start | bytes 12292
  7.2 6.8 %copy-start.10 = (bf16[512,24]{0,1:T(8,128)(2,1)S(1)}, bf16[512,24]{0,1:T(8,128)(2,1)}, u32[]{:S(2)}) copy-start(bf16[512,24]{0,1:T(8,128)(2,1)} %param.28) | copy-start | bytes 73732
  7.2 6.9 %copy-start.8 = (bf16[512,64]{0,1:T(8,128)(2,1)S(1)}, bf16[512,64]{0,1:T(8,128)(2,1)}, u32[]{:S(2)}) copy-start(bf16[512,64]{0,1:T(8,128)(2,1)} %param.30) | copy-start | bytes 196612
  7.2 7.0 %copy-start.9 = (bf16[512,64]{0,1:T(8,128)(2,1)S(1)}, bf16[512,64]{0,1:T(8,128)(2,1)}, u32[]{:S(2)}) copy-start(bf16[512,64]{0,1:T(8,128)(2,1)} %param.31) | copy-start | bytes 196612
  7.2 7.1 %copy-start.13 = (bf16[512,16]{0,1:T(8,128)(2,1)S(1)}, bf16[512,16]{0,1:T(8,128)(2,1)}, u32[]{:S(2)}) copy-start(bf16[512,16]{0,1:T(8,128)(2,1)} %param.35) | copy-start | bytes 49156
  7.3 7.9 %copy-start.14 = (s32[2,512,4]{1,2,0:T(4,128)S(1)}, s32[2,512,4]{1,2,0:T(4,128)}, u32[]{:S(2)}) copy-start(s32[2,512,4]{1,2,0:T(4,128)} %param.22) | copy-start | bytes 49156
  7.3 8.3 %copy-start.7 = (s32[2,512,2]{1,2,0:T(2,128)S(1)}, s32[2,512,2]{1,2,0:T(2,128)}, u32[]{:S(2)}) copy-start(s32[2,512,2]{1,2,0:T(2,128)} %param.23) | copy-start | bytes 24580
  7.3 136.0 %all-gather.13.cloned.1.call-start = ((), (), s32[]{:S(2)}) async-start(), calls=%async_computation.10 | async-start | bytes 5242880 | tf_op jit(solution)/shard_map/all_gather | solution.py:1030
  8.0 135.3 %all-gather.15.cloned.1.call-start = ((), (), s32[]{:S(2)}) async-start(), calls=%async_computation.11 | async-start | bytes 5242880 | tf_op jit(solution)/shard_map/all_gather | solution.py:1030
  8.8 163.6 %all-gather.9.cloned.1.call-start = ((), (), s32[]{:S(2)}) async-start(), calls=%async_computation.8 | async-start | bytes 5242880 | tf_op jit(solution)/shard_map/all_gather | solution.py:1030
  8.8 49.8 %collective-permute-start = (bf16[2,512,512]{2,1,0:T(8,128)(2,1)S(1)}, bf16[2,512,512]{2,1,0:T(8,128)(2,1)}, u32[]{:S(2)}, u32[]{:S(2)}) collective-permute-start(bf16[2,512,512]{2,1,0:T(8,128)(2,1)S(1)} %copy-done.3), channel_id=1, source_target_pairs={{0,16},{4,20},{8,24},{12,28},{16,0},{20,4},{24,8},{28,12},{1,17},{... | collective-permute-start | bytes 3145736 | tf_op jit(solution)/shard_map/ppermute | solution.py:1032
  32.0 27.2 %copy-start.4 = (bf16[2,512,512]{2,1,0:T(8,128)(2,1)S(1)}, bf16[2,512,512]{2,1,0:T(8,128)(2,1)}, u32[]{:S(2)}) copy-start(bf16[2,512,512]{2,1,0:T(8,128)(2,1)} %param.37) | copy-start | bytes 3145732
  58.7 113.7 %all-gather.11.cloned.1.call-start = ((), (), s32[]{:S(2)}) async-start(), calls=%async_computation.9 | async-start | bytes 5242880 | tf_op jit(solution)/shard_map/all_gather | solution.py:1030
  59.2 47.9 %collective-permute-start.1 = (bf16[2,512,512]{2,1,0:T(8,128)(2,1)S(1)}, bf16[2,512,512]{2,1,0:T(8,128)(2,1)S(1)}, u32[]{:S(2)}, u32[]{:S(2)}) collective-permute-start(bf16[2,512,512]{2,1,0:T(8,128)(2,1)S(1)} %copy-done.4), channel_id=1, source_target_pairs={{0,16},{4,20},{8,24},{12,28},{16,0},{20,4},{24,8},{28,12},{1,17},{... | collective-permute-start | bytes 3145736 | tf_op jit(solution)/shard_map/ppermute | solution.py:1032
  107.1 1.0 copy-start.6
  108.1 247.5 %reduce-scatter.11.cloned.1.call-start = ((), (), s32[]{:S(2)}) async-start(), calls=%async_computation.7 | async-start | bytes 5242880 | tf_op jit(solution)/shard_map/reduce_scatter | solution.py:1075
  268.3 124.5 %reduce-scatter.7.cloned.1.call-start = ((), (), s32[]{:S(2)}) async-start(), calls=%async_computation.5 | async-start | bytes 5242880 | tf_op jit(solution)/shard_map/reduce_scatter | solution.py:1075
  268.9 248.0 %reduce-scatter.9.cloned.1.call-start = ((), (), s32[]{:S(2)}) async-start(), calls=%async_computation.6 | async-start | bytes 5242880 | tf_op jit(solution)/shard_map/reduce_scatter | solution.py:1075
  306.5 213.3 %reduce-scatter.5.cloned.1.call-start = ((), (), s32[]{:S(2)}) async-start(), calls=%async_computation.4 | async-start | bytes 5242880 | tf_op jit(solution)/shard_map/reduce_scatter | solution.py:1075
  355.6 161.4 %collective-permute-start.3 = (bf16[2,512,512]{2,1,0:T(8,128)(2,1)}, bf16[2,512,512]{2,1,0:T(8,128)(2,1)S(1)}, u32[]{:S(2)}, u32[]{:S(2)}) collective-permute-start(bf16[2,512,512]{2,1,0:T(8,128)(2,1)} %bitcast.77), channel_id=1, source_target_pairs={{0,16},{4,20},{8,24},{12,28},{16,0},{20,4},{24,8},{28,12},{1,17},{... | collective-permute-start | bytes 3145736 | tf_op jit(solution)/shard_map/ppermute | solution.py:1077
  392.8 127.0 %collective-permute-start.2 = (bf16[2,512,512]{2,1,0:T(8,128)(2,1)}, bf16[2,512,512]{2,1,0:T(8,128)(2,1)S(1)}, u32[]{:S(2)}, u32[]{:S(2)}) collective-permute-start(bf16[2,512,512]{2,1,0:T(8,128)(2,1)} %bitcast.76), channel_id=1, source_target_pairs={{0,16},{4,20},{8,24},{12,28},{16,0},{20,4},{24,8},{28,12},{1,17},{... | collective-permute-start | bytes 3145736 | tf_op jit(solution)/shard_map/ppermute | solution.py:1077
  392.9 7.8 %copy-start.15 = (f32[8,512]{1,0:T(8,128)S(1)}, f32[8,512]{1,0:T(8,128)}, u32[]{:S(2)}) copy-start(f32[8,512]{1,0:T(8,128)} %get-tuple-element.145) | copy-start | bytes 49156
  392.9 8.5 %copy-start.16 = (f32[8,512]{1,0:T(8,128)S(1)}, f32[8,512]{1,0:T(8,128)}, u32[]{:S(2)}) copy-start(f32[8,512]{1,0:T(8,128)} %get-tuple-element.144) | copy-start | bytes 49156
  519.8 2.9 copy-start.5
  522.7 2.0 copy-start
  524.7 2.6 copy-start.2
  527.3 3.0 copy-start.1
Sparse Core Ops, SparseCore 0:
  9.7 37.1 all-gather.12
  48.4 34.6 all-gather.14
  84.7 34.3 all-gather.8
  121.1 34.4 all-gather.10
  268.4 45.0 reduce-scatter.10
  316.1 44.5 reduce-scatter.6
  363.2 44.4 reduce-scatter.8
  410.4 45.0 reduce-scatter.4

commit v4 on v3

--- a/solution.py
+++ b/solution.py
@@ -15,6 +15,7 @@
 GELU_C = math.sqrt(2.0 / math.pi)
 GELU_A = 0.044715
 VMEM_LIMIT = 60 * 1024 * 1024
+STREAMS = 4
 
 
 def mm(left, right):
@@ -222,35 +223,48 @@
     )(*args, *moving)
 
 
-def route_kernel(row_ref, grad_ref, slotrow_ref, slotcol_ref, out_ref):
-    tokens = grad_ref.shape[1]
+def route_kernel(row_ref, slotrow_ref, slotcol_ref):
+    tokens = row_ref.shape[2]
     before = lax.broadcasted_iota(jnp.int32, (tokens, tokens), 0)
     after = lax.broadcasted_iota(jnp.int32, (tokens, tokens), 1)
     upper = jnp.where(before < after, 1.0, 0.0).astype(BF16)
     sub = lax.broadcasted_iota(jnp.int32, (LANES, tokens), 0)
-    row = row_ref[0]
-    named = [jnp.where(sub == row[2 + i : 3 + i, :], 1.0, 0.0) for i in range(2)]
-    rank = mm((named[0] + named[1]).astype(BF16), upper)
-    slots = [fold_rows(named[i] * rank).astype(jnp.int32) + row[4 + i : 5 + i, :] for i in range(2)]
     sub8 = lax.broadcasted_iota(jnp.int32, (8, tokens), 0)
-    slotrow_ref[0] = jnp.where(sub8 == 0, slots[0], slots[1])
-    table = jnp.where(sub == 0, slots[0].astype(F32), slots[1].astype(F32))
-    slotcol_ref[0] = jnp.transpose(table)[:, :8].astype(jnp.int32)
-    dispatch(slots, [grad_ref.at[0]], out_ref.at[0])
-
-
-def route_step(row, grad, slots):
-    micros, count, width = grad.shape
+    for m in range(row_ref.shape[0]):
+        row = row_ref[m]
+        named = [jnp.where(sub == row[2 + i : 3 + i, :], 1.0, 0.0) for i in range(2)]
+        rank = mm((named[0] + named[1]).astype(BF16), upper)
+        slots = [fold_rows(named[i] * rank).astype(jnp.int32) + row[4 + i : 5 + i, :] for i in range(2)]
+        slotrow_ref[m] = jnp.where(sub8 == 0, slots[0], slots[1])
+        table = jnp.where(sub == 0, slots[0].astype(F32), slots[1].astype(F32))
+        slotcol_ref[m] = jnp.transpose(table)[:, :8].astype(jnp.int32)
+
+
+def route_step(row):
+    micros, _, count = row.shape
     out_shape = (
         jax.ShapeDtypeStruct((micros, 8, count), jnp.int32),
         jax.ShapeDtypeStruct((micros, count, 8), jnp.int32),
-        jax.ShapeDtypeStruct((micros, slots, width), BF16),
-    )
-    spec = lambda a, b: pl.BlockSpec((1, a, b), lambda m: (m, 0, 0))
+    )
+    whole = lambda s: pl.BlockSpec(s, lambda i: (0,) * len(s))
     return run_kernel(
-        route_kernel, (row, grad), [spec(8, count), spec(count, width)], out_shape,
-        [spec(8, count), spec(count, 8), spec(slots, width)], (), (micros,), "route_step",
-        pl.CostEstimate(flops=4 * count * width * slots, bytes_accessed=6 << 20, transcendentals=0),
+        route_kernel, (row,), [whole(row.shape)], out_shape, [whole(o.shape) for o in out_shape], (), (1,), "route_step",
+        pl.CostEstimate(flops=10**8, bytes_accessed=1 << 20, transcendentals=0),
+    )
+
+
+def spread_kernel(slotrow_ref, grad_ref, out0_ref, out1_ref):
+    for m, out_ref in enumerate((out0_ref, out1_ref)):
+        dispatch([slotrow_ref[m, 0:1, :], slotrow_ref[m, 1:2, :]], [grad_ref.at[m]], out_ref)
+
+
+def spread_step(slotrow, grad, slots, moving, cid):
+    width = grad.shape[2]
+    whole = lambda s: pl.BlockSpec(s, lambda i: (0,) * len(s))
+    return run_kernel(
+        spread_kernel, (slotrow, grad), [whole(slotrow.shape), whole(grad.shape)],
+        [jax.ShapeDtypeStruct((slots, width), BF16)] * 2, [whole((slots, width))] * 2, (), (1,), "spread_step",
+        pl.CostEstimate(flops=8 * slots * width * grad.shape[1], bytes_accessed=6 << 20, transcendentals=0), moving, cid,
     )
 
 
@@ -817,20 +831,21 @@
     nz = n_expert // nx
     unit = 16 * ny * nx * nz
     units = -(-rows // (2 * unit))
-    first = (units + 1) // 2
-    return (nz, nx, ny), (first * unit, (units - first) * unit)
+    count = min(units, STREAMS)
+    streams = tuple((units // count + (i < units % count)) * unit for i in range(count))
+    return (nz, nx, ny), streams
 
 
 def total_kernel(
-    sizes, parts, pack_ref, small_ref, gq_ref, gproj_ref, gkvr_ref, gfr_ref, sum_ref,
-    buf, done, core_in, land_a, land_b, small_got, small_part, small_got2, sems, small_sems,
+    sizes, streams, pack_ref, small_ref, gq_ref, gproj_ref, gkvr_ref, gfr_ref, sum_ref,
+    buf, done, core_in, land, small_got, small_part, small_got2, sems, small_sems,
 ):
     nz, nx, ny = sizes
     e, h = lax.axis_index("expert"), lax.axis_index("hidden")
     n_expert, n_hidden = nz * nx, ny * 2
     z, x = lax.div(e, nx), lax.rem(e, nx)
     y, c = lax.div(h, 2), lax.rem(h, 2)
-    half = sum(parts)
+    half = sum(streams)
     width = pack_ref.shape[1]
     mesh_id = pl.DeviceIdType.MESH
     barrier = pltpu.get_barrier_semaphore()
@@ -839,30 +854,24 @@
     for k in range(1, n_hidden):
         pl.semaphore_signal(barrier, inc=1, device_id=(e, lax.rem(h + k, n_hidden)), device_id_type=mesh_id)
     pl.semaphore_wait(barrier, n_expert + n_hidden - 2)
-
-    counter = [0]
+    used = {}
 
     def copy(source, target, device, pool=sems):
-        i = counter[0] if pool is sems else counter[1]
-        if pool is sems:
-            counter[0] += 1
-        else:
-            counter[1] += 1
+        i = used.get(id(pool), 0)
+        used[id(pool)] = i + 1
         return pltpu.make_async_remote_copy(
             source, target, pool.at[0, i], pool.at[1, i], device_id=device, device_id_type=mesh_id
         )
 
-    counter.append(0)
-
     def rows_at(ref, start, count):
         return ref.at[pl.ds(pl.multiple_of(start, 16), count)]
 
-    def add_rows(start, count, pieces):
-        step = 112 if count % 112 == 0 else 64 if count % 64 == 0 else 16
+    def add_rows(start, count, base, pieces):
+        step = 64 if count % 64 == 0 else 16
 
         def body(i, carry):
             place = pl.ds(pl.multiple_of(start + i * step, 16), step)
-            total = buf[place, :].astype(F32)
+            total = base[place, :].astype(F32)
             for ref in pieces:
                 total = total + ref[pl.ds(pl.multiple_of(i * step, 16), step), :].astype(F32)
             buf[place, :] = total.astype(BF16)
@@ -871,82 +880,89 @@
         lax.fori_loop(0, count // step, body, 0)
 
     axes = {
+        "c": (2, c, lambda p: (e, y * 2 + p)),
         "y": (ny, y, lambda p: (e, p * 2 + c)),
         "x": (nx, x, lambda p: (z * nx + p, h)),
         "z": (nz, z, lambda p: (p * nx + x, h)),
     }
-    orders = ("yxz", "xyz")
-    lands = (land_a, land_b)
-    starts = [c * half, c * half + parts[0]]
-    spans = list(parts)
-    todo = [i for i in range(2) if parts[i]]
-
-    small = [
-        copy(small_ref, small_got.at[e], (lax.rem(e + k, n_expert), h), small_sems) for k in range(1, n_expert)
-    ]
-    for m in small:
-        m.start()
-    swap = copy(rows_at(pack_ref, (1 - c) * half, half), core_in, (e, h + 1 - 2 * c))
-    swap.start()
-    small_got[e] = small_ref[...]
-    buf[pl.ds(pl.multiple_of(c * half, 16), half), :] = pack_ref[pl.ds(pl.multiple_of(c * half, 16), half), :]
-    swap.wait()
-    add_rows(c * half, half, [core_in])
-    trail = []
-    offset = [0, 0]
-    for stage in range(3):
-        running = []
-        for i in todo:
-            size, me, device = axes[orders[i][stage]]
-            chunk = spans[i] // size
-            moves = []
-            pieces = []
+    landed = [0]
+
+    def travel(first, count, order):
+        moves = [copy(rows_at(pack_ref, (1 - c) * half + first, count), rows_at(core_in, first, count), axes["c"][2](1 - c))]
+        for m in moves:
+            m.start()
+        yield
+        for m in moves:
+            m.wait()
+        start, span = c * half + first, count
+        add_rows(start, span, pack_ref, [core_in.at[pl.ds(first, count)]])
+        trail = []
+        for name in order:
+            size, me, device = axes[name]
+            chunk = span // size
+            moves, pieces = [], []
             for k in range(1, size):
                 peer = lax.rem(me + k, size)
-                piece = lands[i].at[pl.ds(offset[i], chunk)]
-                offset[i] += chunk
-                moves.append(copy(rows_at(buf, starts[i] + peer * chunk, chunk), piece, device(peer)))
-                pieces.append(piece)
+                pieces.append(land.at[pl.ds(landed[0], chunk)])
+                landed[0] += chunk
+                moves.append(copy(rows_at(buf, start + peer * chunk, chunk), pieces[-1], device(peer)))
             for m in moves:
                 m.start()
-            running.append((i, size, me, device, chunk, moves, pieces))
-        for i, size, me, device, chunk, moves, pieces in running:
+            yield
             for m in moves:
                 m.wait()
-            trail.append((stage, i, starts[i], chunk, size, me, device))
-            starts[i] = starts[i] + me * chunk
-            spans[i] = chunk
-            add_rows(starts[i], chunk, pieces)
-        if stage == 0:
-            for m in small:
+            start, span = start + me * chunk, chunk
+            trail.append((start, chunk, size, me, device))
+            add_rows(start, span, buf, pieces)
+        here = pl.ds(pl.multiple_of(start, 16), span)
+        done[here, :] = buf[here, :]
+        for begin, chunk, size, me, device in reversed(trail):
+            place = rows_at(done, begin, chunk)
+            moves = [copy(place, place, device(lax.rem(me + k, size))) for k in range(1, size)]
+            for m in moves:
+                m.start()
+            yield
+            for m in moves:
                 m.wait()
-            small_part[...] = jnp.sum(small_got[...], axis=0)
-            small = [
-                copy(small_part, small_got2.at[h], (e, lax.rem(h + k, n_hidden)), small_sems) for k in range(1, n_hidden)
-            ]
-            for m in small:
-                m.start()
-            small_got2[h] = small_part[...]
-    for i in todo:
-        here = pl.ds(pl.multiple_of(starts[i], 16), spans[i])
-        done[here, :] = buf[here, :]
-    for stage in (2, 1, 0):
-        moves = []
-        for s, i, start, chunk, size, me, device in trail:
-            if s == stage:
-                place = rows_at(done, start + me * chunk, chunk)
-                moves += [copy(place, place, device(lax.rem(me + k, size))) for k in range(1, size)]
+        place = rows_at(done, c * half + first, count)
+        moves = [copy(place, place, axes["c"][2](1 - c))]
         for m in moves:
             m.start()
+        yield
         for m in moves:
             m.wait()
-    place = rows_at(done, c * half, half)
-    swap = copy(place, place, (e, h + 1 - 2 * c))
-    swap.start()
-    for m in small:
-        m.wait()
-    sum_ref[...] = jnp.sum(small_got2[...], axis=0)
-    swap.wait()
+
+    def travel_small():
+        moves = [
+            copy(small_ref, small_got.at[e], (lax.rem(e + k, n_expert), h), small_sems) for k in range(1, n_expert)
+        ]
+        for m in moves:
+            m.start()
+        small_got[e] = small_ref[...]
+        yield
+        yield
+        for m in moves:
+            m.wait()
+        small_part[...] = jnp.sum(small_got[...], axis=0)
+        moves = [
+            copy(small_part, small_got2.at[h], (e, lax.rem(h + k, n_hidden)), small_sems) for k in range(1, n_hidden)
+        ]
+        for m in moves:
+            m.start()
+        small_got2[h] = small_part[...]
+        yield
+        yield
+        for m in moves:
+            m.wait()
+        sum_ref[...] = jnp.sum(small_got2[...], axis=0)
+
+    going, first = [], 0
+    for i, count in enumerate(streams):
+        going.append(travel(first, count, ("yxz", "xyz")[i % 2]))
+        first += count
+    going.append(travel_small())
+    while going:
+        going = [g for g in going if next(g, StopIteration) is not StopIteration]
     blocks = gq_ref.shape[1] // width
 
     def widen(target, lanes, base, count, span):
@@ -968,21 +984,19 @@
 
 
 def total_step(n_expert, n_hidden, rows, pack, small, qw, proj, kvr, frw):
-    sizes, parts = total_plan(n_expert, n_hidden, rows)
+    sizes, streams = total_plan(n_expert, n_hidden, rows)
     nz, nx, ny = sizes
     width = pack.shape[1]
-    half = sum(parts)
+    half = sum(streams)
     vmem = pl.BlockSpec(memory_space=pltpu.VMEM)
-    lands = []
-    for part, order in zip(parts, ((ny, nx, nz), (nx, ny, nz))):
-        total = 0
-        for size in order:
-            part = part // size
-            total += part * (size - 1)
-        lands.append(pltpu.VMEM((max(total, 16), width), BF16))
-    steps = 2 + 4 * ((ny - 1) + (nx - 1) + (nz - 1))
+    landing = 0
+    for i, span in enumerate(streams):
+        for size in ((ny, nx, nz), (nx, ny, nz))[i % 2]:
+            span = span // size
+            landing += span * (size - 1)
+    steps = len(streams) * (2 + 2 * ((ny - 1) + (nx - 1) + (nz - 1)))
     return pl.pallas_call(
-        functools.partial(total_kernel, sizes, parts),
+        functools.partial(total_kernel, sizes, streams),
         out_shape=tuple(jax.ShapeDtypeStruct(a.shape, F32) for a in (qw, proj, kvr, frw, small)),
         in_specs=[vmem] * 2,
         out_specs=[vmem] * 5,
@@ -990,7 +1004,7 @@
             pltpu.VMEM((2 * half, width), BF16),
             pltpu.VMEM((2 * half, width), BF16),
             pltpu.VMEM((half, width), BF16),
-            *lands,
+            pltpu.VMEM((landing, width), BF16),
             pltpu.VMEM((n_expert,) + small.shape, F32),
             pltpu.VMEM(small.shape, F32),
             pltpu.VMEM((n_hidden,) + small.shape, F32),
@@ -1000,13 +1014,6 @@
         compiler_params=pltpu.CompilerParams(collective_id=8, has_side_effects=True, vmem_limit_bytes=VMEM_LIMIT),
         name="total_step",
     )(pack, small)
-
-
-def move_only(moving, cid):
-    return run_kernel(
-        lambda *refs: None, (), [], (), [], (), (1,), "move_only",
-        pl.CostEstimate(flops=0, bytes_accessed=4 << 20, transcendentals=0), moving, cid,
-    )
 
 
 def pad_lanes(a):
@@ -1049,7 +1056,7 @@
     packed = query_w.size // width + attn_proj.shape[0] + width
     packed_rows = 2 * sum(total_plan(n_expert, n_hidden, packed)[1])
 
-    slotrow, slotcol, gslots = route_step(row, grad_out, slots)
+    slotrow, slotcol = route_step(row)
     weights = (vec, hb, query_w, kvr, attn_proj, frw)
     f0 = attention_forward(0, tokens, grad_out, col, row, slotrow, *weights, slots, (), None)
     crossed[0], n0_out = lax.optimization_barrier((crossed[0], f0[9]))
@@ -1057,16 +1064,18 @@
     *f1, n0 = attention_forward(1, tokens, grad_out, col, row, slotrow, *weights, slots, [n0_out.reshape(shape)], 2)
     crossed[1], n1_out = lax.optimization_barrier((crossed[1], f1[9]))
     far_second = gathered(crossed[1])
-    (n1,) = move_only([n1_out.reshape(shape)], 3)
+    gs0, gs1, n1 = spread_step(slotrow, grad_out, slots, [n1_out.reshape(shape)], 3)
     rows = (n0, n1)
-    y0, y1, g1 = expert_forward(0, rows, near_first, near_second, [gslots[1].reshape(shape)], 4)
-    far0, far1, g0 = expert_forward(1, rows, far_first, far_second, [gslots[0].reshape(shape)], 1)
+    y0, y1, g1 = expert_forward(0, rows, near_first, near_second, [gs1.reshape(shape)], 4)
+    far0, far1, g0 = expert_forward(1, rows, far_first, far_second, [gs0.reshape(shape)], 1)
     grads = (g0, g1)
     scal = reading_step((y0, y1, far0, far1), grads, vec)
     cols, ab = scalar_step(scal, (f0[8], f1[8]), slotrow)
-    gf_far, gs_far, bf0, bf1, r0, rf0 = expert_backward(1, rows, grads, ab, vec, far_first, far_second, [y0, far0], 5)
-    gf_near, gs_near, bn0, bn1, qf0, qf1 = expert_backward(
-        0, rows, grads, ab, vec, near_first, near_second, [bf0, bf1], 6
+    gf_far, gs_far, bf0, bf1, r0, rf0, r1 = expert_backward(
+        1, rows, grads, ab, vec, far_first, far_second, [y0, far0, y1], 9
+    )
+    gf_near, gs_near, bn0, bn1, qf0, qf1, rf1 = expert_backward(
+        0, rows, grads, ab, vec, near_first, near_second, [bf0, bf1, far1], 10
     )
 
     flat = lambda a: a.reshape(slots // 2, width)
@@ -1074,21 +1083,26 @@
     def reduced(a):
         return lax.psum_scatter(a, "hidden", scatter_dimension=0, tiled=False)
 
-    far_grads = [lax.ppermute(reduced(a), "expert", across) for a in (gf_far, gs_far)]
+    far_grads = [reduced(a) for a in (gf_far, gs_far)]
     near_grads = [reduced(a) for a in (gf_near, gs_near)]
-    *res0, qn0 = result_step(0, tokens, f0[0], flat(r0), flat(rf0), cols, slotcol, (), [bn0], 7)
+    *res0, qn0, qn1 = result_step(0, tokens, f0[0], flat(r0), flat(rf0), cols, slotcol, (), [bn0, bn1], 11)
     common = (tokens, grad_out, col, vec, query_w, kvr, attn_proj, frw)
-    *out, qn1, r1 = attention_backward(
-        0, False, packed_rows, *common, list(f0[:8]) + [slotcol], flat(qn0), flat(qf0), cols, (), [bn1, y1], 9
-    )
-    *out, rf1 = attention_backward(
-        1, True, packed_rows, *common, list(f1[:8]) + [slotcol], flat(qn1), flat(qf1), cols, tuple(out), [far1], 10
+    far_grads[0], qn0 = lax.optimization_barrier((far_grads[0], qn0))
+    far_grads[0] = lax.ppermute(far_grads[0], "expert", across)
+    out = attention_backward(
+        0, False, packed_rows, *common, list(f0[:8]) + [slotcol], flat(qn0), flat(qf0), cols, (), (), None
     )
     res1 = result_step(1, tokens, f1[0], flat(r1), flat(rf1), cols, slotcol, tuple(res0[:1]), (), None)
+    out, far_grads, res1 = lax.optimization_barrier((tuple(out), far_grads, tuple(res1)))
+    far_grads[1] = lax.ppermute(far_grads[1], "expert", across)
+    out = attention_backward(
+        1, True, packed_rows, *common, list(f1[:8]) + [slotcol], flat(qn1), flat(qf1), cols, tuple(out), (), None
+    )
+    packs = out[1]
     gfirst, gsecond = [a.astype(F32) + b.astype(F32) for a, b in zip(near_grads, far_grads)]
     small = jnp.concatenate([out[2], res0[1] + res1[1]], axis=0)
     gq, gproj, gkvr, gfr, small = total_step(
-        n_expert, n_hidden, packed, out[1], small, query_w, attn_proj, kvr, frw
+        n_expert, n_hidden, packed, packs, small, query_w, attn_proj, kvr, frw
     )
     head = key_w.shape[1]
     return (

time: 546 us -> 527 us (0.965)
  Pallas kernels: 466 us -> 441 us
  waiting for transfers between devices: 8.17 us -> 19.9 us
  local copies, waits for them, and re-layouts: 31.4 us -> 25.2 us
    pallas_call x1, Pallas kernels: 106 us -> 73.9 us  [total_step(): pl.pallas_call(functools.partial(total_kernel, sizes, streams), out_shape...]
    ppermute x2, waiting for transfers between devices: 0.01 us -> 7.89 us  [the longest x1 7.89 us: per_device(): far_grads[0] = lax.ppermute(far_grads[0], 'expert', across)]
    pallas_call x13, Pallas kernels: 337 us -> 344 us  [run_kernel(): pl.pallas_call(body, grid=grid, out_shape=tuple(out_shape) + tuple((jax.S...]
    unnamed x48 -> x43, local copies, waits for them, and re-layouts: 15.8 us -> 12.8 us
  transfers between devices with their start and end apart: 12 -> 12, of which waited for: 2 -> 3; matrix products, arithmetic and copies ran while one was open for 5% -> 5% of each run, Pallas kernels for 69% -> 66%
where the time goes in v4:
time: 527 us; the launch traced here: 520 us
  Pallas kernels  441 us (84%)
  local copies, waits for them, and re-layouts  25.2 us (5%)
  waiting for transfers between devices  19.9 us (4%)
  between operations  15.3 us (3%)
  other arithmetic  9.36 us (2%)
  starting transfers between devices  8.56 us (2%)
    pallas_call x13, Pallas kernels, run_kernel(): pl.pallas_call(body, grid=grid, out_shape=tuple(out_shape) + tuple((jax.S...  344 us
    pallas_call x1, Pallas kernels, total_step(): pl.pallas_call(functools.partial(total_kernel, sizes, streams), out_shape...  73.9 us
    pallas_call x1, Pallas kernels, scalar_step(): pl.pallas_call(scalar_kernel, out_shape=(jax.ShapeDtypeStruct((2, tokens,...  23.4 us
    unnamed x43, local copies, waits for them, and re-layouts  12.8 us
  transfers between devices with their start and end apart: 12, of which 3 were waited for; matrix products, arithmetic and copies ran while one was open for 5% of the time, Pallas kernels for 66%

profile of v4, /device:TPU:0, one launch (start us, length us, event | category | flops | bytes accessed | tf_op | source)
XLA Modules:
  0.0 519.7 jit_solution(7007346397138932130)
XLA Ops:
  8.8 4.1 collective-permute-start
  15.2 1.5 copy.81
  17.4 1.6 pad.9.refs_10_.refs_7_
  20.2 1.5 stack.36.refs_5_.refs_8_.refs_3_
  22.3 1.4 stack.39.refs_0_.refs_3_
  23.7 2.0 route_step.1
  26.6 1.3 pad_add_fusion.refs_2_
  28.4 21.5 %attention_forward.2 = (f32[512,512]{1,0:T(8,128)}, bf16[512,512]{1,0:T(8,128)(2,1)}, bf16[512,512]{1,0:T(8,128)(2,1)}, bf16[512,1536]{1,0:T(8,128)(2,1)}, bf16[...) custom-call(bf16[2,512,512]{2,1,0:T(8,128)(2,1)} %refs_0_.11, ...), custom_call_target="tpu_custom_call" | custom-call | flops 2818572288 | bytes 12582912 | tf_op jit(solution)/shard_map/attention_forward/pallas_call | solution.py:212
  50.0 8.7 %collective-permute-done = bf16[2,512,512]{2,1,0:T(8,128)(2,1)} collective-permute-done((bf16[2,512,512]{2,1,0:T(8,128)(2,1)S(1)}, bf16[2,512,512]{2,1,0:T(8,128)(2,1)}, u32[]{:S(2)}, u32[]{:S(2)}) %collective-permute-start) | collective-permute-done | bytes 1048608 | tf_op jit(solution)/shard_map/ppermute | solution.py:1039
  59.3 47.3 %attention_forward.3 = (f32[512,512]{1,0:T(8,128)}, bf16[512,512]{1,0:T(8,128)(2,1)}, bf16[512,512]{1,0:T(8,128)(2,1)}, bf16[512,1536]{1,0:T(8,128)(2,1)}, bf16[...) custom-call(bf16[2,512,512]{2,1,0:T(8,128)(2,1)} %refs_0_.11, ...), custom_call_target="tpu_custom_call" | custom-call | flops 2818572288 | bytes 12582912 | tf_op jit(solution)/shard_map/attention_forward/pallas_call | solution.py:212
  108.3 33.9 %spread_step.1 = (bf16[2048,512]{1,0:T(8,128)(2,1)}, bf16[2048,512]{1,0:T(8,128)(2,1)}, bf16[2,4,2,128,512]{4,3,2,1,0:T(8,128)(2,1)}) custom-call(s32[2,8,512]{2,1,0:T(8,128)} %get-tuple-element.100.refs_4_.refs_0_.slotrow_ref, bf16[2,512,512]{2,1,0:T(8,128)(2,1)} %refs_1_.9, bf16[2,4,2,128,512]{4,3,2,1,0:T(8,128)(2,1)} %bitcast.74), custom_call_target="tpu_custom_call" | custom-call | flops 4294967296 | bytes 6291456 | tf_op jit(solution)/shard_map/spread_step/pallas_call | solution.py:212
  142.2 28.9 %expert_forward.3 = (bf16[4,2,128,512]{3,2,1,0:T(8,128)(2,1)}, bf16[4,2,128,512]{3,2,1,0:T(8,128)(2,1)}, bf16[2,4,2,128,512]{4,3,2,1,0:T(8,128)(2,1)}) custom-call(bf16[2,4,2,128,512]{4,3,2,1,0:T(8,128)(2,1)} %get-tuple-element.112.refs_0_, bf16[2,4,2,128,512]{4,3,2,1,0:T(8,128)(2,1)} %get-tuple-element.115.refs_1_, bf16[4,2,512,512]{3,2,1,0:T(8,128)(2,1)} %bitcast.63, ...), custom_call_target="tpu_custom_call" | custom-call | flops 8589934592 | bytes 25165824 | tf_op jit(solution)/shard_map/expert_forward/pallas_call | solution.py:212
  171.3 28.1 %expert_forward.2 = (bf16[4,2,128,512]{3,2,1,0:T(8,128)(2,1)}, bf16[4,2,128,512]{3,2,1,0:T(8,128)(2,1)}, bf16[2,4,2,128,512]{4,3,2,1,0:T(8,128)(2,1)}) custom-call(bf16[2,4,2,128,512]{4,3,2,1,0:T(8,128)(2,1)} %get-tuple-element.112.refs_0_, bf16[2,4,2,128,512]{4,3,2,1,0:T(8,128)(2,1)} %get-tuple-element.115.refs_1_, bf16[4,2,512,512]{3,2,1,0:T(8,128)(2,1)} %bitcast.67, ...), custom_call_target="tpu_custom_call" | custom-call | flops 8589934592 | bytes 25165824 | tf_op jit(solution)/shard_map/expert_forward/pallas_call | solution.py:212
  199.3 6.8 %reading_step.1 = f32[4,2,2,2,8,128]{5,4,3,2,1,0:T(8,128)} custom-call(bf16[4,2,128,512]{3,2,1,0:T(8,128)(2,1)} %get-tuple-element.122.refs_0_.refs_8_, bf16[4,2,128,512]{3,2,1,0:T(8,128)(2,1)} %get-tuple-element.123.refs_1_.refs_10_, bf16[4,2,128,512]{3,2,1,0:T(8,128)(2,1)} %get-tuple-element.124.refs_2_.refs_9_, ...), custom_call_target="tpu_custom_call" | custom-call | flops 1000000000 | bytes 8388608 | tf_op jit(solution)/shard_map/reading_step/pallas_call | solution.py:212
  206.1 23.4 %scalar_step.1 = (f32[2,512,8]{2,1,0:T(8,128)}, f32[4,2,4,8,128]{4,3,2,1,0:T(8,128)}) custom-call(f32[4,2,4,8,128]{4,3,2,1,0:T(8,128)} %bitcast.51, f32[8,512]{1,0:T(8,128)} %get-tuple-element.126.rowsc0_ref, f32[8,512]{1,0:T(8,128)} %get-tuple-element.127.rowsc1_ref, s32[2,8,512]{2,1,0:T(8,128)} %get-tuple-element.100.refs_4_.refs_0_.slotrow_ref), custom_call_target="tpu_custom_call" | custom-call | flops 1000000000 | bytes 1048576 | tf_op jit(solution)/shard_map/scalar_step/pallas_call | solution.py:601
  229.6 38.0 %expert_backward.2 = (bf16[4,2,512,512]{3,2,1,0:T(8,128)(2,1)}, bf16[4,2,512,512]{3,2,1,0:T(8,128)(2,1)}, bf16[4,2,128,512]{3,2,1,0:T(8,128)(2,1)}, bf16[4,2,128...) custom-call(bf16[2,4,2,128,512]{4,3,2,1,0:T(8,128)(2,1)} %get-tuple-, ...), custom_call_target="tpu_custom_call" | custom-call | flops 21474836480 | bytes 50331648 | tf_op jit(solution)/shard_map/expert_backward/pallas_call | solution.py:212
  268.4 40.1 %expert_backward.3 = (bf16[4,2,512,512]{3,2,1,0:T(8,128)(2,1)}, bf16[4,2,512,512]{3,2,1,0:T(8,128)(2,1)}, bf16[4,2,128,512]{3,2,1,0:T(8,128)(2,1)}, bf16[4,2,128...) custom-call(bf16[2,4,2,128,512]{4,3,2,1,0:T(8,128)(2,1)} %get-tuple-, ...), custom_call_target="tpu_custom_call" | custom-call | flops 21474836480 | bytes 50331648 | tf_op jit(solution)/shard_map/expert_backward/pallas_call | solution.py:212
  309.3 28.4 %result_step.2 = (bf16[2,512,512]{2,1,0:T(8,128)(2,1)}, f32[8,512]{1,0:T(8,128)}, bf16[4,2,128,512]{3,2,1,0:T(8,128)(2,1)}, bf16[4,2,128,512]{3,2,1,0:T(8,128)(2,1)}) custom-call(bf16[2,512,512]{2,1,0:T(8,128)(2,1)} %refs_0_.11, f32[512,512]{1,0:T(8,128)} %get-tuple-element.101.refs_1_.refs_8_, bf16[1024,512]{1,0:T(8,128)(2,1)} %bitcast.79, ...), custom_call_target="tpu_custom_call" | custom-call | flops 2147483648 | bytes 5242880 | tf_op jit(solution)/shard_map/result_step/pallas_call | solution.py:212
  337.7 3.2 collective-permute-start.2
  340.9 7.7 %result_step.3 = (bf16[2,512,512]{2,1,0:T(8,128)(2,1)}, f32[8,512]{1,0:T(8,128)}) custom-call(bf16[2,512,512]{2,1,0:T(8,128)(2,1)} %refs_0_.11, f32[512,512]{1,0:T(8,128)} %get-tuple-element.148.refs_1_.refs_8_, bf16[1024,512]{1,0:T(8,128)(2,1)} %bitcast.77, bf16[1024,512]{1,0:T(8,128)(2,1)} %bitcast.81, ...), custom_call_target="tpu_custom_call", output_to_operand_aliasing={{0}: (6, {})} | custom-call | flops 2147483648 | bytes 5242880 | tf_op jit(solution)/shard_map/result_step/pallas_call | solution.py:212
  348.6 30.4 %attention_backward.2 = (f32[2,512,512]{2,1,0:T(8,128)}, f32[512,1536]{1,0:T(8,128)}, f32[1536,512]{1,0:T(8,128)}, f32[512,256]{1,0:T(8,128)}, f32[512,128]{1,0:T(8,128)}, /*index=5*/f32[8,512]{1,0:T(8,128)}) custom-call(bf16[2,512,512]{2,1,0:T(8,128)(2,1)} %refs_0_.11, bf16[2,512,512]{2,1,0:T(8,128)(2,1)} %refs_1_.9, s32[2,512,8]{2,1,0:T(8,128)} %pad_add_fusion.refs_2_, ...), custom_call_target="tpu_custom_call" | custom-call | flops 4563402752 | bytes 25165824 | tf_op jit(solution)/shard_map/attention_backward/pallas_call | solution.py:212
  379.1 7.9 %collective-permute-done.2 = bf16[2,512,512]{2,1,0:T(8,128)(2,1)S(1)} collective-permute-done((bf16[2,512,512]{2,1,0:T(8,128)(2,1)}, bf16[2,512,512]{2,1,0:T(8,128)(2,1)S(1)}, u32[]{:S(2)}, u32[]{:S(2)}) %collective-permute-start.2) | collective-permute-done | bytes 1048608 | tf_op jit(solution)/shard_map/ppermute | solution.py:1091
  386.9 31.0 %attention_backward.3 = (f32[2,512,512]{2,1,0:T(8,128)}, bf16[3584,512]{1,0:T(8,128)(2,1)}, f32[8,512]{1,0:T(8,128)}) custom-call(bf16[2,512,512]{2,1,0:T(8,128)(2,1)} %refs_0_.11, bf16[2,512,512]{2,1,0:T(8,128)(2,1)} %refs_1_.9, s32[2,512,8]{2,1,0:T(8,128)} %pad_add_fusion.refs_2_, ...), custom_call_target="tpu_custom_call", output_to_operand_aliasing={{0}: (25, {})} | custom-call | flops 4563402752 | bytes 25165824 | tf_op jit(solution)/shard_map/attention_backward/pallas_call | solution.py:212
  418.0 1.3 pad_maximum_fusion.small_ref
  419.3 73.9 %total_step.1 = (f32[512,1536]{1,0:T(8,128)}, f32[1536,512]{1,0:T(8,128)}, f32[512,256]{1,0:T(8,128)}, f32[512,128]{1,0:T(8,128)}, f32[16,512]{1,0:T(8,128)}) custom-call(bf16[3584,512]{1,0:T(8,128)(2,1)} %get-tuple-element.171.pack_ref, f32[16,512]{1,0:T(8,128)} %pad_maximum_fusion.small_ref), custom_call_target="tpu_custom_call" | custom-call | tf_op jit(solution)/shard_map/total_step/pallas_call | solution.py:998
  495.0 1.3 fusion.4
  499.7 1.5 fusion.5
  501.2 2.8 convert_add_fusion.1
  504.0 3.0 convert_add_fusion
  508.0 1.7 copy.93
  509.7 1.4 copy-done
  511.0 1.7 copy.94
  (81 shorter events, 17.3 us)
Async XLA Ops:
  7.2 1.6 copy-start.2
  7.2 5.7 %copy-start.10 = (s32[2,2,256]{2,1,0:T(2,128)S(1)}, s32[2,2,256]{2,1,0:T(2,128)}, u32[]{:S(2)}) copy-start(s32[2,2,256]{2,1,0:T(2,128)} %param.24) | copy-start | bytes 12292
  7.2 6.1 %copy-start.11 = (s32[2,512]{1,0:T(2,128)S(1)}, s32[2,512]{1,0:T(2,128)}, u32[]{:S(2)}) copy-start(s32[2,512]{1,0:T(2,128)} %param.25) | copy-start | bytes 12292
  7.2 6.3 %copy-start.7 = (s32[2,512,2]{1,2,0:T(2,128)S(1)}, s32[2,512,2]{1,2,0:T(2,128)}, u32[]{:S(2)}) copy-start(s32[2,512,2]{1,2,0:T(2,128)} %param.23) | copy-start | bytes 24580
  7.2 6.5 %copy-start.12 = (s32[2,512,4]{1,2,0:T(4,128)S(1)}, s32[2,512,4]{1,2,0:T(4,128)}, u32[]{:S(2)}) copy-start(s32[2,512,4]{1,2,0:T(4,128)} %param.22) | copy-start | bytes 49156
  7.2 6.8 %copy-start.9 = (bf16[512,24]{0,1:T(8,128)(2,1)S(1)}, bf16[512,24]{0,1:T(8,128)(2,1)}, u32[]{:S(2)}) copy-start(bf16[512,24]{0,1:T(8,128)(2,1)} %param.28) | copy-start | bytes 73732
  7.2 6.9 %copy-start.8 = (bf16[512,64]{0,1:T(8,128)(2,1)S(1)}, bf16[512,64]{0,1:T(8,128)(2,1)}, u32[]{:S(2)}) copy-start(bf16[512,64]{0,1:T(8,128)(2,1)} %param.31) | copy-start | bytes 196612
  7.3 135.0 %all-gather.13.cloned.1.call-start = ((), (), s32[]{:S(2)}) async-start(), calls=%async_computation.10 | async-start | bytes 5242880 | tf_op jit(solution)/shard_map/all_gather | solution.py:1037
  8.0 134.3 %all-gather.15.cloned.1.call-start = ((), (), s32[]{:S(2)}) async-start(), calls=%async_computation.11 | async-start | bytes 5242880 | tf_op jit(solution)/shard_map/all_gather | solution.py:1037
  8.7 162.5 %all-gather.9.cloned.1.call-start = ((), (), s32[]{:S(2)}) async-start(), calls=%async_computation.8 | async-start | bytes 5242880 | tf_op jit(solution)/shard_map/all_gather | solution.py:1037
  8.8 49.8 %collective-permute-start = (bf16[2,512,512]{2,1,0:T(8,128)(2,1)S(1)}, bf16[2,512,512]{2,1,0:T(8,128)(2,1)}, u32[]{:S(2)}, u32[]{:S(2)}) collective-permute-start(bf16[2,512,512]{2,1,0:T(8,128)(2,1)S(1)} %copy-done.2), channel_id=1, source_target_pairs={{0,16},{4,20},{8,24},{12,28},{16,0},{20,4},{24,8},{28,12},{1,17},{... | collective-permute-start | bytes 3145736 | tf_op jit(solution)/shard_map/ppermute | solution.py:1039
  28.4 30.7 %copy-start.3 = (bf16[2,512,512]{2,1,0:T(8,128)(2,1)S(1)}, bf16[2,512,512]{2,1,0:T(8,128)(2,1)}, u32[]{:S(2)}) copy-start(bf16[2,512,512]{2,1,0:T(8,128)(2,1)} %param.37) | copy-start | bytes 3145732
  58.7 112.6 %all-gather.11.cloned.1.call-start = ((), (), s32[]{:S(2)}) async-start(), calls=%async_computation.9 | async-start | bytes 5242880 | tf_op jit(solution)/shard_map/all_gather | solution.py:1037
  59.2 47.9 %collective-permute-start.1 = (bf16[2,512,512]{2,1,0:T(8,128)(2,1)S(1)}, bf16[2,512,512]{2,1,0:T(8,128)(2,1)S(1)}, u32[]{:S(2)}, u32[]{:S(2)}) collective-permute-start(bf16[2,512,512]{2,1,0:T(8,128)(2,1)S(1)} %copy-done.3), channel_id=1, source_target_pairs={{0,16},{4,20},{8,24},{12,28},{16,0},{20,4},{24,8},{28,12},{1,17},{... | collective-permute-start | bytes 3145736 | tf_op jit(solution)/shard_map/ppermute | solution.py:1039
  107.1 1.0 copy-start.4
  108.1 229.6 %reduce-scatter.5.cloned.1.call-start = ((), (), s32[]{:S(2)}) async-start(), calls=%async_computation.4 | async-start | bytes 5242880 | tf_op jit(solution)/shard_map/reduce_scatter | solution.py:1084
  267.6 111.5 %reduce-scatter.7.cloned.1.call-start = ((), (), s32[]{:S(2)}) async-start(), calls=%async_computation.5 | async-start | bytes 5242880 | tf_op jit(solution)/shard_map/reduce_scatter | solution.py:1084
  268.1 233.0 %reduce-scatter.9.cloned.1.call-start = ((), (), s32[]{:S(2)}) async-start(), calls=%async_computation.6 | async-start | bytes 5242880 | tf_op jit(solution)/shard_map/reduce_scatter | solution.py:1084
  308.5 195.5 %reduce-scatter.11.cloned.1.call-start = ((), (), s32[]{:S(2)}) async-start(), calls=%async_computation.7 | async-start | bytes 5242880 | tf_op jit(solution)/shard_map/reduce_scatter | solution.py:1084
  337.7 49.2 %collective-permute-start.2 = (bf16[2,512,512]{2,1,0:T(8,128)(2,1)}, bf16[2,512,512]{2,1,0:T(8,128)(2,1)S(1)}, u32[]{:S(2)}, u32[]{:S(2)}) collective-permute-start(bf16[2,512,512]{2,1,0:T(8,128)(2,1)} %bitcast.72), channel_id=1, source_target_pairs={{0,16},{4,20},{8,24},{12,28},{16,0},{20,4},{24,8},{28,12},{1,17},{... | collective-permute-start | bytes 3145736 | tf_op jit(solution)/shard_map/ppermute | solution.py:1091
  386.9 117.1 %collective-permute-start.3 = (bf16[2,512,512]{2,1,0:T(8,128)(2,1)}, bf16[2,512,512]{2,1,0:T(8,128)(2,1)S(1)}, u32[]{:S(2)}, u32[]{:S(2)}) collective-permute-start(bf16[2,512,512]{2,1,0:T(8,128)(2,1)} %bitcast.71), channel_id=1, source_target_pairs={{0,16},{4,20},{8,24},{12,28},{16,0},{20,4},{24,8},{28,12},{1,17},{... | collective-permute-start | bytes 3145736 | tf_op jit(solution)/shard_map/ppermute | solution.py:1097
  386.9 31.0 %copy-start.13 = (f32[8,512]{1,0:T(8,128)S(1)}, f32[8,512]{1,0:T(8,128)}, u32[]{:S(2)}) copy-start(f32[8,512]{1,0:T(8,128)} %get-tuple-element.173) | copy-start | bytes 49156
  386.9 31.0 %copy-start.14 = (f32[8,512]{1,0:T(8,128)S(1)}, f32[8,512]{1,0:T(8,128)}, u32[]{:S(2)}) copy-start(f32[8,512]{1,0:T(8,128)} %get-tuple-element.174) | copy-start | bytes 49156
  493.2 4.6 copy-start.6
  504.0 3.0 copy-start.5
  504.0 4.0 copy-start.1
  508.0 3.0 copy-start
Sparse Core Ops, SparseCore 0:
  9.6 37.1 all-gather.12
  48.4 34.6 all-gather.14
  84.7 34.3 all-gather.8
  121.0 34.4 all-gather.10
  267.7 45.8 reduce-scatter.4
  316.1 44.5 reduce-scatter.6
  363.2 44.5 reduce-scatter.8
  410.5 59.5 reduce-scatter.10

commit v5 on v4

--- a/solution.py
+++ b/solution.py
@@ -15,7 +15,7 @@
 GELU_C = math.sqrt(2.0 / math.pi)
 GELU_A = 0.044715
 VMEM_LIMIT = 60 * 1024 * 1024
-STREAMS = 4
+STREAMS = 7
 
 
 def mm(left, right):
@@ -52,6 +52,7 @@
 
 
 def pick_head(tiles, route, lane):
+    route = jnp.broadcast_to(route, lane.shape)
     pair = lax.shift_right_logical(route, 1)
     out = tiles[0]
     for j in range(1, len(tiles)):
@@ -62,6 +63,7 @@
 
 def place_heads(parts, routes, count, lane):
     half = lax.shift_right_logical(lane, 6)
+    routes = [jnp.broadcast_to(r, lane.shape) for r in routes]
     kept = [jnp.where(half == (r & 1), p, 0.0) for p, r in zip(parts, routes)]
     pairs = [lax.shift_right_logical(r, 1) for r in routes]
     tiles = []
@@ -544,24 +546,29 @@
     spot = lax.broadcasted_iota(jnp.int32, (cap, tokens), 0)
     sub = lax.broadcasted_iota(jnp.int32, (LANES, tokens), 0)
     sub8 = lax.broadcasted_iota(jnp.int32, (8, tokens), 0)
+    slots = [[slotrow_ref[m, i : i + 1, :] for i in range(2)] for m in range(micros)]
+
+    def onehot(m, s, which):
+        per = local // 2
+        base = (which // per) * (src * per) + s * per + which % per
+        base = spot + base * cap
+        return [jnp.where(base == t, 1.0, 0.0).astype(BF16) for t in slots[m]]
+
+    zero = jnp.zeros((24, tokens), F32)
+
+    def collect(s, carry):
+        carry = list(carry)
+        for which in range(local):
+            for m in range(micros):
+                values = split_three(got[s, m, which])
+                for i, p in enumerate(onehot(m, s, which)):
+                    carry[2 * m + i] = carry[2 * m + i] + mm(values, p)
+        return tuple(carry)
+
+    found_all = [join_three(f) for f in lax.fori_loop(0, src, collect, (zero,) * (2 * micros))]
+    shares = []
     for m, rowsc_ref in enumerate((rowsc0_ref, rowsc1_ref)):
-        slot = [slotrow_ref[m, i : i + 1, :] for i in range(2)]
-
-        def onehot(expert):
-            per = local // 2
-            which = lax.rem(expert, local)
-            base = lax.div(which, per) * (src * per) + lax.div(expert, local) * per + lax.rem(which, per)
-            base = spot + base * cap
-            return [jnp.where(base == s, 1.0, 0.0).astype(BF16) for s in slot]
-
-        zero = jnp.zeros((24, tokens), F32)
-
-        def collect(expert, carry):
-            values = split_three(got[lax.div(expert, local), m, lax.rem(expert, local)])
-            return tuple(c + mm(values, p) for c, p in zip(carry, onehot(expert)))
-
-        found = lax.fori_loop(0, src * local, collect, (zero, zero))
-        found = [join_three(f) for f in found]
+        found = found_all[2 * m : 2 * m + 2]
         stop, pull, gate0, gate1 = [rowsc_ref[i : i + 1, :] for i in range(4)]
         gates = [gate0, gate1]
         yh = [f[0:1, :] for f in found]
@@ -575,16 +582,18 @@
         for i, r in enumerate(keep):
             table = jnp.where(sub == i, r, table)
         cols_ref[m] = jnp.transpose(table)[:, :8]
-        ab = [split_three(jnp.where(sub8 == 0, g * halting, jnp.where(sub8 == 1, g * s, 0.0))) for g in gates]
-
-        def spread(expert, carry):
-            picks = onehot(expert)
-            sent[lax.div(expert, local), m, lax.rem(expert, local)] = join_three(
-                mm_nt(ab[0], picks[0]) + mm_nt(ab[1], picks[1])
-            )
-            return carry
-
-        lax.fori_loop(0, src * local, spread, 0)
+        shares.append(
+            [split_three(jnp.where(sub8 == 0, g * halting, jnp.where(sub8 == 1, g * s, 0.0))) for g in gates]
+        )
+
+    def spread(s, carry):
+        for which in range(local):
+            for m in range(micros):
+                picks = onehot(m, s, which)
+                sent[s, m, which] = join_three(mm_nt(shares[m][0], picks[0]) + mm_nt(shares[m][1], picks[1]))
+        return carry
+
+    lax.fori_loop(0, src, spread, 0)
     moves = group_copies(sent, got2, send_sem2, recv_sem2)
     for c in moves:
         c.start()
@@ -699,7 +708,7 @@
         glog = jnp.where(lane == col[:, 4 + i : 5 + i], cols[:, 2 + i : 3 + i], glog)
     glog = glog.astype(BF16)
     n2 = n2_ref[...]
-    gfr_ref[...] += mm_tn(n2, glog)
+    gfr_ref[...] += mm_tn(glog, n2)
     gn2 = gsum[...] + mm_nt(glog, frw_ref[...])
     hat2, rstd2 = norm_parts(mid_ref[...])
     grad = grad_ref[0].astype(F32)
@@ -709,14 +718,14 @@
     ggain2 = fold_rows(gn2 * hat2)
     gbias2 = fold_rows(gn2)
     gattn = gmid.astype(BF16)
-    gproj_ref[...] += mm_tn(mixed_ref[...], gattn)
+    gproj_ref[...] += mm_tn(gattn, mixed_ref[...])
     gmixed = mm_nt(gattn, proj_ref[...]).astype(BF16).astype(F32)
     pairs = gmixed.shape[1] // LANES
     tiles = [gmixed[:, j * LANES : (j + 1) * LANES] for j in range(pairs)]
     kv = kv_ref[...]
     scale = 0.125
     routes = [col[:, i : i + 1] for i in range(4)]
-    gkv = jnp.zeros((rows, LANES), F32)
+    gkv = jnp.zeros((LANES, rows), F32)
     ggates = []
     parts = []
     for i in range(4):
@@ -729,9 +738,9 @@
         gheads = (gate * sel).astype(BF16)
         gprobs = mm_nt(gheads, kv)
         probs_f = probs.astype(F32)
-        inner = jnp.sum(probs_f * gprobs, axis=-1, keepdims=True)
+        inner = jnp.sum(heads * gheads.astype(F32), axis=-1, keepdims=True)
         gscores = (probs_f * (gprobs - inner)).astype(BF16)
-        gkv = gkv + mm_tn(probs, gheads) + mm_tn(gscores, qs_ref[0, i]) * scale
+        gkv = gkv + mm_tn(gheads, probs) + mm_tn(qs_ref[0, i], gscores) * scale
         gq = mm(gscores, kv) * scale
         parts.append(jnp.where(low, gq, pltpu.roll(gq, LANES // 2, 1)))
     gtiles = place_heads(parts, routes, pairs, lane)
@@ -744,8 +753,8 @@
     alog = jnp.zeros((rows, LANES), F32)
     for i in range(4):
         alog = jnp.where(lane == routes[i], gates_ref[:, i : i + 1] * (ggates[i] - mean), alog)
-    gkvr = jnp.concatenate([gkv.astype(BF16), alog.astype(BF16)], axis=1)
-    gkvr_ref[...] += mm_tn(normed, gkvr)
+    gkvr = jnp.concatenate([jnp.transpose(gkv).astype(BF16), alog.astype(BF16)], axis=1)
+    gkvr_ref[...] += mm_tn(gkvr, normed)
     gnormed = mm_nt(gquery, qw_ref[...]) + mm_nt(gkvr, kvr_ref[...])
     hat, rstd = norm_parts(x_ref[0].astype(F32))
     gtok_ref[0] = grad * (1.0 - halting) + gmid + norm_back(hat, rstd, vec_ref[0:1, :], gnormed)
@@ -767,14 +776,13 @@
         for j in range(blocks):
             pack[j * width : (j + 1) * width, :] = gq_ref[:, j * width : (j + 1) * width].astype(BF16)
         place = blocks * width
-        pack[place : place + gproj_ref.shape[0], :] = gproj_ref[...].astype(BF16)
-        place = place + gproj_ref.shape[0]
-        wide = gkvr_ref.shape[1]
-        pack[place : place + width, :wide] = gkvr_ref[...].astype(BF16)
-        pack[place : place + width, wide : wide + LANES] = gfr_ref[...].astype(BF16)
-        pack[place : place + width, wide + LANES :] = jnp.zeros((width, width - wide - LANES), BF16)
-        if pack.shape[0] > place + width:
-            pack[place + width :, :] = jnp.zeros((pack.shape[0] - place - width, width), BF16)
+        for j in range(blocks):
+            pack[place : place + width, :] = jnp.transpose(gproj_ref[:, j * width : (j + 1) * width]).astype(BF16)
+            place = place + width
+        for ref in (gkvr_ref, gfr_ref):
+            pack[place : place + ref.shape[0], :] = ref[...].astype(BF16)
+            place = place + ref.shape[0]
+        pack[place:, :] = jnp.zeros((pack.shape[0] - place, width), BF16)
 
 
 def attention_backward(micro, last, packed_rows, tokens, grad, col, vec, qw, kvr, proj, frw, saved, near, far, cols, old, moving, cid):
@@ -785,11 +793,12 @@
     whole = lambda a: pl.BlockSpec(a.shape, lambda r: (0,) * a.ndim)
     by_row = lambda c: pl.BlockSpec((SEQ, c), lambda r: (r, 0))
     part = pl.BlockSpec((1, SEQ, width), lambda r: (micro, r, 0))
+    grown = [qw.shape] + [a.shape[::-1] for a in (proj, kvr, frw)]
     out_shape = [jax.ShapeDtypeStruct(tokens.shape, F32)]
     if last:
         out_shape += [jax.ShapeDtypeStruct((packed_rows, width), BF16)]
     else:
-        out_shape += [jax.ShapeDtypeStruct(a.shape, F32) for a in (qw, proj, kvr, frw)]
+        out_shape += [jax.ShapeDtypeStruct(s, F32) for s in grown]
     out_shape += [jax.ShapeDtypeStruct((8, width), F32)]
     old_in = [old[k] for k in (1, 2, 3, 4, 5)] if old else []
     hbm = pl.BlockSpec(memory_space=pl.ANY)
@@ -812,10 +821,7 @@
         out_shape, [part] + [pl.BlockSpec(o.shape, lambda r: (0, 0)) for o in out_shape[1:]],
         [
             pltpu.VMEM((SEQ, width), F32),
-            pltpu.VMEM(qw.shape, F32),
-            pltpu.VMEM(proj.shape, F32),
-            pltpu.VMEM(kvr.shape, F32),
-            pltpu.VMEM(frw.shape, F32),
+            *[pltpu.VMEM(s, F32) for s in grown],
             pltpu.VMEM((8, width), F32),
         ],
         (steps,), "attention_backward",
@@ -837,7 +843,7 @@
 
 
 def total_kernel(
-    sizes, streams, pack_ref, small_ref, gq_ref, gproj_ref, gkvr_ref, gfr_ref, sum_ref,
+    sizes, streams, pack_ref, small_ref, out_ref, sum_ref,
     buf, done, core_in, land, small_got, small_part, small_got2, sems, small_sems,
 ):
     nz, nx, ny = sizes
@@ -887,7 +893,9 @@
     }
     landed = [0]
 
-    def travel(first, count, order):
+    def travel(first, count, order, delay):
+        for _ in range(delay):
+            yield
         moves = [copy(rows_at(pack_ref, (1 - c) * half + first, count), rows_at(core_in, first, count), axes["c"][2](1 - c))]
         for m in moves:
             m.start()
@@ -958,32 +966,22 @@
 
     going, first = [], 0
     for i, count in enumerate(streams):
-        going.append(travel(first, count, ("yxz", "xyz")[i % 2]))
+        going.append(travel(first, count, ("yxz", "xyz")[i % 2], 2 * (i >= len(streams) // 2)))
         first += count
     going.append(travel_small())
     while going:
         going = [g for g in going if next(g, StopIteration) is not StopIteration]
-    blocks = gq_ref.shape[1] // width
-
-    def widen(target, lanes, base, count, span):
-        def body(i, carry):
-            here = pl.multiple_of(i * 64, 64)
-            target[pl.ds(here, 64), lanes] = done[pl.ds(base + here, 64), span].astype(F32)
-            return carry
-
-        lax.fori_loop(0, count // 64, body, 0)
-
-    for j in range(blocks):
-        widen(gq_ref, slice(j * width, (j + 1) * width), j * width, width, slice(0, width))
-    base = blocks * width
-    widen(gproj_ref, slice(0, width), base, gproj_ref.shape[0], slice(0, width))
-    base = base + gproj_ref.shape[0]
-    wide = gkvr_ref.shape[1]
-    widen(gkvr_ref, slice(0, wide), base, width, slice(0, wide))
-    widen(gfr_ref, slice(0, LANES), base, width, slice(wide, wide + LANES))
-
-
-def total_step(n_expert, n_hidden, rows, pack, small, qw, proj, kvr, frw):
+    step = 64 if half % 64 == 0 else 16
+
+    def body(i, carry):
+        here = pl.ds(pl.multiple_of(i * step, step), step)
+        out_ref[here, :] = done[here, :]
+        return carry
+
+    lax.fori_loop(0, 2 * half // step, body, 0)
+
+
+def total_step(n_expert, n_hidden, rows, pack, small):
     sizes, streams = total_plan(n_expert, n_hidden, rows)
     nz, nx, ny = sizes
     width = pack.shape[1]
@@ -997,9 +995,9 @@
     steps = len(streams) * (2 + 2 * ((ny - 1) + (nx - 1) + (nz - 1)))
     return pl.pallas_call(
         functools.partial(total_kernel, sizes, streams),
-        out_shape=tuple(jax.ShapeDtypeStruct(a.shape, F32) for a in (qw, proj, kvr, frw, small)),
+        out_shape=(jax.ShapeDtypeStruct(pack.shape, BF16), jax.ShapeDtypeStruct(small.shape, F32)),
         in_specs=[vmem] * 2,
-        out_specs=[vmem] * 5,
+        out_specs=[vmem] * 2,
         scratch_shapes=[
             pltpu.VMEM((2 * half, width), BF16),
             pltpu.VMEM((2 * half, width), BF16),
@@ -1014,6 +1012,54 @@
         compiler_params=pltpu.CompilerParams(collective_id=8, has_side_effects=True, vmem_limit_bytes=VMEM_LIMIT),
         name="total_step",
     )(pack, small)
+
+
+def unpack_kernel(
+    pack_ref, near_a, near_b, far_a, far_b,
+    gq_ref, gproj_ref, first_ref, second_ref, key_ref, value_ref, router_ref, ffn_ref,
+):
+    step = pl.program_id(0)
+    width = pack_ref.shape[2]
+    blocks = gproj_ref.shape[0]
+    for j in range(blocks):
+        gq_ref[:, j * width : (j + 1) * width] = pack_ref[j].astype(F32)
+        gproj_ref[j] = pack_ref[blocks + j].astype(F32)
+    first_ref[...] = near_a[...].astype(F32) + far_a[...].astype(F32)
+    second_ref[...] = near_b[...].astype(F32) + far_b[...].astype(F32)
+    head = key_ref.shape[0]
+
+    @pl.when(step == 0)
+    def _():
+        key_ref[...] = pack_ref[2 * blocks, :head, :].astype(F32)
+        value_ref[...] = pack_ref[2 * blocks, head : 2 * head, :].astype(F32)
+
+    @pl.when(step == 1)
+    def _():
+        router_ref[...] = pack_ref[2 * blocks, : router_ref.shape[0], :].astype(F32)
+
+    @pl.when(step == 2)
+    def _():
+        ffn_ref[...] = pack_ref[2 * blocks, : ffn_ref.shape[0], :].astype(F32)
+
+
+def unpack_step(pack, near, far, head, routes, experts):
+    steps = 4
+    slabs, width, _ = pack.shape
+    blocks = slabs // 2
+    rows = width // steps
+    out_shape = [
+        jax.ShapeDtypeStruct((width, blocks * width), F32),
+        jax.ShapeDtypeStruct((blocks, width, width), F32),
+        *[jax.ShapeDtypeStruct(a.shape, F32) for a in near],
+        *[jax.ShapeDtypeStruct((n, width), F32) for n in (head, head, routes, experts)],
+    ]
+    cut = lambda a: pl.BlockSpec((a.shape[0], a.shape[1] // steps, a.shape[2]), lambda i: (0, i, 0))
+    return run_kernel(
+        unpack_kernel, (pack, *near, *far), [cut(pack)] + [cut(a) for a in near] * 2, out_shape,
+        [pl.BlockSpec((rows, blocks * width), lambda i: (i, 0)), cut(out_shape[1])] + [cut(a) for a in near]
+        + [pl.BlockSpec(o.shape, lambda i: (0, 0)) for o in out_shape[4:]],
+        (), (steps,), "unpack_step", pl.CostEstimate(flops=0, bytes_accessed=20 << 20, transcendentals=0),
+    )
 
 
 def pad_lanes(a):
@@ -1099,25 +1145,26 @@
         1, True, packed_rows, *common, list(f1[:8]) + [slotcol], flat(qn1), flat(qf1), cols, tuple(out), (), None
     )
     packs = out[1]
-    gfirst, gsecond = [a.astype(F32) + b.astype(F32) for a, b in zip(near_grads, far_grads)]
     small = jnp.concatenate([out[2], res0[1] + res1[1]], axis=0)
-    gq, gproj, gkvr, gfr, small = total_step(
-        n_expert, n_hidden, packed, packs, small, query_w, attn_proj, kvr, frw
-    )
-    head = key_w.shape[1]
+    total, small = total_step(n_expert, n_hidden, packed, packs, small)
+    near_grads = [a.reshape(a.shape[-3:]) for a in near_grads]
+    far_grads = [a.reshape(a.shape[-3:]) for a in far_grads]
+    gq, gproj, gfirst, gsecond, gkey, gvalue, grouter, gfr = unpack_step(
+        total[:packed].reshape(-1, width, width), near_grads, far_grads, key_w.shape[1], attn_router.shape[1], experts
+    )
     return (
         res1[0],
         out[0],
         small[0],
         small[1],
-        gkvr[:, LANES : LANES + attn_router.shape[1]],
+        grouter.T,
         gq,
-        gkvr[:, :head],
-        gkvr[:, head : 2 * head],
-        gproj,
+        gkey.T,
+        gvalue.T,
+        gproj.reshape(attn_proj.shape),
         small[2],
         small[3],
-        gfr[:, :experts],
+        gfr.T,
         gfirst,
         gsecond,
         small[8],

time: 527 us -> 507 us (0.962)
  Pallas kernels: 441 us -> 420 us
  waiting for transfers between devices: 19.9 us -> 34.9 us
  local copies, waits for them, and re-layouts: 25.2 us -> 16.3 us
  other arithmetic: 9.36 us -> 3.53 us
    pallas_call x13 -> x14, Pallas kernels: 344 us -> 329 us  [run_kernel(): pl.pallas_call(body, grid=grid, out_shape=tuple(out_shape) + tuple((jax.S...]
    ppermute x1, waiting for transfers between devices: 7.89 us -> 15.6 us  [per_device(): far_grads[0] = lax.ppermute(far_grads[0], 'expert', across)]
    pallas_call x1, Pallas kernels: 23.4 us -> 16.1 us  [scalar_step(): pl.pallas_call(scalar_kernel, out_shape=(jax.ShapeDtypeStruct((2, tokens,...]
    ppermute x2, waiting for transfers between devices: 9.19 us -> 16.5 us  [per_device(): lax.ppermute(a, 'expert', across)]
    unnamed x43 -> x35, local copies, waits for them, and re-layouts: 12.8 us -> 6.14 us
    add x2 -> x0, other arithmetic: 5.83 us -> none  [per_device(): a.astype(F32) + b.astype(F32)]
  transfers between devices with their start and end apart: 12 -> 12, of which waited for: 3 -> 3; matrix products, arithmetic and copies ran while one was open for 5% -> 3% of each run, Pallas kernels for 66% -> 65%
where the time goes in v5:
time: 507 us; the launch traced here: 499 us
  Pallas kernels  420 us (83%)
  waiting for transfers between devices  34.9 us (7%)
  local copies, waits for them, and re-layouts  16.3 us (3%)
  between operations  15.6 us (3%)
  starting transfers between devices  8.16 us (2%)
    pallas_call x14, Pallas kernels, run_kernel(): pl.pallas_call(body, grid=grid, out_shape=tuple(out_shape) + tuple((jax.S...  329 us
    pallas_call x1, Pallas kernels, total_step(): pl.pallas_call(functools.partial(total_kernel, sizes, streams), out_shape...  75 us
    ppermute x2, waiting for transfers between devices, per_device(): lax.ppermute(a, 'expert', across)  16.5 us
    pallas_call x1, Pallas kernels, scalar_step(): pl.pallas_call(scalar_kernel, out_shape=(jax.ShapeDtypeStruct((2, tokens,...  16.1 us
    ppermute x1, waiting for transfers between devices, per_device(): far_grads[0] = lax.ppermute(far_grads[0], 'expert', across)  15.6 us
  transfers between devices with their start and end apart: 12, of which 3 were waited for; matrix products, arithmetic and copies ran while one was open for 3% of the time, Pallas kernels for 65%

profile of v5, /device:TPU:0, one launch (start us, length us, event | category | flops | bytes accessed | tf_op | source)
XLA Modules:
  0.0 498.6 jit_solution(11007388591295700432)
XLA Ops:
  8.8 4.1 collective-permute-start
  14.3 1.0 copy.67
  15.2 1.5 copy.69
  17.4 1.6 pad.9.refs_10_.refs_7_
  20.2 1.5 stack.36.refs_5_.refs_8_.refs_3_
  22.3 1.4 stack.39.refs_0_.refs_3_
  23.7 2.0 route_step.1
  26.5 1.3 pad_add_fusion.refs_2_
  28.4 14.3 %attention_forward.2 = (f32[512,512]{1,0:T(8,128)}, bf16[512,512]{1,0:T(8,128)(2,1)}, bf16[512,512]{1,0:T(8,128)(2,1)}, bf16[512,1536]{1,0:T(8,128)(2,1)}, bf16[...) custom-call(bf16[2,512,512]{2,1,0:T(8,128)(2,1)} %refs_0_.11, ...), custom_call_target="tpu_custom_call" | custom-call | flops 2818572288 | bytes 12582912 | tf_op jit(solution)/shard_map/attention_forward/pallas_call | solution.py:214
  42.7 15.9 %collective-permute-done = bf16[2,512,512]{2,1,0:T(8,128)(2,1)} collective-permute-done((bf16[2,512,512]{2,1,0:T(8,128)(2,1)S(1)}, bf16[2,512,512]{2,1,0:T(8,128)(2,1)}, u32[]{:S(2)}, u32[]{:S(2)}) %collective-permute-start) | collective-permute-done | bytes 1048608 | tf_op jit(solution)/shard_map/ppermute | solution.py:1085
  58.8 47.2 %attention_forward.3 = (f32[512,512]{1,0:T(8,128)}, bf16[512,512]{1,0:T(8,128)(2,1)}, bf16[512,512]{1,0:T(8,128)(2,1)}, bf16[512,1536]{1,0:T(8,128)(2,1)}, bf16[...) custom-call(bf16[2,512,512]{2,1,0:T(8,128)(2,1)} %refs_0_.11, ...), custom_call_target="tpu_custom_call" | custom-call | flops 2818572288 | bytes 12582912 | tf_op jit(solution)/shard_map/attention_forward/pallas_call | solution.py:214
  106.6 1.0 copy-done.4
  107.8 33.8 %spread_step.1 = (bf16[2048,512]{1,0:T(8,128)(2,1)}, bf16[2048,512]{1,0:T(8,128)(2,1)}, bf16[2,4,2,128,512]{4,3,2,1,0:T(8,128)(2,1)}) custom-call(s32[2,8,512]{2,1,0:T(8,128)} %get-tuple-element.105.refs_4_.refs_0_.slotrow_ref, bf16[2,512,512]{2,1,0:T(8,128)(2,1)} %refs_1_.9, bf16[2,4,2,128,512]{4,3,2,1,0:T(8,128)(2,1)} %bitcast.82), custom_call_target="tpu_custom_call" | custom-call | flops 4294967296 | bytes 6291456 | tf_op jit(solution)/shard_map/spread_step/pallas_call | solution.py:214
  141.7 29.0 %expert_forward.3 = (bf16[4,2,128,512]{3,2,1,0:T(8,128)(2,1)}, bf16[4,2,128,512]{3,2,1,0:T(8,128)(2,1)}, bf16[2,4,2,128,512]{4,3,2,1,0:T(8,128)(2,1)}) custom-call(bf16[2,4,2,128,512]{4,3,2,1,0:T(8,128)(2,1)} %get-tuple-element.117.refs_0_, bf16[2,4,2,128,512]{4,3,2,1,0:T(8,128)(2,1)} %get-tuple-element.120.refs_1_, bf16[4,2,512,512]{3,2,1,0:T(8,128)(2,1)} %bitcast.66, ...), custom_call_target="tpu_custom_call" | custom-call | flops 8589934592 | bytes 25165824 | tf_op jit(solution)/shard_map/expert_forward/pallas_call | solution.py:214
  170.7 28.1 %expert_forward.2 = (bf16[4,2,128,512]{3,2,1,0:T(8,128)(2,1)}, bf16[4,2,128,512]{3,2,1,0:T(8,128)(2,1)}, bf16[2,4,2,128,512]{4,3,2,1,0:T(8,128)(2,1)}) custom-call(bf16[2,4,2,128,512]{4,3,2,1,0:T(8,128)(2,1)} %get-tuple-element.117.refs_0_, bf16[2,4,2,128,512]{4,3,2,1,0:T(8,128)(2,1)} %get-tuple-element.120.refs_1_, bf16[4,2,512,512]{3,2,1,0:T(8,128)(2,1)} %bitcast.70, ...), custom_call_target="tpu_custom_call" | custom-call | flops 8589934592 | bytes 25165824 | tf_op jit(solution)/shard_map/expert_forward/pallas_call | solution.py:214
  198.8 6.8 %reading_step.1 = f32[4,2,2,2,8,128]{5,4,3,2,1,0:T(8,128)} custom-call(bf16[4,2,128,512]{3,2,1,0:T(8,128)(2,1)} %get-tuple-element.127.refs_0_.refs_8_, bf16[4,2,128,512]{3,2,1,0:T(8,128)(2,1)} %get-tuple-element.128.refs_1_.refs_10_, bf16[4,2,128,512]{3,2,1,0:T(8,128)(2,1)} %get-tuple-element.129.refs_2_.refs_9_, ...), custom_call_target="tpu_custom_call" | custom-call | flops 1000000000 | bytes 8388608 | tf_op jit(solution)/shard_map/reading_step/pallas_call | solution.py:214
  205.6 16.1 %scalar_step.1 = (f32[2,512,8]{2,1,0:T(8,128)}, f32[4,2,4,8,128]{4,3,2,1,0:T(8,128)}) custom-call(f32[4,2,4,8,128]{4,3,2,1,0:T(8,128)} %bitcast.54, f32[8,512]{1,0:T(8,128)} %get-tuple-element.131.rowsc0_ref, f32[8,512]{1,0:T(8,128)} %get-tuple-element.132.rowsc1_ref, s32[2,8,512]{2,1,0:T(8,128)} %get-tuple-element.105.refs_4_.refs_0_.slotrow_ref), custom_call_target="tpu_custom_call" | custom-call | flops 1000000000 | bytes 1048576 | tf_op jit(solution)/shard_map/scalar_step/pallas_call | solution.py:610
  221.7 38.0 %expert_backward.2 = (bf16[4,2,512,512]{3,2,1,0:T(8,128)(2,1)}, bf16[4,2,512,512]{3,2,1,0:T(8,128)(2,1)}, bf16[4,2,128,512]{3,2,1,0:T(8,128)(2,1)}, bf16[4,2,128...) custom-call(bf16[2,4,2,128,512]{4,3,2,1,0:T(8,128)(2,1)} %get-tuple-, ...), custom_call_target="tpu_custom_call" | custom-call | flops 21474836480 | bytes 50331648 | tf_op jit(solution)/shard_map/expert_backward/pallas_call | solution.py:214
  260.6 40.1 %expert_backward.3 = (bf16[4,2,512,512]{3,2,1,0:T(8,128)(2,1)}, bf16[4,2,512,512]{3,2,1,0:T(8,128)(2,1)}, bf16[4,2,128,512]{3,2,1,0:T(8,128)(2,1)}, bf16[4,2,128...) custom-call(bf16[2,4,2,128,512]{4,3,2,1,0:T(8,128)(2,1)} %get-tuple-, ...), custom_call_target="tpu_custom_call" | custom-call | flops 21474836480 | bytes 50331648 | tf_op jit(solution)/shard_map/expert_backward/pallas_call | solution.py:214
  301.5 28.4 %result_step.2 = (bf16[2,512,512]{2,1,0:T(8,128)(2,1)}, f32[8,512]{1,0:T(8,128)}, bf16[4,2,128,512]{3,2,1,0:T(8,128)(2,1)}, bf16[4,2,128,512]{3,2,1,0:T(8,128)(2,1)}) custom-call(bf16[2,512,512]{2,1,0:T(8,128)(2,1)} %refs_0_.11, f32[512,512]{1,0:T(8,128)} %get-tuple-element.106.refs_1_.refs_8_, bf16[1024,512]{1,0:T(8,128)(2,1)} %bitcast.87, ...), custom_call_target="tpu_custom_call" | custom-call | flops 2147483648 | bytes 5242880 | tf_op jit(solution)/shard_map/result_step/pallas_call | solution.py:214
  329.9 3.3 collective-permute-start.2
  333.2 7.7 %result_step.3 = (bf16[2,512,512]{2,1,0:T(8,128)(2,1)}, f32[8,512]{1,0:T(8,128)}) custom-call(bf16[2,512,512]{2,1,0:T(8,128)(2,1)} %refs_0_.11, f32[512,512]{1,0:T(8,128)} %get-tuple-element.153.refs_1_.refs_8_, bf16[1024,512]{1,0:T(8,128)(2,1)} %bitcast.85, bf16[1024,512]{1,0:T(8,128)(2,1)} %bitcast.89, ...), custom_call_target="tpu_custom_call", output_to_operand_aliasing={{0}: (6, {})} | custom-call | flops 2147483648 | bytes 5242880 | tf_op jit(solution)/shard_map/result_step/pallas_call | solution.py:214
  340.9 22.7 %attention_backward.2 = (f32[2,512,512]{2,1,0:T(8,128)}, f32[512,1536]{1,0:T(8,128)}, f32[512,1536]{1,0:T(8,128)}, f32[256,512]{1,0:T(8,128)}, f32[128,512]{1,0:T(8,128)}, /*index=5*/f32[8,512]{1,0:T(8,128)}) custom-call(bf16[2,512,512]{2,1,0:T(8,128)(2,1)} %refs_0_.11, bf16[2,512,512]{2,1,0:T(8,128)(2,1)} %refs_1_.9, s32[2,512,8]{2,1,0:T(8,128)} %pad_add_fusion.refs_2_, ...), custom_call_target="tpu_custom_call" | custom-call | flops 4563402752 | bytes 25165824 | tf_op jit(solution)/shard_map/attention_backward/pallas_call | solution.py:214
  363.6 15.6 %collective-permute-done.2.refs_3_ = bf16[2,512,512]{2,1,0:T(8,128)(2,1)S(1)} collective-permute-done((bf16[2,512,512]{2,1,0:T(8,128)(2,1)}, bf16[2,512,512]{2,1,0:T(8,128)(2,1)S(1)}, u32[]{:S(2)}, u32[]{:S(2)}) %collective-permute-start.2) | collective-permute-done | bytes 1048608 | tf_op jit(solution)/shard_map/ppermute | solution.py:1137
  379.2 23.5 %attention_backward.3 = (f32[2,512,512]{2,1,0:T(8,128)}, bf16[3584,512]{1,0:T(8,128)(2,1)}, f32[8,512]{1,0:T(8,128)}) custom-call(bf16[2,512,512]{2,1,0:T(8,128)(2,1)} %refs_0_.11, bf16[2,512,512]{2,1,0:T(8,128)(2,1)} %refs_1_.9, s32[2,512,8]{2,1,0:T(8,128)} %pad_add_fusion.refs_2_, ...), custom_call_target="tpu_custom_call", output_to_operand_aliasing={{0}: (25, {})} | custom-call | flops 4563402752 | bytes 25165824 | tf_op jit(solution)/shard_map/attention_backward/pallas_call | solution.py:214
  402.7 1.3 pad_maximum_fusion.small_ref
  404.1 75.0 %total_step.1 = (bf16[3584,512]{1,0:T(8,128)(2,1)}, f32[16,512]{1,0:T(8,128)}) custom-call(bf16[3584,512]{1,0:T(8,128)(2,1)} %get-tuple-element.176.pack_ref, f32[16,512]{1,0:T(8,128)} %pad_maximum_fusion.small_ref), custom_call_target="tpu_custom_call" | custom-call | tf_op jit(solution)/shard_map/total_step/pallas_call | solution.py:996
  479.0 1.2 slice.39
  480.2 1.5 fusion.4
  481.8 1.0 copy-done.1
  482.8 7.6 %unpack_step.1 = (f32[512,1536]{1,0:T(8,128)}, f32[3,512,512]{2,1,0:T(8,128)}, f32[2,512,512]{2,1,0:T(8,128)}, f32[2,512,512]{2,1,0:T(8,128)}, f32[64,512]{1,0:T...) custom-call(bf16[7,512,512]{2,1,0:T(8,128)(2,1)} %bitcast.49, bf16[2,512,512]{2,1,0:T(8,128)(2,1)} %bitcast.50, ...), custom_call_target="tpu_custom_call" | custom-call | bytes 20971520 | tf_op jit(solution)/shard_map/unpack_step/pallas_call | solution.py:214
  490.4 1.0 copy.74
  (70 shorter events, 8.8 us)
Async XLA Ops:
  7.2 1.6 copy-start.2
  7.2 5.7 %copy-start.9 = (s32[2,2,256]{2,1,0:T(2,128)S(1)}, s32[2,2,256]{2,1,0:T(2,128)}, u32[]{:S(2)}) copy-start(s32[2,2,256]{2,1,0:T(2,128)} %param.24) | copy-start | bytes 12292
  7.2 6.1 %copy-start.10 = (s32[2,512]{1,0:T(2,128)S(1)}, s32[2,512]{1,0:T(2,128)}, u32[]{:S(2)}) copy-start(s32[2,512]{1,0:T(2,128)} %param.25) | copy-start | bytes 12292
  7.2 6.3 %copy-start.6 = (s32[2,512,2]{1,2,0:T(2,128)S(1)}, s32[2,512,2]{1,2,0:T(2,128)}, u32[]{:S(2)}) copy-start(s32[2,512,2]{1,2,0:T(2,128)} %param.23) | copy-start | bytes 24580
  7.2 6.5 %copy-start.11 = (s32[2,512,4]{1,2,0:T(4,128)S(1)}, s32[2,512,4]{1,2,0:T(4,128)}, u32[]{:S(2)}) copy-start(s32[2,512,4]{1,2,0:T(4,128)} %param.22) | copy-start | bytes 49156
  7.2 6.8 %copy-start.8 = (bf16[512,24]{0,1:T(8,128)(2,1)S(1)}, bf16[512,24]{0,1:T(8,128)(2,1)}, u32[]{:S(2)}) copy-start(bf16[512,24]{0,1:T(8,128)(2,1)} %param.28) | copy-start | bytes 73732
  7.2 6.9 %copy-start.7 = (bf16[512,64]{0,1:T(8,128)(2,1)S(1)}, bf16[512,64]{0,1:T(8,128)(2,1)}, u32[]{:S(2)}) copy-start(bf16[512,64]{0,1:T(8,128)(2,1)} %param.31) | copy-start | bytes 196612
  7.3 134.4 %all-gather.13.cloned.1.call-start = ((), (), s32[]{:S(2)}) async-start(), calls=%async_computation.10 | async-start | bytes 5242880 | tf_op jit(solution)/shard_map/all_gather | solution.py:1083
  8.0 133.7 %all-gather.15.cloned.1.call-start = ((), (), s32[]{:S(2)}) async-start(), calls=%async_computation.11 | async-start | bytes 5242880 | tf_op jit(solution)/shard_map/all_gather | solution.py:1083
  8.7 162.0 %all-gather.9.cloned.1.call-start = ((), (), s32[]{:S(2)}) async-start(), calls=%async_computation.8 | async-start | bytes 5242880 | tf_op jit(solution)/shard_map/all_gather | solution.py:1083
  8.8 49.8 %collective-permute-start = (bf16[2,512,512]{2,1,0:T(8,128)(2,1)S(1)}, bf16[2,512,512]{2,1,0:T(8,128)(2,1)}, u32[]{:S(2)}, u32[]{:S(2)}) collective-permute-start(bf16[2,512,512]{2,1,0:T(8,128)(2,1)S(1)} %copy-done.2), channel_id=1, source_target_pairs={{0,16},{4,20},{8,24},{12,28},{16,0},{20,4},{24,8},{28,12},{1,17},{... | collective-permute-start | bytes 3145736 | tf_op jit(solution)/shard_map/ppermute | solution.py:1085
  28.4 30.3 %copy-start.3 = (bf16[2,512,512]{2,1,0:T(8,128)(2,1)S(1)}, bf16[2,512,512]{2,1,0:T(8,128)(2,1)}, u32[]{:S(2)}) copy-start(bf16[2,512,512]{2,1,0:T(8,128)(2,1)} %param.37) | copy-start | bytes 3145732
  58.7 112.1 %all-gather.11.cloned.1.call-start = ((), (), s32[]{:S(2)}) async-start(), calls=%async_computation.9 | async-start | bytes 5242880 | tf_op jit(solution)/shard_map/all_gather | solution.py:1083
  58.7 47.9 %collective-permute-start.1 = (bf16[2,512,512]{2,1,0:T(8,128)(2,1)S(1)}, bf16[2,512,512]{2,1,0:T(8,128)(2,1)S(1)}, u32[]{:S(2)}, u32[]{:S(2)}) collective-permute-start(bf16[2,512,512]{2,1,0:T(8,128)(2,1)S(1)} %copy-done.3), channel_id=1, source_target_pairs={{0,16},{4,20},{8,24},{12,28},{16,0},{20,4},{24,8},{28,12},{1,17},{... | collective-permute-start | bytes 3145736 | tf_op jit(solution)/shard_map/ppermute | solution.py:1085
  106.6 1.0 copy-start.4
  107.6 222.3 %reduce-scatter.5.cloned.1.call-start = ((), (), s32[]{:S(2)}) async-start(), calls=%async_computation.4 | async-start | bytes 5242880 | tf_op jit(solution)/shard_map/reduce_scatter | solution.py:1130
  259.7 103.9 %reduce-scatter.7.cloned.1.call-start = ((), (), s32[]{:S(2)}) async-start(), calls=%async_computation.5 | async-start | bytes 5242880 | tf_op jit(solution)/shard_map/reduce_scatter | solution.py:1130
  260.3 221.4 %reduce-scatter.9.cloned.1.call-start = ((), (), s32[]{:S(2)}) async-start(), calls=%async_computation.6 | async-start | bytes 5242880 | tf_op jit(solution)/shard_map/reduce_scatter | solution.py:1130
  300.7 181.0 %reduce-scatter.11.cloned.1.call-start = ((), (), s32[]{:S(2)}) async-start(), calls=%async_computation.7 | async-start | bytes 5242880 | tf_op jit(solution)/shard_map/reduce_scatter | solution.py:1130
  329.9 49.3 %collective-permute-start.2 = (bf16[2,512,512]{2,1,0:T(8,128)(2,1)}, bf16[2,512,512]{2,1,0:T(8,128)(2,1)S(1)}, u32[]{:S(2)}, u32[]{:S(2)}) collective-permute-start(bf16[2,512,512]{2,1,0:T(8,128)(2,1)} %bitcast.76), channel_id=1, source_target_pairs={{0,16},{4,20},{8,24},{12,28},{16,0},{20,4},{24,8},{28,12},{1,17},{... | collective-permute-start | bytes 3145736 | tf_op jit(solution)/shard_map/ppermute | solution.py:1137
  340.9 38.3 %copy-start.12 = (f32[8,512]{1,0:T(8,128)S(1)}, f32[8,512]{1,0:T(8,128)}, u32[]{:S(2)}) copy-start(f32[8,512]{1,0:T(8,128)} %get-tuple-element.178) | copy-start | bytes 49156
  340.9 38.3 %copy-start.13 = (f32[8,512]{1,0:T(8,128)S(1)}, f32[8,512]{1,0:T(8,128)}, u32[]{:S(2)}) copy-start(f32[8,512]{1,0:T(8,128)} %get-tuple-element.179) | copy-start | bytes 49156
  379.2 23.5 %copy-start = (bf16[2,512,512]{2,1,0:T(8,128)(2,1)}, bf16[2,512,512]{2,1,0:T(8,128)(2,1)S(1)}, u32[]{:S(2)}) copy-start(bf16[2,512,512]{2,1,0:T(8,128)(2,1)S(1)} %collective-permute-done.2.refs_3_) | copy-start | bytes 3145732
  379.2 102.6 %collective-permute-start.3 = (bf16[2,512,512]{2,1,0:T(8,128)(2,1)}, bf16[2,512,512]{2,1,0:T(8,128)(2,1)S(1)}, u32[]{:S(2)}, u32[]{:S(2)}) collective-permute-start(bf16[2,512,512]{2,1,0:T(8,128)(2,1)} %bitcast.75), channel_id=1, source_target_pairs={{0,16},{4,20},{8,24},{12,28},{16,0},{20,4},{24,8},{28,12},{1,17},{... | collective-permute-start | bytes 3145736 | tf_op jit(solution)/shard_map/ppermute | solution.py:1143
  481.8 1.0 copy-start.1
  482.8 7.6 %copy-start.5 = (bf16[2,512,512]{2,1,0:T(8,128)(2,1)S(1)}, bf16[2,512,512]{2,1,0:T(8,128)(2,1)}, u32[]{:S(2)}) copy-start(bf16[2,512,512]{2,1,0:T(8,128)(2,1)} %get-tuple-element.221) | copy-start | bytes 3145732
Sparse Core Ops, SparseCore 0:
  9.6 37.1 all-gather.12
  48.4 34.4 all-gather.14
  84.5 34.5 all-gather.8
  121.1 34.4 all-gather.10
  259.8 45.8 reduce-scatter.4
  308.3 44.4 reduce-scatter.6
  355.3 44.4 reduce-scatter.8
  402.5 59.9 reduce-scatter.10

commit v6 on v5

--- a/solution.py
+++ b/solution.py
@@ -136,7 +136,12 @@
     return me, size, e - me
 
 
-def group_greet():
+def other_core():
+    e, h = lax.axis_index("expert"), lax.axis_index("hidden")
+    return e, h + 1 - 2 * lax.rem(h, 2)
+
+
+def group_greet(mate=False):
     me, size, base = group_of()
     other = lax.axis_index("hidden")
     barrier = pltpu.get_barrier_semaphore()
@@ -144,7 +149,9 @@
         pl.semaphore_signal(
             barrier, inc=1, device_id=(base + lax.rem(me + k, size), other), device_id_type=pl.DeviceIdType.MESH
         )
-    pl.semaphore_wait(barrier, size - 1)
+    if mate:
+        pl.semaphore_signal(barrier, inc=1, device_id=other_core(), device_id_type=pl.DeviceIdType.MESH)
+    pl.semaphore_wait(barrier, size if mate else size - 1)
 
 
 def group_copies(source, target, send_sem, recv_sem):
@@ -170,7 +177,7 @@
     return found
 
 
-def run_kernel(kernel, args, in_specs, out_shape, out_specs, scratch, grid, name, cost, moving=(), cid=None, aliases=None):
+def run_kernel(kernel, args, in_specs, out_shape, out_specs, scratch, grid, name, cost, moving=(), cid=None, aliases=None, mate=False):
     n_in, n_out, n_move = len(args), len(out_shape), len(moving)
     peers = lax.axis_size("expert") // 2 - 1
     hbm = pl.BlockSpec(memory_space=pl.ANY)
@@ -194,7 +201,7 @@
 
             @pl.when(at_step((0, grid)))
             def _():
-                group_greet()
+                group_greet(mate)
                 for c in moves + owns:
                     c.start()
 
@@ -465,9 +472,52 @@
     )[0].reshape(src, 2, 2 * local, 8, cap)
 
 
+def add_cores(grown, gfirst_ref, gsecond_ref, keep, away, land, send_sem, recv_sem):
+    step = pl.program_id(0) * pl.num_programs(1) + pl.program_id(1)
+    steps = pl.num_programs(0) * pl.num_programs(1)
+    pair = lax.div(step, 2)
+    owned = lax.rem(step, 2) == lax.rem(lax.axis_index("hidden"), 2)
+
+    def crossing(k):
+        return [
+            pltpu.make_async_remote_copy(
+                away[i].at[k], land[i].at[k], send_sem.at[i, k], recv_sem.at[i, k],
+                device_id=other_core(), device_id_type=pl.DeviceIdType.MESH,
+            )
+            for i in range(2)
+        ]
+
+    @pl.when(owned)
+    def _():
+        for i in range(2):
+            keep[i][pair] = grown[i]
+
+    @pl.when(jnp.logical_not(owned))
+    def _():
+        for i in range(2):
+            away[i][pair] = grown[i]
+        for c in crossing(pair):
+            c.start()
+
+    def finish(k):
+        for c in crossing(k):
+            c.wait()
+        local, y = lax.div(k, gfirst_ref.shape[0]), lax.rem(k, gfirst_ref.shape[0])
+        for ref, mine, got in ((gfirst_ref, keep[0], land[0]), (gsecond_ref, keep[1], land[1])):
+            ref[y, local] = (mine[k].astype(F32) + got[k].astype(F32)).astype(BF16)
+
+    @pl.when((lax.rem(step, 2) == 0) & (step >= 2))
+    def _():
+        finish(pair - 1)
+
+    @pl.when(step == steps - 1)
+    def _():
+        finish(pair)
+
+
 def expert_backward_kernel(
-    rows0_ref, rows1_ref, grad0_ref, grad1_ref, ab_ref, vec_ref, first_ref, second_ref,
-    gfirst_ref, gsecond_ref, out0_ref, out1_ref, total, gin_all,
+    fold, rows0_ref, rows1_ref, grad0_ref, grad1_ref, ab_ref, vec_ref, first_ref, second_ref,
+    gfirst_ref, gsecond_ref, out0_ref, out1_ref, total, gin_all, *crossed,
 ):
     part = pl.program_id(1)
     _, src, _, cap, width = rows0_ref.shape
@@ -492,8 +542,11 @@
     act = (pre * part_one).astype(BF16)
     slope = part_one + 0.5 * pre * (1.0 - inner * inner) * (GELU_C + (3.0 * GELU_C * GELU_A) * square)
     gpre = (gact * slope).astype(BF16)
-    gsecond_ref[0, 0] = mm_tn(act, gin).astype(BF16)
-    gfirst_ref[0, 0] = mm_tn(rows, gpre).astype(BF16)
+    grown = (mm_tn(rows, gpre).astype(BF16), mm_tn(act, gin).astype(BF16))
+    if fold:
+        add_cores(grown, gfirst_ref, gsecond_ref, *crossed)
+    else:
+        gfirst_ref[0, 0], gsecond_ref[0, 0] = grown
     res = mm_nt(gpre, first)
 
     @pl.when(part == 0)
@@ -518,17 +571,21 @@
     spec_first = pl.BlockSpec((1, 1, width, hid), lambda e, h: (h, e, 0, 0))
     spec_second = pl.BlockSpec((1, 1, hid, width), lambda e, h: (h, e, 0, 0))
     work = 2 * src * local * cap * width * hid * parts
+    fold = kind == 0
+    grown = [((parts // 2,) + a.shape[1:] if fold else a.shape) for a in (first, second)]
+    pairs = local * parts // 2
+    kept = [pltpu.VMEM((pairs,) + a.shape[2:], BF16) for a in (first, second)]
     return run_kernel(
-        expert_backward_kernel, (*rows, *grads, ab, vec, first, second),
+        functools.partial(expert_backward_kernel, fold), (*rows, *grads, ab, vec, first, second),
         [spec_in] * 4
         + [pl.BlockSpec((src, 2, 1, 8, cap), lambda e, h: (0, 0, kind * local + e, 0, 0)), pl.BlockSpec(vec.shape, lambda e, h: (0, 0))]
         + [spec_first, spec_second],
-        [jax.ShapeDtypeStruct(first.shape, BF16), jax.ShapeDtypeStruct(second.shape, BF16)]
-        + [jax.ShapeDtypeStruct(r.shape[1:], BF16) for r in rows],
-        [spec_first, spec_second, spec_rows, spec_rows],
-        [pltpu.VMEM((2 * src * cap, width), F32), pltpu.VMEM((2 * src * cap, width), BF16)],
+        [jax.ShapeDtypeStruct(s, BF16) for s in grown] + [jax.ShapeDtypeStruct(r.shape[1:], BF16) for r in rows],
+        ([pl.BlockSpec(s, lambda e, h: (0, 0, 0, 0)) for s in grown] if fold else [spec_first, spec_second]) + [spec_rows] * 2,
+        [pltpu.VMEM((2 * src * cap, width), F32), pltpu.VMEM((2 * src * cap, width), BF16)]
+        + ([kept] * 3 + [pltpu.SemaphoreType.DMA((2, pairs))] * 2 if fold else []),
         (local, parts), "expert_backward",
-        pl.CostEstimate(flops=10 * work, bytes_accessed=48 << 20, transcendentals=work // width), moving, cid,
+        pl.CostEstimate(flops=10 * work, bytes_accessed=48 << 20, transcendentals=work // width), moving, cid, mate=fold,
     )
 
 
@@ -1127,7 +1184,9 @@
     flat = lambda a: a.reshape(slots // 2, width)
 
     def reduced(a):
-        return lax.psum_scatter(a, "hidden", scatter_dimension=0, tiled=False)
+        ranks = [[2 * y + c for y in range(n_hidden // 2)] for c in range(2)]
+        groups = ranks if a.shape[0] < n_hidden else None
+        return lax.psum_scatter(a, "hidden", scatter_dimension=0, axis_index_groups=groups, tiled=False)
 
     far_grads = [reduced(a) for a in (gf_far, gs_far)]
     near_grads = [reduced(a) for a in (gf_near, gs_near)]
@@ -1139,7 +1198,7 @@
         0, False, packed_rows, *common, list(f0[:8]) + [slotcol], flat(qn0), flat(qf0), cols, (), (), None
     )
     res1 = result_step(1, tokens, f1[0], flat(r1), flat(rf1), cols, slotcol, tuple(res0[:1]), (), None)
-    out, far_grads, res1 = lax.optimization_barrier((tuple(out), far_grads, tuple(res1)))
+    out, far_grads[1] = lax.optimization_barrier((tuple(out), far_grads[1]))
     far_grads[1] = lax.ppermute(far_grads[1], "expert", across)
     out = attention_backward(
         1, True, packed_rows, *common, list(f1[:8]) + [slotcol], flat(qn1), flat(qf1), cols, tuple(out), (), None

time: 507 us -> 501 us (0.988)
  waiting for transfers between devices: 34.9 us -> 22.1 us
  Pallas kernels: 420 us -> 429 us
    ppermute x1, waiting for transfers between devices: 15.6 us -> 0.01 us  [per_device(): far_grads[0] = lax.ppermute(far_grads[0], 'expert', across)]
    pallas_call x14, Pallas kernels: 329 us -> 335 us  [run_kernel(): pl.pallas_call(body, grid=grid, out_shape=tuple(out_shape) + tuple((jax.S...]
  transfers between devices with their start and end apart: 12 -> 12, of which waited for: 3 -> 2; matrix products, arithmetic and copies ran while one was open for 3% -> 3% of each run, Pallas kernels for 65% -> 67%
where the time goes in v6:
time: 501 us; the launch traced here: 493 us
  Pallas kernels  429 us (86%)
  waiting for transfers between devices  22.1 us (4%)
  between operations  15.6 us (3%)
  local copies, waits for them, and re-layouts  13.8 us (3%)
  starting transfers between devices  8 us (2%)
    pallas_call x14, Pallas kernels, run_kernel(): pl.pallas_call(body, grid=grid, out_shape=tuple(out_shape) + tuple((jax.S...  335 us
    pallas_call x1, Pallas kernels, total_step(): pl.pallas_call(functools.partial(total_kernel, sizes, streams), out_shape...  78.4 us
    ppermute x2, waiting for transfers between devices, per_device(): lax.ppermute(a, 'expert', across)  19.3 us
    pallas_call x1, Pallas kernels, scalar_step(): pl.pallas_call(scalar_kernel, out_shape=(jax.ShapeDtypeStruct((2, tokens,...  16 us
  transfers between devices with their start and end apart: 12, of which 2 were waited for; matrix products, arithmetic and copies ran while one was open for 3% of the time, Pallas kernels for 67%

profile of v6, /device:TPU:0, one launch (start us, length us, event | category | flops | bytes accessed | tf_op | source)
XLA Modules:
  0.0 492.8 jit_solution(4554383724020271929)
XLA Ops:
  8.8 4.1 collective-permute-start
  14.4 0.8 copy.69
  15.9 1.6 pad.9.refs_10_.refs_7_
  18.1 1.4 stack.32.refs_0_.refs_3_
  19.5 1.4 stack.39.refs_5_.refs_8_.refs_3_
  20.9 2.0 route_step.1
  23.0 0.8 fusion.1.refs_8_.refs_5_
  23.8 1.3 pad_add_fusion.refs_2_
  25.7 14.2 %attention_forward.2 = (f32[512,512]{1,0:T(8,128)}, bf16[512,512]{1,0:T(8,128)(2,1)}, bf16[512,512]{1,0:T(8,128)(2,1)}, bf16[512,1536]{1,0:T(8,128)(2,1)}, bf16[...) custom-call(bf16[2,512,512]{2,1,0:T(8,128)(2,1)} %refs_0_.11, ...), custom_call_target="tpu_custom_call" | custom-call | flops 2818572288 | bytes 12582912 | tf_op jit(solution)/shard_map/attention_forward/pallas_call | solution.py:221
  40.0 18.7 %collective-permute-done = bf16[2,512,512]{2,1,0:T(8,128)(2,1)} collective-permute-done((bf16[2,512,512]{2,1,0:T(8,128)(2,1)S(1)}, bf16[2,512,512]{2,1,0:T(8,128)(2,1)}, u32[]{:S(2)}, u32[]{:S(2)}) %collective-permute-start) | collective-permute-done | bytes 1048608 | tf_op jit(solution)/shard_map/ppermute | solution.py:1142
  58.8 47.2 %attention_forward.3 = (f32[512,512]{1,0:T(8,128)}, bf16[512,512]{1,0:T(8,128)(2,1)}, bf16[512,512]{1,0:T(8,128)(2,1)}, bf16[512,1536]{1,0:T(8,128)(2,1)}, bf16[...) custom-call(bf16[2,512,512]{2,1,0:T(8,128)(2,1)} %refs_0_.11, ...), custom_call_target="tpu_custom_call" | custom-call | flops 2818572288 | bytes 12582912 | tf_op jit(solution)/shard_map/attention_forward/pallas_call | solution.py:221
  106.6 1.0 copy-done.4
  107.8 33.8 %spread_step.1 = (bf16[2048,512]{1,0:T(8,128)(2,1)}, bf16[2048,512]{1,0:T(8,128)(2,1)}, bf16[2,4,2,128,512]{4,3,2,1,0:T(8,128)(2,1)}) custom-call(s32[2,8,512]{2,1,0:T(8,128)} %get-tuple-element.102.refs_4_.refs_0_.slotrow_ref, bf16[2,512,512]{2,1,0:T(8,128)(2,1)} %refs_1_.9, bf16[2,4,2,128,512]{4,3,2,1,0:T(8,128)(2,1)} %bitcast.82), custom_call_target="tpu_custom_call" | custom-call | flops 4294967296 | bytes 6291456 | tf_op jit(solution)/shard_map/spread_step/pallas_call | solution.py:221
  141.7 29.0 %expert_forward.3 = (bf16[4,2,128,512]{3,2,1,0:T(8,128)(2,1)}, bf16[4,2,128,512]{3,2,1,0:T(8,128)(2,1)}, bf16[2,4,2,128,512]{4,3,2,1,0:T(8,128)(2,1)}) custom-call(bf16[2,4,2,128,512]{4,3,2,1,0:T(8,128)(2,1)} %get-tuple-element.106.refs_0_, bf16[2,4,2,128,512]{4,3,2,1,0:T(8,128)(2,1)} %get-tuple-element.109.refs_1_, bf16[4,2,512,512]{3,2,1,0:T(8,128)(2,1)} %bitcast.66, ...), custom_call_target="tpu_custom_call" | custom-call | flops 8589934592 | bytes 25165824 | tf_op jit(solution)/shard_map/expert_forward/pallas_call | solution.py:221
  170.7 28.1 %expert_forward.2 = (bf16[4,2,128,512]{3,2,1,0:T(8,128)(2,1)}, bf16[4,2,128,512]{3,2,1,0:T(8,128)(2,1)}, bf16[2,4,2,128,512]{4,3,2,1,0:T(8,128)(2,1)}) custom-call(bf16[2,4,2,128,512]{4,3,2,1,0:T(8,128)(2,1)} %get-tuple-element.106.refs_0_, bf16[2,4,2,128,512]{4,3,2,1,0:T(8,128)(2,1)} %get-tuple-element.109.refs_1_, bf16[4,2,512,512]{3,2,1,0:T(8,128)(2,1)} %bitcast.70, ...), custom_call_target="tpu_custom_call" | custom-call | flops 8589934592 | bytes 25165824 | tf_op jit(solution)/shard_map/expert_forward/pallas_call | solution.py:221
  198.8 6.8 %reading_step.1 = f32[4,2,2,2,8,128]{5,4,3,2,1,0:T(8,128)} custom-call(bf16[4,2,128,512]{3,2,1,0:T(8,128)(2,1)} %get-tuple-element.116.refs_0_.refs_8_, bf16[4,2,128,512]{3,2,1,0:T(8,128)(2,1)} %get-tuple-element.117.refs_1_.refs_10_, bf16[4,2,128,512]{3,2,1,0:T(8,128)(2,1)} %get-tuple-element.118.refs_2_.refs_9_, ...), custom_call_target="tpu_custom_call" | custom-call | flops 1000000000 | bytes 8388608 | tf_op jit(solution)/shard_map/reading_step/pallas_call | solution.py:221
  205.6 16.0 %scalar_step.1 = (f32[2,512,8]{2,1,0:T(8,128)}, f32[4,2,4,8,128]{4,3,2,1,0:T(8,128)}) custom-call(f32[4,2,4,8,128]{4,3,2,1,0:T(8,128)} %bitcast.54, f32[8,512]{1,0:T(8,128)} %get-tuple-element.120.rowsc0_ref, f32[8,512]{1,0:T(8,128)} %get-tuple-element.121.rowsc1_ref, s32[2,8,512]{2,1,0:T(8,128)} %get-tuple-element.102.refs_4_.refs_0_.slotrow_ref), custom_call_target="tpu_custom_call" | custom-call | flops 1000000000 | bytes 1048576 | tf_op jit(solution)/shard_map/scalar_step/pallas_call | solution.py:667
  221.7 38.0 %expert_backward.2 = (bf16[4,2,512,512]{3,2,1,0:T(8,128)(2,1)}, bf16[4,2,512,512]{3,2,1,0:T(8,128)(2,1)}, bf16[4,2,128,512]{3,2,1,0:T(8,128)(2,1)}, bf16[4,2,128...) custom-call(bf16[2,4,2,128,512]{4,3,2,1,0:T(8,128)(2,1)} %get-tuple-, ...), custom_call_target="tpu_custom_call" | custom-call | flops 21474836480 | bytes 50331648 | tf_op jit(solution)/shard_map/expert_backward/pallas_call | solution.py:221
  260.6 44.4 %expert_backward.3 = (bf16[2,2,512,512]{3,2,1,0:T(8,128)(2,1)}, bf16[2,2,512,512]{3,2,1,0:T(8,128)(2,1)}, bf16[4,2,128,512]{3,2,1,0:T(8,128)(2,1)}, bf16[4,2,128...) custom-call(bf16[2,4,2,128,512]{4,3,2,1,0:T(8,128)(2,1)} %get-tuple-, ...), custom_call_target="tpu_custom_call" | custom-call | flops 21474836480 | bytes 50331648 | tf_op jit(solution)/shard_map/expert_backward/pallas_call | solution.py:221
  305.8 29.5 %result_step.2 = (bf16[2,512,512]{2,1,0:T(8,128)(2,1)}, f32[8,512]{1,0:T(8,128)}, bf16[4,2,128,512]{3,2,1,0:T(8,128)(2,1)}, bf16[4,2,128,512]{3,2,1,0:T(8,128)(2,1)}) custom-call(bf16[2,512,512]{2,1,0:T(8,128)(2,1)} %refs_0_.11, f32[512,512]{1,0:T(8,128)} %get-tuple-element.129.refs_1_.refs_8_, bf16[1024,512]{1,0:T(8,128)(2,1)} %bitcast.87, ...), custom_call_target="tpu_custom_call" | custom-call | flops 2147483648 | bytes 5242880 | tf_op jit(solution)/shard_map/result_step/pallas_call | solution.py:221
  335.3 2.7 collective-permute-start.2
  338.0 22.1 %attention_backward.2 = (f32[2,512,512]{2,1,0:T(8,128)}, f32[512,1536]{1,0:T(8,128)}, f32[512,1536]{1,0:T(8,128)}, f32[256,512]{1,0:T(8,128)}, f32[128,512]{1,0:T(8,128)}, /*index=5*/f32[8,512]{1,0:T(8,128)}) custom-call(bf16[2,512,512]{2,1,0:T(8,128)(2,1)} %refs_0_.11, bf16[2,512,512]{2,1,0:T(8,128)(2,1)} %refs_1_.9, s32[2,512,8]{2,1,0:T(8,128)} %pad_add_fusion.refs_2_, ...), custom_call_target="tpu_custom_call" | custom-call | flops 4563402752 | bytes 25165824 | tf_op jit(solution)/shard_map/attention_backward/pallas_call | solution.py:221
  360.6 8.4 %result_step.3 = (bf16[2,512,512]{2,1,0:T(8,128)(2,1)}, f32[8,512]{1,0:T(8,128)}) custom-call(bf16[2,512,512]{2,1,0:T(8,128)(2,1)} %refs_0_.11, f32[512,512]{1,0:T(8,128)} %get-tuple-element.105.refs_1_.refs_8_, bf16[1024,512]{1,0:T(8,128)(2,1)} %bitcast.85, bf16[1024,512]{1,0:T(8,128)(2,1)} %bitcast.86, ...), custom_call_target="tpu_custom_call", output_to_operand_aliasing={{0}: (6, {})} | custom-call | flops 2147483648 | bytes 5242880 | tf_op jit(solution)/shard_map/result_step/pallas_call | solution.py:221
  369.0 0.7 add.28
  369.7 23.4 %attention_backward.3 = (f32[2,512,512]{2,1,0:T(8,128)}, bf16[3584,512]{1,0:T(8,128)(2,1)}, f32[8,512]{1,0:T(8,128)}) custom-call(bf16[2,512,512]{2,1,0:T(8,128)(2,1)} %refs_0_.11, bf16[2,512,512]{2,1,0:T(8,128)(2,1)} %refs_1_.9, s32[2,512,8]{2,1,0:T(8,128)} %pad_add_fusion.refs_2_, ...), custom_call_target="tpu_custom_call", output_to_operand_aliasing={{0}: (25, {})} | custom-call | flops 4563402752 | bytes 25165824 | tf_op jit(solution)/shard_map/attention_backward/pallas_call | solution.py:221
  393.1 1.3 pad_maximum_fusion.small_ref
  394.5 78.4 %total_step.1 = (bf16[3584,512]{1,0:T(8,128)(2,1)}, f32[16,512]{1,0:T(8,128)}) custom-call(bf16[3584,512]{1,0:T(8,128)(2,1)} %get-tuple-element.170.pack_ref, f32[16,512]{1,0:T(8,128)} %pad_maximum_fusion.small_ref), custom_call_target="tpu_custom_call" | custom-call | tf_op jit(solution)/shard_map/total_step/pallas_call | solution.py:1053
  472.9 1.2 slice.39
  474.1 1.5 fusion.4
  475.6 0.9 copy-done
  476.9 7.6 %unpack_step.1 = (f32[512,1536]{1,0:T(8,128)}, f32[3,512,512]{2,1,0:T(8,128)}, f32[2,512,512]{2,1,0:T(8,128)}, f32[2,512,512]{2,1,0:T(8,128)}, f32[64,512]{1,0:T...) custom-call(bf16[7,512,512]{2,1,0:T(8,128)(2,1)} %bitcast.49, bf16[2,512,512]{2,1,0:T(8,128)(2,1)} %bitcast.50, ...), custom_call_target="tpu_custom_call" | custom-call | bytes 20971520 | tf_op jit(solution)/shard_map/unpack_step/pallas_call | solution.py:221
  484.5 1.0 copy.74
  (72 shorter events, 7.7 us)
Async XLA Ops:
  7.2 1.6 copy-start.2
  7.2 5.7 %copy-start.10 = (s32[2,2,256]{2,1,0:T(2,128)S(1)}, s32[2,2,256]{2,1,0:T(2,128)}, u32[]{:S(2)}) copy-start(s32[2,2,256]{2,1,0:T(2,128)} %param.24) | copy-start | bytes 12292
  7.2 6.7 %copy-start.11 = (s32[2,512]{1,0:T(2,128)S(1)}, s32[2,512]{1,0:T(2,128)}, u32[]{:S(2)}) copy-start(s32[2,512]{1,0:T(2,128)} %param.25) | copy-start | bytes 12292
  7.2 6.8 %copy-start.9 = (bf16[512,24]{0,1:T(8,128)(2,1)S(1)}, bf16[512,24]{0,1:T(8,128)(2,1)}, u32[]{:S(2)}) copy-start(bf16[512,24]{0,1:T(8,128)(2,1)} %param.28) | copy-start | bytes 73732
  7.2 6.9 %copy-start.7 = (bf16[512,64]{0,1:T(8,128)(2,1)S(1)}, bf16[512,64]{0,1:T(8,128)(2,1)}, u32[]{:S(2)}) copy-start(bf16[512,64]{0,1:T(8,128)(2,1)} %param.30) | copy-start | bytes 196612
  7.2 7.0 %copy-start.8 = (bf16[512,64]{0,1:T(8,128)(2,1)S(1)}, bf16[512,64]{0,1:T(8,128)(2,1)}, u32[]{:S(2)}) copy-start(bf16[512,64]{0,1:T(8,128)(2,1)} %param.31) | copy-start | bytes 196612
  7.2 7.1 %copy-start.12 = (bf16[512,16]{0,1:T(8,128)(2,1)S(1)}, bf16[512,16]{0,1:T(8,128)(2,1)}, u32[]{:S(2)}) copy-start(bf16[512,16]{0,1:T(8,128)(2,1)} %param.35) | copy-start | bytes 49156
  7.3 7.9 %copy-start.13 = (s32[2,512,4]{1,2,0:T(4,128)S(1)}, s32[2,512,4]{1,2,0:T(4,128)}, u32[]{:S(2)}) copy-start(s32[2,512,4]{1,2,0:T(4,128)} %param.22) | copy-start | bytes 49156
  7.3 8.3 %copy-start.6 = (s32[2,512,2]{1,2,0:T(2,128)S(1)}, s32[2,512,2]{1,2,0:T(2,128)}, u32[]{:S(2)}) copy-start(s32[2,512,2]{1,2,0:T(2,128)} %param.23) | copy-start | bytes 24580
  7.3 134.4 %all-gather.13.cloned.1.call-start = ((), (), s32[]{:S(2)}) async-start(), calls=%async_computation.10 | async-start | bytes 5242880 | tf_op jit(solution)/shard_map/all_gather | solution.py:1140
  8.0 133.7 %all-gather.15.cloned.1.call-start = ((), (), s32[]{:S(2)}) async-start(), calls=%async_computation.11 | async-start | bytes 5242880 | tf_op jit(solution)/shard_map/all_gather | solution.py:1140
  8.8 161.9 %all-gather.9.cloned.1.call-start = ((), (), s32[]{:S(2)}) async-start(), calls=%async_computation.8 | async-start | bytes 5242880 | tf_op jit(solution)/shard_map/all_gather | solution.py:1140
  8.8 49.8 %collective-permute-start = (bf16[2,512,512]{2,1,0:T(8,128)(2,1)S(1)}, bf16[2,512,512]{2,1,0:T(8,128)(2,1)}, u32[]{:S(2)}, u32[]{:S(2)}) collective-permute-start(bf16[2,512,512]{2,1,0:T(8,128)(2,1)S(1)} %copy-done.2), channel_id=1, source_target_pairs={{0,16},{4,20},{8,24},{12,28},{16,0},{20,4},{24,8},{28,12},{1,17},{... | collective-permute-start | bytes 3145736 | tf_op jit(solution)/shard_map/ppermute | solution.py:1142
  25.7 33.0 %copy-start.3 = (bf16[2,512,512]{2,1,0:T(8,128)(2,1)S(1)}, bf16[2,512,512]{2,1,0:T(8,128)(2,1)}, u32[]{:S(2)}) copy-start(bf16[2,512,512]{2,1,0:T(8,128)(2,1)} %param.37) | copy-start | bytes 3145732
  58.7 112.1 %all-gather.11.cloned.1.call-start = ((), (), s32[]{:S(2)}) async-start(), calls=%async_computation.9 | async-start | bytes 5242880 | tf_op jit(solution)/shard_map/all_gather | solution.py:1140
  58.7 47.9 %collective-permute-start.1 = (bf16[2,512,512]{2,1,0:T(8,128)(2,1)S(1)}, bf16[2,512,512]{2,1,0:T(8,128)(2,1)S(1)}, u32[]{:S(2)}, u32[]{:S(2)}) collective-permute-start(bf16[2,512,512]{2,1,0:T(8,128)(2,1)S(1)} %copy-done.3), channel_id=1, source_target_pairs={{0,16},{4,20},{8,24},{12,28},{16,0},{20,4},{24,8},{28,12},{1,17},{... | collective-permute-start | bytes 3145736 | tf_op jit(solution)/shard_map/ppermute | solution.py:1142
  106.6 1.0 copy-start.4
  107.6 227.7 %reduce-scatter.5.cloned.1.call-start = ((), (), s32[]{:S(2)}) async-start(), calls=%async_computation.4 | async-start | bytes 5242880 | tf_op jit(solution)/shard_map/reduce_scatter | solution.py:1189
  259.7 100.4 %reduce-scatter.7.cloned.1.call-start = ((), (), s32[]{:S(2)}) async-start(), calls=%async_computation.5 | async-start | bytes 5242880 | tf_op jit(solution)/shard_map/reduce_scatter | solution.py:1189
  260.3 215.2 %reduce-scatter.9.cloned.1.call-start = ((), (), s32[]{:S(2)}) async-start(), calls=%async_computation.6 | async-start | bytes 3145728 | tf_op jit(solution)/shard_map/reduce_scatter | solution.py:1189
  305.0 170.5 %reduce-scatter.11.cloned.1.call-start = ((), (), s32[]{:S(2)}) async-start(), calls=%async_computation.7 | async-start | bytes 3145728 | tf_op jit(solution)/shard_map/reduce_scatter | solution.py:1189
  335.3 140.3 %collective-permute-start.2 = (bf16[2,512,512]{2,1,0:T(8,128)(2,1)}, bf16[2,512,512]{2,1,0:T(8,128)(2,1)S(1)}, u32[]{:S(2)}, u32[]{:S(2)}) collective-permute-start(bf16[2,512,512]{2,1,0:T(8,128)(2,1)} %bitcast.75), channel_id=1, source_target_pairs={{0,16},{4,20},{8,24},{12,28},{16,0},{20,4},{24,8},{28,12},{1,17},{... | collective-permute-start | bytes 3145736 | tf_op jit(solution)/shard_map/ppermute | solution.py:1196
  360.1 115.5 %collective-permute-start.3 = (bf16[2,512,512]{2,1,0:T(8,128)(2,1)}, bf16[2,512,512]{2,1,0:T(8,128)(2,1)S(1)}, u32[]{:S(2)}, u32[]{:S(2)}) collective-permute-start(bf16[2,512,512]{2,1,0:T(8,128)(2,1)} %bitcast.76), channel_id=1, source_target_pairs={{0,16},{4,20},{8,24},{12,28},{16,0},{20,4},{24,8},{28,12},{1,17},{... | collective-permute-start | bytes 3145736 | tf_op jit(solution)/shard_map/ppermute | solution.py:1202
  360.5 8.4 %copy-start.14 = (f32[8,512]{1,0:T(8,128)S(1)}, f32[8,512]{1,0:T(8,128)}, u32[]{:S(2)}) copy-start(f32[8,512]{1,0:T(8,128)} %get-tuple-element.172) | copy-start | bytes 49156
  475.6 1.0 copy-start
  475.6 1.3 copy-start.1
  476.9 7.6 %copy-start.5 = (bf16[2,512,512]{2,1,0:T(8,128)(2,1)S(1)}, bf16[2,512,512]{2,1,0:T(8,128)(2,1)}, u32[]{:S(2)}) copy-start(bf16[2,512,512]{2,1,0:T(8,128)(2,1)} %get-tuple-element.215) | copy-start | bytes 3145732
Sparse Core Ops, SparseCore 0:
  9.7 37.1 all-gather.12
  48.4 34.4 all-gather.14
  84.5 34.4 all-gather.8
  121.1 34.4 all-gather.10
  259.9 46.4 reduce-scatter.4
  308.9 44.5 reduce-scatter.6
  355.7 31.8 reduce-scatter.8
  389.9 38.8 reduce-scatter.10

commit v7 on v6

--- a/solution.py
+++ b/solution.py
@@ -397,7 +397,25 @@
     return square, inner
 
 
-def expert_forward_kernel(rows0_ref, rows1_ref, first_ref, second_ref, out0_ref, out1_ref, total):
+def read_rows(low, grad, vec_ref):
+    cap, width = low.shape
+    halt = split_three(jnp.broadcast_to(vec_ref[4:5, :], (8, width)))
+    ones = jnp.ones((8, width), BF16)
+    sub8 = lax.broadcasted_iota(jnp.int32, (8, cap), 0)
+    stop = join_three(mm_nt(halt, low))
+    prod = low.astype(F32) * grad.astype(F32)
+    high = prod.astype(BF16)
+    rest = (prod - high.astype(F32)).astype(BF16)
+    pull = mm_nt(ones, high) + mm_nt(ones, rest)
+    return jnp.where(sub8 == 0, stop, pull)
+
+
+def expert_forward_kernel(rows0_ref, rows1_ref, first_ref, second_ref, *refs):
+    total = refs[-1]
+    if len(refs) == 3:
+        out0_ref, out1_ref = refs[:2]
+    else:
+        near_ref, near_grad_ref, far_grad_ref, vec_ref, out0_ref, out1_ref, scal_ref = refs[:-1]
     part = pl.program_id(1)
     _, src, _, cap, width = rows0_ref.shape
     half = src * cap
@@ -419,83 +437,78 @@
     def _():
         out0_ref[...] = total[:half, :].astype(BF16).reshape(out0_ref.shape)
         out1_ref[...] = total[half:, :].astype(BF16).reshape(out1_ref.shape)
-
-
-def expert_forward(kind, rows, first, second, moving, cid):
+        if len(refs) > 3:
+            for s in range(src):
+                scal_ref[s, 0, 0] = read_rows(near_ref[s, 0], near_grad_ref[0, s, 0], vec_ref)
+                mine = total[half + s * cap : half + (s + 1) * cap, :].astype(BF16)
+                scal_ref[s, 1, 0] = read_rows(mine, far_grad_ref[0, s, 0], vec_ref)
+
+
+def expert_forward(kind, rows, first, second, moving, cid, read=()):
     _, src, local, cap, width = rows[0].shape
     parts, _, _, hid = first.shape
     spec_in = pl.BlockSpec((1, src, 1, cap, width), lambda e, h: (kind, 0, e, 0, 0))
     spec_rows = pl.BlockSpec((src, 1, cap, width), lambda e, h: (0, e, 0, 0))
     work = 2 * src * local * cap * width * hid * parts
+    args, more, shapes, specs = (), [], [], []
+    if read:
+        near, grad, vec = read
+        spec_grad = lambda k: pl.BlockSpec((1, src, 1, cap, width), lambda e, h: (k, 0, e, 0, 0))
+        args = (near, grad, grad, vec)
+        more = [spec_rows, spec_grad(0), spec_grad(1), pl.BlockSpec(vec.shape, lambda e, h: (0, 0))]
+        shapes = [jax.ShapeDtypeStruct((src, 2, local, 8, cap), F32)]
+        specs = [pl.BlockSpec((src, 2, 1, 8, cap), lambda e, h: (0, 0, e, 0, 0))]
     return run_kernel(
-        expert_forward_kernel, (*rows, first, second),
+        expert_forward_kernel, (*rows, first, second, *args),
         [
             spec_in, spec_in,
             pl.BlockSpec((1, 1, width, hid), lambda e, h: (h, e, 0, 0)),
             pl.BlockSpec((1, 1, hid, width), lambda e, h: (h, e, 0, 0)),
-        ],
-        [jax.ShapeDtypeStruct(r.shape[1:], BF16) for r in rows], [spec_rows] * 2,
+        ] + more,
+        [jax.ShapeDtypeStruct(r.shape[1:], BF16) for r in rows] + shapes, [spec_rows] * 2 + specs,
         [pltpu.VMEM((2 * src * cap, width), F32)], (local, parts), "expert_forward",
         pl.CostEstimate(flops=4 * work, bytes_accessed=24 << 20, transcendentals=work // width), moving, cid,
     )
 
 
-def reading_kernel(*refs):
-    outs, grads = refs[:4], refs[4:8]
-    vec_ref, scal_ref = refs[8:]
-    src, _, cap, width = outs[0].shape
-    halt = split_three(jnp.broadcast_to(vec_ref[4:5, :], (8, width)))
-    ones = jnp.ones((8, width), BF16)
-    sub8 = lax.broadcasted_iota(jnp.int32, (8, cap), 0)
-    for kind in range(2):
-        for m in range(2):
-            for s in range(src):
-                low = outs[2 * kind + m][s, 0]
-                stop = join_three(mm_nt(halt, low))
-                prod = low.astype(F32) * grads[2 * kind + m][0, s, 0].astype(F32)
-                high = prod.astype(BF16)
-                rest = (prod - high.astype(F32)).astype(BF16)
-                pull = mm_nt(ones, high) + mm_nt(ones, rest)
-                scal_ref[s, m, kind, 0] = jnp.where(sub8 == 0, stop, pull)
-
-
-def reading_step(outs, grads, vec):
-    src, local, cap, width = outs[0].shape
+def reading_kernel(near_ref, far_ref, near_grad_ref, far_grad_ref, vec_ref, scal_ref):
+    for kind, (ref, grad_ref) in enumerate(((near_ref, near_grad_ref), (far_ref, far_grad_ref))):
+        for s in range(ref.shape[0]):
+            scal_ref[s, kind, 0] = read_rows(ref[s, 0], grad_ref[0, s, 0], vec_ref)
+
+
+def reading_step(near, far, grad, vec):
+    src, local, cap, width = near.shape
     spec_rows = pl.BlockSpec((src, 1, cap, width), lambda e: (0, e, 0, 0))
     spec_grad = lambda kind: pl.BlockSpec((1, src, 1, cap, width), lambda e: (kind, 0, e, 0, 0))
     return run_kernel(
-        reading_kernel, (*outs, *grads, *grads, vec),
-        [spec_rows] * 4 + [spec_grad(0)] * 2 + [spec_grad(1)] * 2 + [pl.BlockSpec(vec.shape, lambda e: (0, 0))],
-        [jax.ShapeDtypeStruct((src, 2, 2, local, 8, cap), F32)],
-        [pl.BlockSpec((src, 2, 2, 1, 8, cap), lambda e: (0, 0, 0, e, 0, 0))], (), (local,), "reading_step",
-        pl.CostEstimate(flops=10**9, bytes_accessed=8 << 20, transcendentals=0),
-    )[0].reshape(src, 2, 2 * local, 8, cap)
-
-
-def add_cores(grown, gfirst_ref, gsecond_ref, keep, away, land, send_sem, recv_sem):
+        reading_kernel, (near, far, grad, grad, vec),
+        [spec_rows] * 2 + [spec_grad(0), spec_grad(1), pl.BlockSpec(vec.shape, lambda e: (0, 0))],
+        [jax.ShapeDtypeStruct((src, 2, local, 8, cap), F32)],
+        [pl.BlockSpec((src, 2, 1, 8, cap), lambda e: (0, 0, e, 0, 0))], (), (local,), "reading_step",
+        pl.CostEstimate(flops=10**9, bytes_accessed=4 << 20, transcendentals=0),
+    )[0]
+
+
+def add_cores(grown, gfirst_ref, gsecond_ref, stash, land, send_sem, recv_sem):
     step = pl.program_id(0) * pl.num_programs(1) + pl.program_id(1)
     steps = pl.num_programs(0) * pl.num_programs(1)
+    core = lax.rem(lax.axis_index("hidden"), 2)
     pair = lax.div(step, 2)
-    owned = lax.rem(step, 2) == lax.rem(lax.axis_index("hidden"), 2)
+    for i in range(2):
+        stash[i][step] = grown[i]
 
     def crossing(k):
         return [
             pltpu.make_async_remote_copy(
-                away[i].at[k], land[i].at[k], send_sem.at[i, k], recv_sem.at[i, k],
+                stash[i].at[2 * k + 1 - core], land[i].at[k], send_sem.at[i, k], recv_sem.at[i, k],
                 device_id=other_core(), device_id_type=pl.DeviceIdType.MESH,
             )
             for i in range(2)
         ]
 
-    @pl.when(owned)
-    def _():
-        for i in range(2):
-            keep[i][pair] = grown[i]
-
-    @pl.when(jnp.logical_not(owned))
-    def _():
-        for i in range(2):
-            away[i][pair] = grown[i]
+    @pl.when(lax.rem(step, 2) != core)
+    def _():
         for c in crossing(pair):
             c.start()
 
@@ -503,8 +516,8 @@
         for c in crossing(k):
             c.wait()
         local, y = lax.div(k, gfirst_ref.shape[0]), lax.rem(k, gfirst_ref.shape[0])
-        for ref, mine, got in ((gfirst_ref, keep[0], land[0]), (gsecond_ref, keep[1], land[1])):
-            ref[y, local] = (mine[k].astype(F32) + got[k].astype(F32)).astype(BF16)
+        for ref, mine, got in ((gfirst_ref, stash[0], land[0]), (gsecond_ref, stash[1], land[1])):
+            ref[y, local] = (mine[2 * k + core].astype(F32) + got[k].astype(F32)).astype(BF16)
 
     @pl.when((lax.rem(step, 2) == 0) & (step >= 2))
     def _():
@@ -574,7 +587,7 @@
     fold = kind == 0
     grown = [((parts // 2,) + a.shape[1:] if fold else a.shape) for a in (first, second)]
     pairs = local * parts // 2
-    kept = [pltpu.VMEM((pairs,) + a.shape[2:], BF16) for a in (first, second)]
+    stash, kept = [[pltpu.VMEM((n,) + a.shape[2:], BF16) for a in (first, second)] for n in (2 * pairs, pairs)]
     return run_kernel(
         functools.partial(expert_backward_kernel, fold), (*rows, *grads, ab, vec, first, second),
         [spec_in] * 4
@@ -583,21 +596,27 @@
         [jax.ShapeDtypeStruct(s, BF16) for s in grown] + [jax.ShapeDtypeStruct(r.shape[1:], BF16) for r in rows],
         ([pl.BlockSpec(s, lambda e, h: (0, 0, 0, 0)) for s in grown] if fold else [spec_first, spec_second]) + [spec_rows] * 2,
         [pltpu.VMEM((2 * src * cap, width), F32), pltpu.VMEM((2 * src * cap, width), BF16)]
-        + ([kept] * 3 + [pltpu.SemaphoreType.DMA((2, pairs))] * 2 if fold else []),
+        + ([stash, kept] + [pltpu.SemaphoreType.DMA((2, pairs))] * 2 if fold else []),
         (local, parts), "expert_backward",
         pl.CostEstimate(flops=10 * work, bytes_accessed=48 << 20, transcendentals=work // width), moving, cid, mate=fold,
     )
 
 
-def scalar_kernel(scal_ref, rowsc0_ref, rowsc1_ref, slotrow_ref, cols_ref, ab_ref, got, sent, got2, send_sem, recv_sem, send_sem2, recv_sem2):
-    src, micros, local, _, cap = scal_ref.shape
+def scalar_kernel(
+    scal0_ref, scal1_ref, rowsc0_ref, rowsc1_ref, slotrow_ref, cols_ref, ab_ref,
+    got0, got1, sent, got2, send_sem, recv_sem, send_sem1, recv_sem1, send_sem2, recv_sem2,
+):
+    src, local, _, cap = scal0_ref.shape
+    micros = 2
+    got = (got0, got1)
     tokens = rowsc0_ref.shape[1]
     me = group_of()[0]
     group_greet()
-    moves = group_copies(scal_ref, got, send_sem, recv_sem)
+    moves = group_copies(scal0_ref, got0, send_sem, recv_sem) + group_copies(scal1_ref, got1, send_sem1, recv_sem1)
     for c in moves:
         c.start()
-    got[me] = scal_ref[me]
+    got0[me] = scal0_ref[me]
+    got1[me] = scal1_ref[me]
     for c in moves:
         c.wait()
     spot = lax.broadcasted_iota(jnp.int32, (cap, tokens), 0)
@@ -617,7 +636,7 @@
         carry = list(carry)
         for which in range(local):
             for m in range(micros):
-                values = split_three(got[s, m, which])
+                values = split_three(got[m][s, which])
                 for i, p in enumerate(onehot(m, s, which)):
                     carry[2 * m + i] = carry[2 * m + i] + mm(values, p)
         return tuple(carry)
@@ -663,17 +682,19 @@
 def scalar_step(scal, rowsc, slotrow):
     vmem = pl.BlockSpec(memory_space=pltpu.VMEM)
     tokens = rowsc[0].shape[1]
-    peers = scal.shape[0] - 1
+    src = scal[0].shape[0]
+    both = (src, 2) + scal[0].shape[1:]
     return pl.pallas_call(
         scalar_kernel,
-        out_shape=(jax.ShapeDtypeStruct((2, tokens, 8), F32), jax.ShapeDtypeStruct(scal.shape, F32)),
-        in_specs=[vmem] * 4,
+        out_shape=(jax.ShapeDtypeStruct((2, tokens, 8), F32), jax.ShapeDtypeStruct(both, F32)),
+        in_specs=[vmem] * 5,
         out_specs=[vmem] * 2,
-        scratch_shapes=[pltpu.VMEM(scal.shape, F32)] * 3 + [pltpu.SemaphoreType.DMA((peers,))] * 4,
+        scratch_shapes=[pltpu.VMEM(scal[0].shape, F32)] * 2 + [pltpu.VMEM(both, F32)] * 2
+        + [pltpu.SemaphoreType.DMA((src - 1,))] * 6,
         compiler_params=pltpu.CompilerParams(collective_id=0, has_side_effects=True),
         cost_estimate=pl.CostEstimate(flops=10**9, bytes_accessed=1 << 20, transcendentals=tokens),
         name="scalar_step",
-    )(scal, *rowsc, slotrow)
+    )(*scal, *rowsc, slotrow)
 
 
 def result_kernel(has_old, *refs):
@@ -1170,9 +1191,9 @@
     gs0, gs1, n1 = spread_step(slotrow, grad_out, slots, [n1_out.reshape(shape)], 3)
     rows = (n0, n1)
     y0, y1, g1 = expert_forward(0, rows, near_first, near_second, [gs1.reshape(shape)], 4)
-    far0, far1, g0 = expert_forward(1, rows, far_first, far_second, [gs0.reshape(shape)], 1)
+    far0, far1, scal1, g0 = expert_forward(1, rows, far_first, far_second, [gs0.reshape(shape)], 1, (y1, g1, vec))
     grads = (g0, g1)
-    scal = reading_step((y0, y1, far0, far1), grads, vec)
+    scal = [a.reshape(group, 2 * per, 8, capacity) for a in (reading_step(y0, far0, g0, vec), scal1)]
     cols, ab = scalar_step(scal, (f0[8], f1[8]), slotrow)
     gf_far, gs_far, bf0, bf1, r0, rf0, r1 = expert_backward(
         1, rows, grads, ab, vec, far_first, far_second, [y0, far0, y1], 9

time: 501 us -> 499 us (level)
  transfers between devices with their start and end apart: 12 -> 12, of which waited for: 2 -> 2; matrix products, arithmetic and copies ran while one was open for 3% -> 3% of each run, Pallas kernels for 67% -> 68%
where the time goes in v7:
time: 499 us; the launch traced here: 491 us
  Pallas kernels  427 us (86%)
  waiting for transfers between devices  22.1 us (4%)
  between operations  15.6 us (3%)
  local copies, waits for them, and re-layouts  13.8 us (3%)
  starting transfers between devices  8.02 us (2%)
    pallas_call x14, Pallas kernels, run_kernel(): pl.pallas_call(body, grid=grid, out_shape=tuple(out_shape) + tuple((jax.S...  332 us
    pallas_call x1, Pallas kernels, total_step(): pl.pallas_call(functools.partial(total_kernel, sizes, streams), out_shape...  79.5 us
    ppermute x2, waiting for transfers between devices, per_device(): lax.ppermute(a, 'expert', across)  19.3 us
    pallas_call x1, Pallas kernels, scalar_step(): pl.pallas_call(scalar_kernel, out_shape=(jax.ShapeDtypeStruct((2, tokens,...  16.1 us
  transfers between devices with their start and end apart: 12, of which 2 were waited for; matrix products, arithmetic and copies ran while one was open for 3% of the time, Pallas kernels for 68%

profile of v7, /device:TPU:0, one launch (start us, length us, event | category | flops | bytes accessed | tf_op | source)
XLA Modules:
  0.0 491.0 jit_solution(5944931959261586584)
XLA Ops:
  8.8 4.1 collective-permute-start
  14.4 0.8 copy.69
  15.9 1.6 pad.9.refs_10_.refs_7_
  18.1 1.4 stack.32.refs_0_.refs_3_
  19.5 1.4 stack.39.refs_5_.refs_7_.refs_4_.refs_3_
  20.9 2.0 route_step.1
  23.0 0.8 fusion.1.refs_8_.refs_5_
  23.8 1.3 pad_add_fusion.refs_2_
  25.7 14.2 %attention_forward.2 = (f32[512,512]{1,0:T(8,128)}, bf16[512,512]{1,0:T(8,128)(2,1)}, bf16[512,512]{1,0:T(8,128)(2,1)}, bf16[512,1536]{1,0:T(8,128)(2,1)}, bf16[...) custom-call(bf16[2,512,512]{2,1,0:T(8,128)(2,1)} %refs_0_.11, ...), custom_call_target="tpu_custom_call" | custom-call | flops 2818572288 | bytes 12582912 | tf_op jit(solution)/shard_map/attention_forward/pallas_call | solution.py:221
  40.0 18.7 %collective-permute-done = bf16[2,512,512]{2,1,0:T(8,128)(2,1)} collective-permute-done((bf16[2,512,512]{2,1,0:T(8,128)(2,1)S(1)}, bf16[2,512,512]{2,1,0:T(8,128)(2,1)}, u32[]{:S(2)}, u32[]{:S(2)}) %collective-permute-start) | collective-permute-done | bytes 1048608 | tf_op jit(solution)/shard_map/ppermute | solution.py:1163
  58.8 47.2 %attention_forward.3 = (f32[512,512]{1,0:T(8,128)}, bf16[512,512]{1,0:T(8,128)(2,1)}, bf16[512,512]{1,0:T(8,128)(2,1)}, bf16[512,1536]{1,0:T(8,128)(2,1)}, bf16[...) custom-call(bf16[2,512,512]{2,1,0:T(8,128)(2,1)} %refs_0_.11, ...), custom_call_target="tpu_custom_call" | custom-call | flops 2818572288 | bytes 12582912 | tf_op jit(solution)/shard_map/attention_forward/pallas_call | solution.py:221
  106.6 1.0 copy-done.4
  107.8 33.9 %spread_step.1 = (bf16[2048,512]{1,0:T(8,128)(2,1)}, bf16[2048,512]{1,0:T(8,128)(2,1)}, bf16[2,4,2,128,512]{4,3,2,1,0:T(8,128)(2,1)}) custom-call(s32[2,8,512]{2,1,0:T(8,128)} %get-tuple-element.103.refs_4_.refs_0_.slotrow_ref, bf16[2,512,512]{2,1,0:T(8,128)(2,1)} %refs_1_.9, bf16[2,4,2,128,512]{4,3,2,1,0:T(8,128)(2,1)} %bitcast.83), custom_call_target="tpu_custom_call" | custom-call | flops 4294967296 | bytes 6291456 | tf_op jit(solution)/shard_map/spread_step/pallas_call | solution.py:221
  141.8 29.0 %expert_forward.2 = (bf16[4,2,128,512]{3,2,1,0:T(8,128)(2,1)}, bf16[4,2,128,512]{3,2,1,0:T(8,128)(2,1)}, bf16[2,4,2,128,512]{4,3,2,1,0:T(8,128)(2,1)}) custom-call(bf16[2,4,2,128,512]{4,3,2,1,0:T(8,128)(2,1)} %get-tuple-element.107.refs_0_, bf16[2,4,2,128,512]{4,3,2,1,0:T(8,128)(2,1)} %get-tuple-element.110.refs_1_, bf16[4,2,512,512]{3,2,1,0:T(8,128)(2,1)} %bitcast.67, ...), custom_call_target="tpu_custom_call" | custom-call | flops 8589934592 | bytes 25165824 | tf_op jit(solution)/shard_map/expert_forward/pallas_call | solution.py:221
  170.8 28.6 %expert_forward.3 = (bf16[4,2,128,512]{3,2,1,0:T(8,128)(2,1)}, bf16[4,2,128,512]{3,2,1,0:T(8,128)(2,1)}, f32[4,2,2,8,128]{4,3,2,1,0:T(8,128)}, bf16[2,4,2,128,512]{4,3,2,1,0:T(8,128)(2,1)}) custom-call(bf16[2,4,2,128,512]{4,3,2,1,0:T(8,128)(2,1)} %get-tuple-element.107.refs_0_, bf16[2,4,2,128,512]{4,3,2,1,0:T(8,128)(2,1)} %get-tuple-element.110.refs_1_, ...), custom_call_target="tpu_custom_call" | custom-call | flops 8589934592 | bytes 25165824 | tf_op jit(solution)/shard_map/expert_forward/pallas_call | solution.py:221
  199.4 4.3 reading_step.1
  203.7 16.1 %scalar_step.1 = (f32[2,512,8]{2,1,0:T(8,128)}, f32[4,2,4,8,128]{4,3,2,1,0:T(8,128)}) custom-call(f32[4,4,8,128]{3,2,1,0:T(8,128)} %bitcast.55, f32[4,4,8,128]{3,2,1,0:T(8,128)} %bitcast.92, f32[8,512]{1,0:T(8,128)} %get-tuple-element.121.rowsc0_ref, f32[8,512]{1,0:T(8,128)} %get-tuple-element.122.rowsc1_ref, ...), custom_call_target="tpu_custom_call" | custom-call | flops 1000000000 | bytes 1048576 | tf_op jit(solution)/shard_map/scalar_step/pallas_call | solution.py:687
  219.7 38.0 %expert_backward.2 = (bf16[4,2,512,512]{3,2,1,0:T(8,128)(2,1)}, bf16[4,2,512,512]{3,2,1,0:T(8,128)(2,1)}, bf16[4,2,128,512]{3,2,1,0:T(8,128)(2,1)}, bf16[4,2,128...) custom-call(bf16[2,4,2,128,512]{4,3,2,1,0:T(8,128)(2,1)} %get-tuple-, ...), custom_call_target="tpu_custom_call" | custom-call | flops 21474836480 | bytes 50331648 | tf_op jit(solution)/shard_map/expert_backward/pallas_call | solution.py:221
  258.6 43.5 %expert_backward.3 = (bf16[2,2,512,512]{3,2,1,0:T(8,128)(2,1)}, bf16[2,2,512,512]{3,2,1,0:T(8,128)(2,1)}, bf16[4,2,128,512]{3,2,1,0:T(8,128)(2,1)}, bf16[4,2,128...) custom-call(bf16[2,4,2,128,512]{4,3,2,1,0:T(8,128)(2,1)} %get-tuple-, ...), custom_call_target="tpu_custom_call" | custom-call | flops 21474836480 | bytes 50331648 | tf_op jit(solution)/shard_map/expert_backward/pallas_call | solution.py:221
  302.9 29.8 %result_step.2 = (bf16[2,512,512]{2,1,0:T(8,128)(2,1)}, f32[8,512]{1,0:T(8,128)}, bf16[4,2,128,512]{3,2,1,0:T(8,128)(2,1)}, bf16[4,2,128,512]{3,2,1,0:T(8,128)(2,1)}) custom-call(bf16[2,512,512]{2,1,0:T(8,128)(2,1)} %refs_0_.11, f32[512,512]{1,0:T(8,128)} %get-tuple-element.131.refs_1_.refs_8_, bf16[1024,512]{1,0:T(8,128)(2,1)} %bitcast.88, ...), custom_call_target="tpu_custom_call" | custom-call | flops 2147483648 | bytes 5242880 | tf_op jit(solution)/shard_map/result_step/pallas_call | solution.py:221
  332.7 2.5 collective-permute-start.2
  335.2 22.1 %attention_backward.2 = (f32[2,512,512]{2,1,0:T(8,128)}, f32[512,1536]{1,0:T(8,128)}, f32[512,1536]{1,0:T(8,128)}, f32[256,512]{1,0:T(8,128)}, f32[128,512]{1,0:T(8,128)}, /*index=5*/f32[8,512]{1,0:T(8,128)}) custom-call(bf16[2,512,512]{2,1,0:T(8,128)(2,1)} %refs_0_.11, bf16[2,512,512]{2,1,0:T(8,128)(2,1)} %refs_1_.9, s32[2,512,8]{2,1,0:T(8,128)} %pad_add_fusion.refs_2_, ...), custom_call_target="tpu_custom_call" | custom-call | flops 4563402752 | bytes 25165824 | tf_op jit(solution)/shard_map/attention_backward/pallas_call | solution.py:221
  358.0 8.2 %result_step.3 = (bf16[2,512,512]{2,1,0:T(8,128)(2,1)}, f32[8,512]{1,0:T(8,128)}) custom-call(bf16[2,512,512]{2,1,0:T(8,128)(2,1)} %refs_0_.11, f32[512,512]{1,0:T(8,128)} %get-tuple-element.106.refs_1_.refs_8_, bf16[1024,512]{1,0:T(8,128)(2,1)} %bitcast.86, bf16[1024,512]{1,0:T(8,128)(2,1)} %bitcast.87, ...), custom_call_target="tpu_custom_call", output_to_operand_aliasing={{0}: (6, {})} | custom-call | flops 2147483648 | bytes 5242880 | tf_op jit(solution)/shard_map/result_step/pallas_call | solution.py:221
  366.1 0.7 add.28
  366.9 23.4 %attention_backward.3 = (f32[2,512,512]{2,1,0:T(8,128)}, bf16[3584,512]{1,0:T(8,128)(2,1)}, f32[8,512]{1,0:T(8,128)}) custom-call(bf16[2,512,512]{2,1,0:T(8,128)(2,1)} %refs_0_.11, bf16[2,512,512]{2,1,0:T(8,128)(2,1)} %refs_1_.9, s32[2,512,8]{2,1,0:T(8,128)} %pad_add_fusion.refs_2_, ...), custom_call_target="tpu_custom_call", output_to_operand_aliasing={{0}: (25, {})} | custom-call | flops 4563402752 | bytes 25165824 | tf_op jit(solution)/shard_map/attention_backward/pallas_call | solution.py:221
  390.3 1.3 pad_maximum_fusion.small_ref
  391.6 79.5 %total_step.1 = (bf16[3584,512]{1,0:T(8,128)(2,1)}, f32[16,512]{1,0:T(8,128)}) custom-call(bf16[3584,512]{1,0:T(8,128)(2,1)} %get-tuple-element.172.pack_ref, f32[16,512]{1,0:T(8,128)} %pad_maximum_fusion.small_ref), custom_call_target="tpu_custom_call" | custom-call | tf_op jit(solution)/shard_map/total_step/pallas_call | solution.py:1074
  471.1 1.2 slice.39
  472.3 1.5 fusion.4
  473.8 0.9 copy-done
  475.2 7.6 %unpack_step.1 = (f32[512,1536]{1,0:T(8,128)}, f32[3,512,512]{2,1,0:T(8,128)}, f32[2,512,512]{2,1,0:T(8,128)}, f32[2,512,512]{2,1,0:T(8,128)}, f32[64,512]{1,0:T...) custom-call(bf16[7,512,512]{2,1,0:T(8,128)(2,1)} %bitcast.50, bf16[2,512,512]{2,1,0:T(8,128)(2,1)} %bitcast.51, ...), custom_call_target="tpu_custom_call" | custom-call | bytes 20971520 | tf_op jit(solution)/shard_map/unpack_step/pallas_call | solution.py:221
  482.7 1.0 copy.74
  (72 shorter events, 7.9 us)
Async XLA Ops:
  7.2 1.6 copy-start.2
  7.2 5.7 %copy-start.10 = (s32[2,2,256]{2,1,0:T(2,128)S(1)}, s32[2,2,256]{2,1,0:T(2,128)}, u32[]{:S(2)}) copy-start(s32[2,2,256]{2,1,0:T(2,128)} %param.24) | copy-start | bytes 12292
  7.2 6.7 %copy-start.11 = (s32[2,512]{1,0:T(2,128)S(1)}, s32[2,512]{1,0:T(2,128)}, u32[]{:S(2)}) copy-start(s32[2,512]{1,0:T(2,128)} %param.25) | copy-start | bytes 12292
  7.2 6.8 %copy-start.9 = (bf16[512,24]{0,1:T(8,128)(2,1)S(1)}, bf16[512,24]{0,1:T(8,128)(2,1)}, u32[]{:S(2)}) copy-start(bf16[512,24]{0,1:T(8,128)(2,1)} %param.28) | copy-start | bytes 73732
  7.2 6.9 %copy-start.7 = (bf16[512,64]{0,1:T(8,128)(2,1)S(1)}, bf16[512,64]{0,1:T(8,128)(2,1)}, u32[]{:S(2)}) copy-start(bf16[512,64]{0,1:T(8,128)(2,1)} %param.30) | copy-start | bytes 196612
  7.2 7.0 %copy-start.8 = (bf16[512,64]{0,1:T(8,128)(2,1)S(1)}, bf16[512,64]{0,1:T(8,128)(2,1)}, u32[]{:S(2)}) copy-start(bf16[512,64]{0,1:T(8,128)(2,1)} %param.31) | copy-start | bytes 196612
  7.2 7.1 %copy-start.12 = (bf16[512,16]{0,1:T(8,128)(2,1)S(1)}, bf16[512,16]{0,1:T(8,128)(2,1)}, u32[]{:S(2)}) copy-start(bf16[512,16]{0,1:T(8,128)(2,1)} %param.35) | copy-start | bytes 49156
  7.3 7.9 %copy-start.13 = (s32[2,512,4]{1,2,0:T(4,128)S(1)}, s32[2,512,4]{1,2,0:T(4,128)}, u32[]{:S(2)}) copy-start(s32[2,512,4]{1,2,0:T(4,128)} %param.22) | copy-start | bytes 49156
  7.3 8.3 %copy-start.6 = (s32[2,512,2]{1,2,0:T(2,128)S(1)}, s32[2,512,2]{1,2,0:T(2,128)}, u32[]{:S(2)}) copy-start(s32[2,512,2]{1,2,0:T(2,128)} %param.23) | copy-start | bytes 24580
  7.3 134.5 %all-gather.13.cloned.1.call-start = ((), (), s32[]{:S(2)}) async-start(), calls=%async_computation.10 | async-start | bytes 5242880 | tf_op jit(solution)/shard_map/all_gather | solution.py:1161
  8.0 133.7 %all-gather.15.cloned.1.call-start = ((), (), s32[]{:S(2)}) async-start(), calls=%async_computation.11 | async-start | bytes 5242880 | tf_op jit(solution)/shard_map/all_gather | solution.py:1161
  8.8 162.0 %all-gather.9.cloned.1.call-start = ((), (), s32[]{:S(2)}) async-start(), calls=%async_computation.8 | async-start | bytes 5242880 | tf_op jit(solution)/shard_map/all_gather | solution.py:1161
  8.8 49.8 %collective-permute-start = (bf16[2,512,512]{2,1,0:T(8,128)(2,1)S(1)}, bf16[2,512,512]{2,1,0:T(8,128)(2,1)}, u32[]{:S(2)}, u32[]{:S(2)}) collective-permute-start(bf16[2,512,512]{2,1,0:T(8,128)(2,1)S(1)} %copy-done.2), channel_id=1, source_target_pairs={{0,16},{4,20},{8,24},{12,28},{16,0},{20,4},{24,8},{28,12},{1,17},{... | collective-permute-start | bytes 3145736 | tf_op jit(solution)/shard_map/ppermute | solution.py:1163
  25.7 33.0 %copy-start.3 = (bf16[2,512,512]{2,1,0:T(8,128)(2,1)S(1)}, bf16[2,512,512]{2,1,0:T(8,128)(2,1)}, u32[]{:S(2)}) copy-start(bf16[2,512,512]{2,1,0:T(8,128)(2,1)} %param.37) | copy-start | bytes 3145732
  58.7 112.1 %all-gather.11.cloned.1.call-start = ((), (), s32[]{:S(2)}) async-start(), calls=%async_computation.9 | async-start | bytes 5242880 | tf_op jit(solution)/shard_map/all_gather | solution.py:1161
  58.7 47.9 %collective-permute-start.1 = (bf16[2,512,512]{2,1,0:T(8,128)(2,1)S(1)}, bf16[2,512,512]{2,1,0:T(8,128)(2,1)S(1)}, u32[]{:S(2)}, u32[]{:S(2)}) collective-permute-start(bf16[2,512,512]{2,1,0:T(8,128)(2,1)S(1)} %copy-done.3), channel_id=1, source_target_pairs={{0,16},{4,20},{8,24},{12,28},{16,0},{20,4},{24,8},{28,12},{1,17},{... | collective-permute-start | bytes 3145736 | tf_op jit(solution)/shard_map/ppermute | solution.py:1163
  106.6 1.0 copy-start.4
  107.6 225.1 %reduce-scatter.5.cloned.1.call-start = ((), (), s32[]{:S(2)}) async-start(), calls=%async_computation.4 | async-start | bytes 5242880 | tf_op jit(solution)/shard_map/reduce_scatter | solution.py:1210
  257.8 99.6 %reduce-scatter.7.cloned.1.call-start = ((), (), s32[]{:S(2)}) async-start(), calls=%async_computation.5 | async-start | bytes 5242880 | tf_op jit(solution)/shard_map/reduce_scatter | solution.py:1210
  258.3 215.4 %reduce-scatter.9.cloned.1.call-start = ((), (), s32[]{:S(2)}) async-start(), calls=%async_computation.6 | async-start | bytes 3145728 | tf_op jit(solution)/shard_map/reduce_scatter | solution.py:1210
  302.2 171.6 %reduce-scatter.11.cloned.1.call-start = ((), (), s32[]{:S(2)}) async-start(), calls=%async_computation.7 | async-start | bytes 3145728 | tf_op jit(solution)/shard_map/reduce_scatter | solution.py:1210
  332.7 141.1 %collective-permute-start.2 = (bf16[2,512,512]{2,1,0:T(8,128)(2,1)}, bf16[2,512,512]{2,1,0:T(8,128)(2,1)S(1)}, u32[]{:S(2)}, u32[]{:S(2)}) collective-permute-start(bf16[2,512,512]{2,1,0:T(8,128)(2,1)} %bitcast.76), channel_id=1, source_target_pairs={{0,16},{4,20},{8,24},{12,28},{16,0},{20,4},{24,8},{28,12},{1,17},{... | collective-permute-start | bytes 3145736 | tf_op jit(solution)/shard_map/ppermute | solution.py:1217
  357.3 116.5 %collective-permute-start.3 = (bf16[2,512,512]{2,1,0:T(8,128)(2,1)}, bf16[2,512,512]{2,1,0:T(8,128)(2,1)S(1)}, u32[]{:S(2)}, u32[]{:S(2)}) collective-permute-start(bf16[2,512,512]{2,1,0:T(8,128)(2,1)} %bitcast.77), channel_id=1, source_target_pairs={{0,16},{4,20},{8,24},{12,28},{16,0},{20,4},{24,8},{28,12},{1,17},{... | collective-permute-start | bytes 3145736 | tf_op jit(solution)/shard_map/ppermute | solution.py:1223
  358.0 8.2 %copy-start.14 = (f32[8,512]{1,0:T(8,128)S(1)}, f32[8,512]{1,0:T(8,128)}, u32[]{:S(2)}) copy-start(f32[8,512]{1,0:T(8,128)} %get-tuple-element.174) | copy-start | bytes 49156
  473.8 1.0 copy-start
  473.8 1.3 copy-start.1
  475.2 7.6 %copy-start.5 = (bf16[2,512,512]{2,1,0:T(8,128)(2,1)S(1)}, bf16[2,512,512]{2,1,0:T(8,128)(2,1)}, u32[]{:S(2)}) copy-start(bf16[2,512,512]{2,1,0:T(8,128)(2,1)} %get-tuple-element.217) | copy-start | bytes 3145732
Sparse Core Ops, SparseCore 0:
  9.7 37.1 all-gather.12
  48.4 34.4 all-gather.14
  84.5 34.4 all-gather.8
  121.1 34.4 all-gather.10
  257.9 46.5 reduce-scatter.4
  307.1 44.4 reduce-scatter.6
  353.8 31.8 reduce-scatter.8
  388.0 38.8 reduce-scatter.10
